TPU v7x, 32 devices: a whole 2x2x4 slice. The times are simulated.
32 devices in a mesh: row: 4 (over y, core), col: 8 (over z, x).
Axes of the slice: x: 2, y: 2, z: 4, core: 2. Of those that a mesh axis runs over, the one named last changes fastest.
Arguments:
- probes: float32 [32768, 256], P(('row', 'col')), may hold values from -6 to 6
- near_blocks: bfloat16 [32, 8, 1024, 1024], P(('row', 'col')), may hold values from -0.09375 to 0.09375
- near_leaves: int32 [32, 8], P(('row', 'col')), may hold values from 0 to 7, as said below
- near_count: int32 [32], P(('row', 'col')), may hold values from 1 to 8, as said below
- leaf_rank: int32 [32], P(('row', 'col')), may hold values from 128 to 256
- leaf_basis: float32 [32768, 256], P(('row', 'col')), may hold values from -0.1875 to 0.1875
- leaf_transfer: float32 [32, 256, 512], P(('row', 'col')), may hold values from -0.125 to 0.125
- leaf_links: int32 [32, 4], P(('row', 'col')), may hold values from 0 to 7, as said below
- leaf_link_blocks: float32 [32, 4, 256, 256], P(('row', 'col')), may hold values from -0.1875 to 0.1875
- parent_links: int32 [4, 2], P('row'), may hold values from 0 to 3, as said below
- parent_link_blocks: float32 [4, 2, 512, 512], P('row'), may hold values from -0.1875 to 0.1875
Outputs:
- term_one: float32 [32768, 256], P(('row', 'col'))
- term_two: float32 [32768, 256], P(('row', 'col'))
Inputs may be any that keep to these rules, and one draw needn't show every extreme that they name: `near_leaves`: slot 0 of every leaf is the leaf's own position; slots 1 to near_count - 1 are distinct other positions of the same group; later slots repeat the leaf's own position. `near_count`: some leaf has 8 live slots in every draw. `leaf_links`: each leaf's 4 coupled positions are distinct and differ from its own. `parent_links`: each parent's 2 coupled parents are distinct and differ from itself.
All inputs are finite; a program needn't handle non-finite values.
Results may differ from a plain program's by a relative error of at most 0.0034.
Values may be sent and summed in bfloat16 or wider, within the bound.
No kernel may reach another device: no remote copies, remote signals or barrier semaphores. Data moves between devices by JAX's collectives and lax.ppermute only.
A program may use at most 128 MiB of HBM per device.

v0:
```python
import jax
import jax.numpy as jnp
from jax import lax
from jax.sharding import PartitionSpec as P


def local(
    probes,
    near_blocks,
    near_leaves,
    near_count,
    leaf_rank,
    leaf_basis,
    leaf_transfer,
    leaf_links,
    leaf_link_blocks,
    parent_links,
    parent_link_blocks,
):
    highest = lax.Precision.HIGHEST
    span_col = lax.axis_size("col")
    span_row = lax.axis_size("row")
    leaf_rows = probes.shape[0]
    probe_cols = probes.shape[1]
    rank_cols = leaf_basis.shape[1]
    parent_cols = leaf_transfer.shape[2]
    rank_mask = (jnp.arange(rank_cols, dtype=jnp.int32) < leaf_rank[0]).astype(jnp.float32)[:, None]
    transfer = leaf_transfer[0]
    own_blocks = near_blocks[0]
    own_near = near_leaves[0]

    def multiply(vector):
        packed = vector.astype(jnp.bfloat16)
        empty = jnp.zeros((leaf_rows, probe_cols), jnp.float32)
        stacked = lax.all_gather(packed, "col", axis=0, tiled=True).reshape(
            span_col, leaf_rows, probe_cols
        )

        def add_slot(slot, total):
            near_block = lax.dynamic_index_in_dim(own_blocks, slot, 0, False)
            source = lax.dynamic_index_in_dim(stacked, own_near[slot], 0, False)
            return total + jnp.dot(near_block, source, preferred_element_type=jnp.float32)

        near_sum = lax.fori_loop(0, near_count[0], add_slot, empty)
        skeleton = jnp.dot(leaf_basis.T, vector, precision=highest) * rank_mask
        gathered = lax.all_gather(skeleton, "col", axis=0, tiled=True).reshape(
            span_col, rank_cols, probe_cols
        )
        linked = gathered[leaf_links[0]]
        coupled = jnp.einsum("kab,kbp->ap", leaf_link_blocks[0], linked, precision=highest)
        upward = jnp.dot(transfer.T, skeleton, precision=highest)
        portion = lax.psum_scatter(upward, "col", scatter_dimension=1, tiled=True)
        every_parent = lax.all_gather(portion, "row", axis=0, tiled=True).reshape(
            span_row, parent_cols, -1
        )
        far_portion = jnp.einsum(
            "kab,kbp->ap", parent_link_blocks[0], every_parent[parent_links[0]], precision=highest
        )
        far_parent = lax.all_gather(far_portion, "col", axis=1, tiled=True)
        combined = (coupled + jnp.dot(transfer, far_parent, precision=highest)) * rank_mask
        return jnp.dot(leaf_basis, combined, precision=highest) + near_sum

    term_one = multiply(probes)
    term_two = 2.0 * multiply(term_one) - probes
    return (term_one, term_two)


def solution(mesh):
    in_specs = (
        P(("row", "col"), None),
        P(("row", "col"), None, None, None),
        P(("row", "col"), None),
        P(("row", "col")),
        P(("row", "col")),
        P(("row", "col"), None),
        P(("row", "col"), None, None),
        P(("row", "col"), None),
        P(("row", "col"), None, None, None),
        P("row", None),
        P("row", None, None, None),
    )
    out_specs = (P(("row", "col"), None), P(("row", "col"), None))
    return jax.shard_map(local, mesh=mesh, in_specs=in_specs, out_specs=out_specs, check_vma=False)
```

profile of v0, /device:TPU:16, one launch (start us, length us, event | category | flops | bytes accessed | tf_op | source)
XLA Modules:
  0.0 512.9 jit_solution(4543359432863506335)
XLA Ops:
  8.0 3.5 convolution_multiply_fusion.1
  11.5 2.6 convolution_bitcast_fusion.3
  14.9 0.8 convert_element_type.14
  15.9 61.2 %reduce-scatter.3.cloned.1.call-done = f32[512,32]{0,1:T(8,128)} async-done(((f32[512,256]{0,1:T(8,128)}), f32[512,32]{0,1:T(8,128)}) %reduce-scatter.3.cloned.1.call-update) | async-done | bytes 65552 | tf_op jit(solution)/shard_map/reduce_scatter | solution.py:52
  77.1 6.0 %all_gather.25 = f32[2048,32]{0,1:T(8,128)S(1)} all-gather(f32[512,32]{0,1:T(8,128)} %reduce-scatter.3.cloned.1.call-done), channel_id=1, replica_groups=mesh['row'=4,'col'=8] {'row'}, dimensions={0}, use_global_device_ids=true | all-gather | bytes 327680 | tf_op jit(solution)/shard_map/all_gather | solution.py:53
  83.7 2.0 fusion.28
  85.7 29.1 %all_gather.26 = f32[512,256]{0,1:T(8,128)S(1)} all-gather(f32[512,32]{0,1:T(8,128)S(1)} %fusion.28), channel_id=1, replica_groups=mesh['row'=4,'col'=8] {'col'}, dimensions={1}, use_global_device_ids=true | all-gather | bytes 589824 | tf_op jit(solution)/shard_map/all_gather | solution.py:59
  114.9 16.6 %all-gather.5.cloned.1.call-done = f32[2048,256]{1,0:T(8,128)} async-done(((f32[256,256]{1,0:T(8,128)}), f32[2048,256]{1,0:T(8,128)}) %all-gather.5.cloned.1.call-update) | async-done | bytes 2097168 | tf_op jit(solution)/shard_map/all_gather | solution.py:46
  131.5 3.2 gather_fusion
  134.7 3.4 convolution_bitcast_fusion.5
  138.7 67.3 %all-gather.7.cloned.1.call-done = bf16[8192,256]{1,0:T(8,128)(2,1)} async-done(((bf16[1024,256]{1,0:T(8,128)(2,1)}), bf16[8192,256]{1,0:T(8,128)(2,1)}) %all-gather.7.cloned.1.call-update) | async-done | bytes 4194320 | tf_op jit(solution)/shard_map/all_gather | solution.py:35
  206.1 45.6 %while.20 = (s32[]{:T(128)}, f32[1024,256]{1,0:T(8,128)S(1)}, s32[]{:T(128)}, bf16[8,1024,1024]{2,1,0:T(8,128)(2,1)}, s32[8]{0:T(128)S(1)}, /*index=5*/bf16[8,10...) while((s32[]{:T(128)}, f32[1024,256]{1,0:T(8,128)S(1)}, s32[]{:T(128)}, ...), condition=%wide.region_2.3_spmd, body=%wide.region_1.2_spmd.sunk | while | flops 537133056 | bytes 4718773 | solution.py:44
  209.3 2.4 fusion.67
  214.9 2.4 fusion.67
  220.5 2.4 fusion.67
  226.1 2.4 fusion.67
  231.8 2.4 fusion.67
  237.4 2.4 fusion.67
  243.0 2.4 fusion.67
  248.6 2.4 fusion.67
  251.7 1.3 copy.20
  253.0 3.5 fusion.42
  256.5 1.0 convolution_multiply_fusion
  257.9 1.4 convolution_bitcast_fusion.2
  260.5 1.4 copy.25
  261.9 2.5 copy.26
  264.4 54.9 %reduce-scatter.5.cloned.1.call-done = f32[512,32]{0,1:T(8,128)} async-done(((f32[512,256]{0,1:T(8,128)}), f32[512,32]{0,1:T(8,128)}) %reduce-scatter.5.cloned.1.call-update) | async-done | bytes 65552 | tf_op jit(solution)/shard_map/reduce_scatter | solution.py:52
  319.3 6.0 %all_gather.29 = f32[2048,32]{0,1:T(8,128)S(1)} all-gather(f32[512,32]{0,1:T(8,128)} %reduce-scatter.5.cloned.1.call-done), channel_id=1, replica_groups=mesh['row'=4,'col'=8] {'row'}, dimensions={0}, use_global_device_ids=true | all-gather | bytes 327680 | tf_op jit(solution)/shard_map/all_gather | solution.py:53
  325.9 2.0 fusion.31
  327.9 29.8 %all_gather.30 = f32[512,256]{0,1:T(8,128)S(1)} all-gather(f32[512,32]{0,1:T(8,128)S(1)} %fusion.31), channel_id=1, replica_groups=mesh['row'=4,'col'=8] {'col'}, dimensions={1}, use_global_device_ids=true | all-gather | bytes 589824 | tf_op jit(solution)/shard_map/all_gather | solution.py:59
  357.7 16.8 %all-gather.9.cloned.1.call-done = f32[2048,256]{0,1:T(8,128)} async-done(((f32[256,256]{0,1:T(8,128)}), f32[2048,256]{0,1:T(8,128)}) %all-gather.9.cloned.1.call-update) | async-done | bytes 2097168 | tf_op jit(solution)/shard_map/all_gather | solution.py:46
  374.5 3.0 copy.28
  377.5 3.2 gather_fusion.2
  380.7 3.4 convolution_bitcast_fusion.4
  384.7 63.7 %all-gather.11.cloned.1.call-done = bf16[8192,256]{0,1:T(8,128)(2,1)} async-done(((bf16[1024,256]{0,1:T(8,128)(2,1)}), bf16[8192,256]{0,1:T(8,128)(2,1)}) %all-gather.11.cloned.1.call-update) | async-done | bytes 4194320 | tf_op jit(solution)/shard_map/all_gather | solution.py:35
  448.4 6.5 %copy.29 = bf16[8192,256]{1,0:T(8,128)(2,1)} copy(bf16[8192,256]{0,1:T(8,128)(2,1)} %all-gather.11.cloned.1.call-done) | data formatting | bytes 8388608 | tf_op jit(solution)/shard_map/while | solution.py:44
  454.9 45.6 %while.21 = (s32[]{:T(128)}, f32[1024,256]{1,0:T(8,128)S(1)}, s32[]{:T(128)}, bf16[8,1024,1024]{2,1,0:T(8,128)(2,1)}, s32[8]{0:T(128)S(1)}, /*index=5*/bf16[8,10...) while((s32[]{:T(128)}, f32[1024,256]{1,0:T(8,128)S(1)}, s32[]{:T(128)}, ...), condition=%wide.region_5.6_spmd, body=%wide.region_4.5_spmd.sunk | while | flops 537133056 | bytes 4718773 | solution.py:44
  458.1 2.4 fusion.70
  463.7 2.4 fusion.70
  469.4 2.4 fusion.70
  475.0 2.4 fusion.70
  480.6 2.4 fusion.70
  486.2 2.4 fusion.70
  491.8 2.4 fusion.70
  497.5 2.4 fusion.70
  500.5 1.3 copy.24
  501.8 2.9 fusion.25
  504.8 1.3 copy.27
  (67 shorter events, 14.4 us)
Async XLA Ops:
  7.2 76.5 %copy-start = (f32[1,2,512,512]{3,2,1,0:T(8,128)S(1)}, f32[1,2,512,512]{3,2,1,0:T(8,128)}, u32[]{:S(2)}) copy-start(f32[1,2,512,512]{3,2,1,0:T(8,128)} %param.25) | copy-start | bytes 6291460
  7.2 70.0 %reduce-scatter.3.cloned.1.call-start = ((), (), s32[]{:S(2)}) async-start(), calls=%async_computation.3 | async-start | bytes 589824 | tf_op jit(solution)/shard_map/reduce_scatter | solution.py:52
  8.0 6.9 %copy-start.2 = (f32[1024,256]{1,0:T(8,128)S(1)}, f32[1024,256]{1,0:T(8,128)}, u32[]{:S(2)}) copy-start(f32[1024,256]{1,0:T(8,128)} %param.15) | copy-start | bytes 3145732
  11.5 2.7 copy-start.8
  11.5 4.3 copy-start.10
  11.5 4.4 copy-start.11
  14.1 117.3 %all-gather.5.cloned.1.call-start = ((), (), s32[]{:S(2)}) async-start(), calls=%async_computation.2 | async-start | bytes 2359296 | tf_op jit(solution)/shard_map/all_gather | solution.py:46
  14.9 191.1 %all-gather.7.cloned.1.call-start = ((), (), s32[]{:S(2)}) async-start(), calls=%async_computation.4 | async-start | bytes 4718592 | tf_op jit(solution)/shard_map/all_gather | solution.py:35
  15.8 303.5 %reduce-scatter.5.cloned.1.call-start = ((), (), s32[]{:S(2)}) async-start(), calls=%async_computation.6 | async-start | bytes 589824 | tf_op jit(solution)/shard_map/reduce_scatter | solution.py:52
  131.5 6.6 %copy-start.5 = (f32[1,256,512]{2,1,0:T(8,128)S(1)}, f32[1,256,512]{2,1,0:T(8,128)}, u32[]{:S(2)}) copy-start(f32[1,256,512]{2,1,0:T(8,128)} %param.21) | copy-start | bytes 1572868
  134.7 71.4 %copy-start.12 = (s32[1,8]{1,0:T(1,128)S(1)}, s32[1,8]{1,0:T(1,128)}, u32[]{:S(2)}) copy-start(s32[1,8]{1,0:T(1,128)} %param.17) | copy-start | bytes 100
  253.0 3.5 copy-start.1
  256.5 1.0 copy-start.4
  256.5 1.4 copy-start.6
  256.5 4.0 copy-start.3
  257.9 1.5 copy-start.9
  259.3 115.2 %all-gather.9.cloned.1.call-start = ((), (), s32[]{:S(2)}) async-start(), calls=%async_computation.5 | async-start | bytes 2359296 | tf_op jit(solution)/shard_map/all_gather | solution.py:46
  259.9 188.5 %all-gather.11.cloned.1.call-start = ((), (), s32[]{:S(2)}) async-start(), calls=%async_computation.7 | async-start | bytes 4718592 | tf_op jit(solution)/shard_map/all_gather | solution.py:35
  377.5 6.6 %copy-start.7 = (f32[1,256,512]{2,1,0:T(8,128)S(1)}, f32[1,256,512]{2,1,0:T(8,128)}, u32[]{:S(2)}) copy-start(f32[1,256,512]{2,1,0:T(8,128)} %param.21) | copy-start | bytes 1572868
Sparse Core Ops, SparseCore 0:
  14.2 62.8 reduce-scatter.2
  79.3 52.1 all-gather.4
  134.2 71.7 all-gather.6
  259.5 59.8 reduce-scatter.4
  321.2 53.2 all-gather.8
  376.5 71.8 all-gather.10
where the time goes:
time: 516 us; the launch traced here: 513 us
  waiting for transfers between devices  282 us (55%)
  blocking collectives  70.9 us (14%)
  matrix products  65.5 us (13%)
  loops' own time  43.2 us (8%)
  local copies, waits for them, and re-layouts  34.8 us (7%)
  between operations  15.2 us (3%)
    all_gather x2, waiting for transfers between devices, multiply(): lax.all_gather(packed, 'col', axis=0, tiled=True)  131 us
    reduce_scatter x2, waiting for transfers between devices, multiply(): portion = lax.psum_scatter(upward, 'col', scatter_dimension=1, tiled=True)  116 us
    all_gather x2, blocking collectives, multiply(): far_parent = lax.all_gather(far_portion, 'col', axis=1, tiled=True)  58.9 us
    another operation x2, loops' own time, multiply(): near_sum = lax.fori_loop(0, near_count[0], add_slot, empty)  43.2 us
    dot_general x16, matrix products, add_slot(): jnp.dot(near_block, source, preferred_element_type=jnp.float32)  38.6 us
    all_gather x2, waiting for transfers between devices, multiply(): lax.all_gather(skeleton, 'col', axis=0, tiled=True)  33.4 us
    all_gather x2, blocking collectives, multiply(): lax.all_gather(portion, 'row', axis=0, tiled=True)  11.9 us
  transfers between devices with their start and end apart: 6, of which 6 were waited for; matrix products, arithmetic and copies ran while one was open for 5% of the time, Pallas kernels for 0%

commit v1 on v0

v1 whole, which is shorter than its diff:
```python
import functools

import jax
import jax.numpy as jnp
from jax import lax
from jax.experimental import pallas as pl
from jax.experimental.pallas import tpu as pltpu
from jax.sharding import PartitionSpec as P


F32 = jnp.float32
BF16 = jnp.bfloat16
VMEM = pl.BlockSpec(memory_space=pltpu.VMEM)
SMEM = pl.BlockSpec(memory_space=pltpu.SMEM)


def ring_order(n):
    return list(range(0, n, 2)) + list(range(n - 1, 0, -2))


def halves(x):
    high = x.astype(BF16)
    low = (x - high.astype(F32)).astype(BF16)
    return high, low


def contract(a, b, dims):
    return lax.dot_general(a, b, (dims, ((), ())), preferred_element_type=F32)


def contract3(a, b, dims):
    a_high, a_low = halves(a)
    b_high, b_low = halves(b)
    small = contract(a_low, b_high, dims) + contract(a_high, b_low, dims)
    return small + contract(a_high, b_high, dims)


def contract2(a, b, dims):
    a_high, a_low = halves(a)
    return contract(a_low, b, dims) + contract(a_high, b, dims)


NN = ((1,), (0,))
NT = ((1,), (1,))
TN = ((0,), (0,))


def cost(flops, moved):
    return pl.CostEstimate(flops=int(flops), bytes_accessed=int(moved), transcendentals=0)


def share_of(me, bits):
    share = me & 1
    for b in range(1, bits):
        share = 2 * share + ((me >> b) & 1)
    return share


def front_body(me_ref, rank_ref, v_ref, basis_ref, transfer_ref, bottom_ref, away_ref, kept_ref, upward_ref):
    leaf_rows = v_ref.shape[0]
    part = bottom_ref.shape[0]
    v = v_ref[...]
    skeleton = contract3(basis_ref[...], v, TN)
    row = lax.broadcasted_iota(jnp.int32, skeleton.shape, 0)
    skeleton = jnp.where(row < rank_ref[0], skeleton, 0.0)
    bottom_ref[: leaf_rows - part, :] = v[part:, :].astype(BF16)
    bottom_ref[leaf_rows - part :, :] = skeleton.astype(BF16)
    upward_ref[...] = contract3(skeleton, transfer_ref[...], TN)
    half = kept_ref.shape[0]
    bit = me_ref[0] & 1
    away_ref[...] = upward_ref[pl.ds(pl.multiple_of((1 - bit) * half, half), half), :].astype(BF16)
    kept_ref[...] = upward_ref[pl.ds(pl.multiple_of(bit * half, half), half), :]


def front(me, v, basis, transfer, rank):
    leaf_rows, probe_cols = v.shape
    rank_cols, parent_cols = transfer.shape
    part = (leaf_rows + rank_cols) // 2
    return pl.pallas_call(
        front_body,
        out_shape=(
            jax.ShapeDtypeStruct((part, probe_cols), BF16),
            jax.ShapeDtypeStruct((probe_cols // 2, parent_cols), BF16),
            jax.ShapeDtypeStruct((probe_cols // 2, parent_cols), F32),
        ),
        in_specs=[SMEM, SMEM, VMEM, VMEM, VMEM],
        out_specs=(VMEM,) * 3,
        scratch_shapes=[pltpu.VMEM((probe_cols, parent_cols), F32)],
        cost_estimate=cost(6 * v.size * rank_cols, 8 * v.size),
        name="front",
    )(me, rank, v, basis, transfer)


ANY = pl.BlockSpec(memory_space=pl.ANY)


DEPTH = 3


class Copies:
    def __init__(self, sems):
        self.sems = sems
        self.made = []

    def start(self, source, target, when=None):
        copy = pltpu.make_async_copy(source, target, self.sems.at[len(self.made)])
        self.made.append(copy)
        if when is None:
            copy.start()
        else:
            pl.when(when)(copy.start)
        return copy


def origin(me, j, n):
    place = jnp.where(me & 1 == 1, n - ((me + 1) >> 1), me >> 1)
    step = (j + 1) // 2
    place = place - step if j % 2 else place + step
    place = jnp.where(place < 0, place + n, jnp.where(place >= n, place - n, place))
    return jnp.where(place < n // 2, 2 * place, 2 * (n - place) - 1)


def named(me_ref, near_ref, count_ref, links_ref, j, n):
    leaf = origin(me_ref[0], j, n)
    slot = jnp.int32(-1)
    for k in range(near_ref.shape[1]):
        slot = jnp.where((near_ref[0, k] == leaf) & (k < count_ref[0]), k, slot)
    link = jnp.int32(-1)
    for k in range(links_ref.shape[1]):
        link = jnp.where(links_ref[0, k] == leaf, k, link)
    return slot >= 0, jnp.maximum(slot, 0), link >= 0, jnp.maximum(link, 0)


def absorb(tables, n, first, blocks, links, messages, sums):
    leaf_rows = blocks.shape[1]
    rank_cols = links.shape[1]
    part, probe_cols = messages[0][0].shape
    count = len(messages)
    outs = (
        jax.ShapeDtypeStruct((leaf_rows, probe_cols), F32),
        jax.ShapeDtypeStruct((rank_cols, probe_cols), F32),
    )
    operands = [p for message in messages for p in message] + list(sums)

    def body(me_ref, nears_ref, count_ref, ties_ref, blocks_ref, links_ref, *refs):
        near_out, coupled_out, block_ref, link_ref, held_ref, sems = refs[len(operands) :]
        copies = Copies(sems)

        def fetch(j):
            at = j % DEPTH
            live, slot, linked, link = named(me_ref, nears_ref, count_ref, ties_ref, first + j, n)
            got = [copies.start(refs[2 * j + c], held_ref.at[at, pl.ds(c * part, part)]) for c in (0, 1)]
            block = copies.start(blocks_ref.at[slot], block_ref.at[at], live)
            tie = copies.start(links_ref.at[link], link_ref.at[at], linked)
            return live, linked, got, block, tie

        if sums:
            base = [copies.start(refs[2 * count], near_out), copies.start(refs[2 * count + 1], coupled_out)]
        fetched = [fetch(j) for j in range(min(count, DEPTH - 1))]
        if sums:
            for copy in base:
                copy.wait()
        else:
            near_out[...] = jnp.zeros_like(near_out)
            coupled_out[...] = jnp.zeros_like(coupled_out)
        for j in range(count):
            live, linked, got, block, tie = fetched[j]
            at = j % DEPTH
            for copy in got:
                copy.wait()
            pl.when(live)(block.wait)
            if j + DEPTH - 1 < count:
                fetched.append(fetch(j + DEPTH - 1))

            @pl.when(live)
            def _():
                near_out[...] += contract(block_ref[at], held_ref[at, :leaf_rows, :], NN)

            @pl.when(linked)
            def _():
                tie.wait()
                coupled_out[...] += contract2(link_ref[at], held_ref[at, leaf_rows:, :], NN)

    return pl.pallas_call(
        body,
        out_shape=outs,
        in_specs=[SMEM] * 4 + [ANY] * (2 + len(operands)),
        out_specs=(VMEM, VMEM),
        scratch_shapes=[
            pltpu.VMEM((DEPTH,) + blocks.shape[1:], BF16),
            pltpu.VMEM((DEPTH,) + links.shape[1:], F32),
            pltpu.VMEM((DEPTH, 2 * part, probe_cols), BF16),
            pltpu.SemaphoreType.DMA((4 * count + 2,)),
        ],
        cost_estimate=cost(2 * count * blocks[0].size * probe_cols, 4 * count * blocks[0].size),
        name="absorb",
    )(*tables, blocks, links, *operands)


def far_body(count, row_ref, links_ref, *refs):
    parents, blocks_ref, out_ref = refs[:count], refs[count], refs[count + 1]
    total = jnp.zeros(out_ref.shape, F32)
    for k in range(blocks_ref.shape[0]):
        chosen = parents[0][...]
        away = jnp.bitwise_xor(links_ref[0, k], row_ref[0])
        for e in range(1, count):
            chosen = jnp.where(away == e, parents[e][...], chosen)
        high, low = halves(blocks_ref[k])
        total += contract(chosen, low, NT) + contract(chosen, high, NT)
    out_ref[...] = total.astype(BF16)


def far_share(row, links, parents, blocks):
    return pl.pallas_call(
        functools.partial(far_body, len(parents)),
        out_shape=jax.ShapeDtypeStruct(parents[0].shape, BF16),
        in_specs=[SMEM, SMEM] + [VMEM] * (len(parents) + 1),
        out_specs=VMEM,
        cost_estimate=cost(2**24, blocks.size * 4),
        name="far",
    )(row, links, *parents, blocks)


def far_bits(far):
    total = sum(piece.shape[0] for piece in far) // far[0].shape[0]
    return total.bit_length() - 1


def reversed_bits(at, bits):
    return sum(((at >> b) & 1) << (bits - 1 - b) for b in range(bits))


def back(tables, n, rank, blocks, links, parts, near, coupled, far, transfer, basis, start):
    leaf_rows = blocks.shape[1]
    half = leaf_rows // 2
    final = start is not None
    part = parts[0].shape[0]
    count = len(far)
    bits = far_bits(far)
    operands = list(far) + [transfer, coupled, *parts, basis, near] + ([start] if final else [])

    def body(me_ref, nears_ref, count_ref, ties_ref, rank_ref, blocks_ref, links_ref, *refs):
        far_refs = refs[:count]
        transfer_in, coupled_in, top_ref, bottom_ref, basis_in, near_in = refs[count : count + 6]
        rest = refs[len(operands) :]
        out_ref, *sent_refs = rest[: 1 if final else 2]
        transfer_ref, basis_ref, block_ref, link_ref, held_ref, spread_ref, combined_ref = rest[
            len(sent_refs) + 1 : len(sent_refs) + 8
        ]
        sems = rest[-1]
        copies = Copies(sems)
        live, slot, linked, link = named(me_ref, nears_ref, count_ref, ties_ref, n - 1, n)
        rows = far_refs[0].shape[0]
        early = []
        at = 0
        for ref in far_refs:
            for piece in range(ref.shape[0] // rows):
                share = share_of(jnp.bitwise_xor(me_ref[0], reversed_bits(at, bits)), bits)
                early.append(
                    copies.start(
                        ref.at[pl.ds(piece * rows, rows)],
                        spread_ref.at[pl.ds(pl.multiple_of(share * rows, rows), rows)],
                    )
                )
                at += 1
        early.append(copies.start(transfer_in, transfer_ref))
        early.append(copies.start(coupled_in, combined_ref))
        bottom = copies.start(bottom_ref, held_ref.at[pl.ds(part, part)])
        tie = copies.start(links_ref.at[link], link_ref, linked)
        basis_copy = copies.start(basis_in, basis_ref)
        base = copies.start(near_in, out_ref)
        for copy in early:
            copy.wait()
        top = copies.start(top_ref, held_ref.at[pl.ds(0, part)])
        ready = [
            copies.start(
                blocks_ref.at[slot, pl.ds(c * half, half)], block_ref.at[pl.ds(c * half, half)], live
            )
            for c in (0, 1)
        ]
        if final:
            past = copies.start(refs[len(operands) - 1], rest[-2])

        combined_ref[...] += contract2(transfer_ref[...], spread_ref[...], NT)
        bottom.wait()

        @pl.when(linked)
        def _():
            tie.wait()
            combined_ref[...] += contract2(link_ref[...], held_ref[leaf_rows:, :], NN)

        row = lax.broadcasted_iota(jnp.int32, combined_ref.shape, 0)
        combined = jnp.where(row < rank_ref[0], combined_ref[...], 0.0)
        basis_copy.wait()
        base.wait()
        out_ref[...] += contract3(basis_ref[...], combined, NN)
        top.wait()

        @pl.when(live)
        def _():
            for c in (0, 1):
                ready[c].wait()
                at = pl.ds(c * half, half)
                out_ref[at, :] += contract(block_ref[at, :], held_ref[:leaf_rows, :], NN)

        if final:
            past.wait()
            out_ref[...] = 2.0 * out_ref[...] - rest[-2][...]
        else:
            sent_refs[0][...] = out_ref[:part, :].astype(BF16)

    out = jax.ShapeDtypeStruct(near.shape, F32)
    outs = (out,) if final else (out, jax.ShapeDtypeStruct(parts[0].shape, BF16))
    return pl.pallas_call(
        body,
        out_shape=outs,
        in_specs=[SMEM] * 5 + [ANY] * (2 + len(operands)),
        out_specs=(VMEM,) * len(outs),
        scratch_shapes=[
            pltpu.VMEM(transfer.shape, F32),
            pltpu.VMEM(basis.shape, F32),
            pltpu.VMEM(blocks.shape[1:], BF16),
            pltpu.VMEM(links.shape[1:], F32),
            pltpu.VMEM((2 * part, near.shape[1]), BF16),
            pltpu.VMEM((near.shape[1], transfer.shape[1]), BF16),
            pltpu.VMEM(coupled.shape, F32),
        ]
        + ([pltpu.VMEM(near.shape, F32)] if final else [])
        + [pltpu.SemaphoreType.DMA((12 + (1 << bits),))],
        cost_estimate=cost(6 * blocks[0].size * near.shape[1], 6 * blocks[0].size),
        name="back",
    )(*tables, rank, blocks, links, *operands)


def local(
    probes,
    near_blocks,
    near_leaves,
    near_count,
    leaf_rank,
    leaf_basis,
    leaf_transfer,
    leaf_links,
    leaf_link_blocks,
    parent_links,
    parent_link_blocks,
):
    n = lax.axis_size("col")
    span_row = lax.axis_size("row")
    me = lax.axis_index("col")
    my_row = lax.axis_index("row")
    leaf_rows, _ = probes.shape
    transfer = leaf_transfer[0]
    blocks = near_blocks[0]
    link_blocks = leaf_link_blocks[0]
    bits = n.bit_length() - 1
    assert 1 << bits == n

    order = ring_order(n)
    to_right = [(order[i], order[(i + 1) % n]) for i in range(n)]
    to_left = [(b, a) for a, b in to_right]
    steps = n // 2 - 1

    mine = jnp.reshape(me, (1,))
    tables = (mine, near_leaves, near_count, leaf_links)

    def swap(value, axis, size, distance):
        return lax.ppermute(value, axis, [(i, i ^ distance) for i in range(size)])

    def pass_on(value, perm):
        return lax.ppermute(value, "col", perm)

    def multiply(vector, top, start):
        bottom, away, kept = front(mine, vector, leaf_basis, transfer, leaf_rank)

        for b in range(bits):
            if b:
                pair = total.reshape(2, total.shape[0] // 2, total.shape[1])
                bit = (me >> b) & 1
                away = lax.dynamic_index_in_dim(pair, 1 - bit, 0, False).astype(BF16)
                kept = lax.dynamic_index_in_dim(pair, bit, 0, False)
            total = kept + swap(away, "col", n, 1 << b).astype(F32)
        share = total.astype(BF16)
        parents = [share] + [swap(share, "row", span_row, e) for e in range(1, span_row)]
        far = [far_share(jnp.reshape(my_row, (1,)), parent_links, parents, parent_link_blocks[0])]
        for b in reversed(range(bits)):
            held = far[0] if len(far) == 1 else jnp.concatenate(far)
            far.append(swap(held, "col", n, 1 << b))

        messages = [(top, bottom)]
        right = left = (top, bottom)
        for _ in range(1, steps + 1):
            right = tuple(pass_on(right[c], to_right) for c in (0, 1))
            left = tuple(pass_on(left[c], to_left) for c in (0, 1))
            messages += [right, left]
        opposite = (pass_on(right[0], to_right), pass_on(left[1], to_left))
        sums = ()
        first = 0
        for s in range(1, steps + 1):
            taken = messages[first : 2 * s + 1]
            sums = absorb(tables, n, first, blocks, link_blocks, taken, sums)
            first = 2 * s + 1
        return back(
            tables, n, leaf_rank, blocks, link_blocks, opposite, *sums, far,
            transfer, leaf_basis, start,
        )

    part = (leaf_rows + leaf_basis.shape[1]) // 2
    term_one, top = multiply(probes, probes[:part].astype(BF16), None)
    (term_two,) = multiply(term_one, top, probes)
    return (term_one, term_two)


def solution(mesh):
    in_specs = (
        P(("row", "col"), None),
        P(("row", "col"), None, None, None),
        P(("row", "col"), None),
        P(("row", "col")),
        P(("row", "col")),
        P(("row", "col"), None),
        P(("row", "col"), None, None),
        P(("row", "col"), None),
        P(("row", "col"), None, None, None),
        P("row", None),
        P("row", None, None, None),
    )
    out_specs = (P(("row", "col"), None), P(("row", "col"), None))
    return jax.shard_map(local, mesh=mesh, in_specs=in_specs, out_specs=out_specs, check_vma=False)
```

time: 516 us -> 169 us (0.33)
  waiting for transfers between devices: 282 us -> 51.3 us
  blocking collectives: 70.9 us -> 0 us
  matrix products: 65.5 us -> 0 us
  Pallas kernels: 0 us -> 61.9 us
  loops' own time: 43.2 us -> 0 us
  starting transfers between devices: 0.42 us -> 42 us
  local copies, waits for them, and re-layouts: 34.8 us -> 3.88 us
  between operations: 15.2 us -> 2.63 us
    all_gather x4 -> x0, waiting for transfers between devices: 164 us -> none  [the longest x2 131 us: multiply(): lax.all_gather(packed, 'col', axis=0, tiled=True)]
    reduce_scatter x2 -> x0, waiting for transfers between devices: 116 us -> none  [multiply(): portion = lax.psum_scatter(upward, 'col', scatter_dimension=1, tiled=True)]
    all_gather x4 -> x0, blocking collectives: 70.9 us -> none  [the longest x2 58.9 us: multiply(): far_parent = lax.all_gather(far_portion, 'col', axis=1, tiled=True)]
    dot_general x28 -> x0, matrix products: 65.5 us -> none  [the longest x16 38.6 us: add_slot(): jnp.dot(near_block, source, preferred_element_type=jnp.float32)]
    pallas_call x0 -> x12, Pallas kernels: none -> 61.9 us  [the longest x6 35.8 us: absorb(): pl.pallas_call(body, out_shape=outs, in_specs=[SMEM] * 4 + [ANY] * (2 + l...]
    ppermute x0 -> x46, waiting for transfers between devices: none -> 51.3 us  [the longest x18 26.1 us: swap(): return lax.ppermute(value, axis, [(i, i ^ distance) for i in range(size)])]
    another operation x2 -> x0, loops' own time: 43.2 us -> none  [multiply(): near_sum = lax.fori_loop(0, near_count[0], add_slot, empty)]
    ppermute x0 -> x46, starting transfers between devices: none -> 42 us  [the longest x28 30.6 us: pass_on(): return lax.ppermute(value, 'col', perm)]
  transfers between devices with their start and end apart: 6 -> 46, of which waited for: 6 -> 19; matrix products, arithmetic and copies ran while one was open for 5% -> 3% of each run, Pallas kernels for 0% -> 25%
where the time goes in v1:
time: 169 us; the launch traced here: 165 us
  Pallas kernels  61.9 us (37%)
  waiting for transfers between devices  51.3 us (30%)
  starting transfers between devices  42 us (25%)
  local copies, waits for them, and re-layouts  3.88 us (2%)
  other arithmetic  3.59 us (2%)
  between operations  2.63 us (2%)
    pallas_call x6, Pallas kernels, absorb(): pl.pallas_call(body, out_shape=outs, in_specs=[SMEM] * 4 + [ANY] * (2 + l...  35.8 us
    ppermute x28, starting transfers between devices, pass_on(): return lax.ppermute(value, 'col', perm)  30.6 us
    ppermute x18, waiting for transfers between devices, swap(): return lax.ppermute(value, axis, [(i, i ^ distance) for i in range(size)])  26.1 us
    ppermute x28, waiting for transfers between devices, pass_on(): return lax.ppermute(value, 'col', perm)  25.2 us
    pallas_call x2, Pallas kernels, back(): pl.pallas_call(body, out_shape=outs, in_specs=[SMEM] * 5 + [ANY] * (2 + l...  12.4 us
    ppermute x18, starting transfers between devices, swap(): return lax.ppermute(value, axis, [(i, i ^ distance) for i in range(size)])  11.4 us
    pallas_call x2, Pallas kernels, front(): pl.pallas_call(front_body, out_shape=(jax.ShapeDtypeStruct((part, probe_c...  7.67 us
    pallas_call x2, Pallas kernels, far_share(): pl.pallas_call(functools.partial(far_body, len(parents)), out_shape=jax.S...  6.05 us
  transfers between devices with their start and end apart: 46, of which 19 were waited for; matrix products, arithmetic and copies ran while one was open for 3% of the time, Pallas kernels for 25%

profile of v1, /device:TPU:16, one launch (start us, length us, event | category | flops | bytes accessed | tf_op | source)
XLA Modules:
  0.0 165.4 jit_solution(16837001629775751430)
XLA Ops:
  1.3 3.8 %front.2 = (bf16[640,256]{1,0:T(8,128)(2,1)}, bf16[128,512]{1,0:T(8,128)(2,1)}, f32[128,512]{1,0:T(8,128)}) custom-call(s32[1]{0:T(128)} %bitcast.me_ref, s32[1]{0:T(128)S(6)} %copy.14.rank_ref, f32[1024,256]{1,0:T(8,128)} %refs_10_.1, f32[1024,256]{1,0:T(8,128)} %refs_8_.3, f32[256,512]{1,0:T(8,128)} %bitcast.46), custom_call_target="tpu_custom_call" | custom-call | flops 402653184 | bytes 2097152 | tf_op jit(solution)/shard_map/front/pallas_call | solution.py:79
  5.1 1.5 collective-permute-start
  7.0 1.1 slice.7.refs_0_
  8.2 1.6 collective-permute-start.9
  11.6 2.8 %collective-permute-start.1 = (bf16[64,512]{1,0:T(8,128)(2,1)S(1)}, bf16[64,512]{1,0:T(8,128)(2,1)S(1)}, u32[]{:S(2)}, u32[]{:S(2)}) collective-permute-start(bf16[64,512]{1,0:T(8,128)(2,1)S(1)} %fusion), channel_id=1, source_target_pairs={{0,2},{1,3},{2,0},{3,1},{4,6},{5,7},{6,4},{7,5},{8,10},{9,11},{10,... | collective-permute-start | bytes 196616 | tf_op jit(solution)/shard_map/ppermute | solution.py:368
  14.4 2.0 %collective-permute-start.15 = (bf16[640,256]{1,0:T(8,128)(2,1)S(1)}, bf16[640,256]{1,0:T(8,128)(2,1)S(1)}, u32[]{:S(2)}, u32[]{:S(2)}) collective-permute-start(bf16[640,256]{1,0:T(8,128)(2,1)S(1)} %slice.7.refs_0_), channel_id=1, source_target_pairs={{2,0},{4,2},{6,4},{7,6},{5,7},{3,5},{1,3},{0,1},{10,8},{12,10},{14... | collective-permute-start | bytes 983048 | tf_op jit(solution)/shard_map/ppermute | solution.py:371
  16.4 1.0 collective-permute-done.18.refs_5_
  17.4 1.4 collective-permute-done.9.refs_2_
  18.8 1.6 collective-permute-start.10
  20.8 5.6 %collective-permute-done.12.refs_3_ = bf16[640,256]{1,0:T(8,128)(2,1)S(1)} collective-permute-done((bf16[640,256]{1,0:T(8,128)(2,1)}, bf16[640,256]{1,0:T(8,128)(2,1)S(1)}, u32[]{:S(2)}, u32[]{:S(2)}) %collective-permute-start.12) | collective-permute-done | bytes 327712 | tf_op jit(solution)/shard_map/ppermute | solution.py:371
  26.4 2.4 %collective-permute-start.13 = (bf16[640,256]{1,0:T(8,128)(2,1)S(1)}, bf16[640,256]{1,0:T(8,128)(2,1)}, u32[]{:S(2)}, u32[]{:S(2)}) collective-permute-start(bf16[640,256]{1,0:T(8,128)(2,1)S(1)} %collective-permute-done.12.refs_3_), channel_id=1, source_target_pairs={{0,2},{2,4},{4,6},{6,7},{7,5},{5,3},{3,1},{1,0},{8,10},{10,12},{12... | collective-permute-start | bytes 983048 | tf_op jit(solution)/shard_map/ppermute | solution.py:371
  28.8 4.0 %collective-permute-done.19.refs_3_ = bf16[640,256]{1,0:T(8,128)(2,1)S(1)} collective-permute-done((bf16[640,256]{1,0:T(8,128)(2,1)S(1)}, bf16[640,256]{1,0:T(8,128)(2,1)S(1)}, u32[]{:S(2)}, u32[]{:S(2)}) %collective-permute-start.19) | collective-permute-done | bytes 327712 | tf_op jit(solution)/shard_map/ppermute | solution.py:371
  32.8 1.0 collective-permute-start.20
  34.1 2.5 %collective-permute-start.11 = (bf16[640,256]{1,0:T(8,128)(2,1)S(1)}, bf16[640,256]{1,0:T(8,128)(2,1)S(1)}, u32[]{:S(2)}, u32[]{:S(2)}) collective-permute-start(bf16[640,256]{1,0:T(8,128)(2,1)S(1)} %collective-permute-done.10.refs_0_), channel_id=1, source_target_pairs={{0,2},{2,4},{4,6},{6,7},{7,5},{5,3},{3,1},{1,0},{8,10},{10,12},{12... | collective-permute-start | bytes 983048 | tf_op jit(solution)/shard_map/ppermute | solution.py:371
  36.7 1.2 collective-permute-done.3.refs_1_
  37.9 1.5 collective-permute-start.4
  39.4 2.4 %collective-permute-done.4.refs_2_ = bf16[32,512]{1,0:T(8,128)(2,1)S(1)} collective-permute-done((bf16[32,512]{1,0:T(8,128)(2,1)S(1)}, bf16[32,512]{1,0:T(8,128)(2,1)S(1)}, u32[]{:S(2)}, u32[]{:S(2)}) %collective-permute-start.4) | collective-permute-done | bytes 32800 | tf_op jit(solution)/shard_map/ppermute | solution.py:368
  42.3 3.1 %collective-permute-done.5.refs_3_ = bf16[32,512]{1,0:T(8,128)(2,1)S(1)} collective-permute-done((bf16[32,512]{1,0:T(8,128)(2,1)S(1)}, bf16[32,512]{1,0:T(8,128)(2,1)S(1)}, u32[]{:S(2)}, u32[]{:S(2)}) %collective-permute-start.5) | collective-permute-done | bytes 32800 | tf_op jit(solution)/shard_map/ppermute | solution.py:368
  46.0 3.0 %far.2.refs_0_ = bf16[32,512]{1,0:T(8,128)(2,1)} custom-call(s32[1]{0:T(128)} %bitcast.3.row_ref, s32[1,2]{1,0:T(1,128)} %links_ref.3, bf16[32,512]{1,0:T(8,128)(2,1)} %copy-done.28, bf16[32,512]{1,0:T(8,128)(2,1)} %copy-done.30, bf16[32,512]{1,0:T(8,128)(2,1)} %copy-done.31, bf16[32,512]{1,0:T(8,128)(2,1)} %copy-done.33, f32[2,512,512]{2,1,0:T(8,128)} %bitcast.50), custom_call_target="tpu_custom_call" | custom-call | flops 16777216 | bytes 2097152 | tf_op jit(solution)/shard_map/far/pallas_call | solution.py:214
  49.7 4.4 %collective-permute-done.6.refs_1_ = bf16[32,512]{1,0:T(8,128)(2,1)S(1)} collective-permute-done((bf16[32,512]{1,0:T(8,128)(2,1)}, bf16[32,512]{1,0:T(8,128)(2,1)S(1)}, u32[]{:S(2)}, u32[]{:S(2)}) %collective-permute-start.6) | collective-permute-done | bytes 32800 | tf_op jit(solution)/shard_map/ppermute | solution.py:368
  54.8 2.0 %collective-permute-start.14 = (bf16[640,256]{1,0:T(8,128)(2,1)}, bf16[640,256]{1,0:T(8,128)(2,1)}, u32[]{:S(2)}, u32[]{:S(2)}) collective-permute-start(bf16[640,256]{1,0:T(8,128)(2,1)} %collective-permute-done.13.refs_1_), channel_id=1, source_target_pairs={{0,2},{2,4},{4,6},{6,7},{7,5},{5,3},{3,1},{1,0},{8,10},{10,12},{12... | collective-permute-start | bytes 983048 | tf_op jit(solution)/shard_map/ppermute | solution.py:371
  56.9 1.1 collective-permute-start.22
  59.0 6.6 %absorb.6 = (f32[1024,256]{1,0:T(8,128)}, f32[256,256]{1,0:T(8,128)}) custom-call(s32[1]{0:T(128)} %bitcast.me_ref, s32[1,8]{1,0:T(1,128)} %nears_ref.15, s32[1]{0:T(128)S(6)} %copy.13.count_ref, s32[1,4]{1,0:T(1,128)} %ties_ref.15, bf16[8,1024,1024]{2,1,0:T(8,128)(2,1)} %bitcast.30, f32[4,256,256]{2,1,0:T(8,128)} %bitcast.38, bf16[640,256]{1,0:T(8,128)(2,1)} %copy-done, ...), custom_call_target="tpu_custom_call" | custom-call | flops 1610612736 | bytes 12582912 | tf_op jit(solution)/shard_map/absorb/pallas_call | solution.py:184
  65.8 5.7 %absorb.7 = (f32[1024,256]{1,0:T(8,128)}, f32[256,256]{1,0:T(8,128)}) custom-call(s32[1]{0:T(128)} %bitcast.me_ref, s32[1,8]{1,0:T(1,128)} %nears_ref.15, s32[1]{0:T(128)S(6)} %copy.13.count_ref, s32[1,4]{1,0:T(1,128)} %ties_ref.15, bf16[8,1024,1024]{2,1,0:T(8,128)(2,1)} %bitcast.31, f32[4,256,256]{2,1,0:T(8,128)} %bitcast.39, bf16[640,256]{1,0:T(8,128)(2,1)} %copy-done.10, ...), custom_call_target="tpu_custom_call" | custom-call | flops 1073741824 | bytes 8388608 | tf_op jit(solution)/shard_map/absorb/pallas_call | solution.py:184
  71.5 5.6 %absorb.8 = (f32[1024,256]{1,0:T(8,128)}, f32[256,256]{1,0:T(8,128)}) custom-call(s32[1]{0:T(128)} %bitcast.me_ref, s32[1,8]{1,0:T(1,128)} %nears_ref.15, s32[1]{0:T(128)S(6)} %copy.13.count_ref, s32[1,4]{1,0:T(1,128)} %ties_ref.15, bf16[8,1024,1024]{2,1,0:T(8,128)(2,1)} %bitcast.32, f32[4,256,256]{2,1,0:T(8,128)} %bitcast.40, bf16[640,256]{1,0:T(8,128)(2,1)} %copy-done.16, ...), custom_call_target="tpu_custom_call" | custom-call | flops 1073741824 | bytes 8388608 | tf_op jit(solution)/shard_map/absorb/pallas_call | solution.py:184
  77.9 6.3 %back.2 = (f32[1024,256]{1,0:T(8,128)}, bf16[640,256]{1,0:T(8,128)(2,1)}) custom-call(s32[1]{0:T(128)} %bitcast.me_ref, s32[1,8]{1,0:T(1,128)} %nears_ref.15, s32[1]{0:T(128)S(6)} %copy.13.count_ref, s32[1,4]{1,0:T(1,128)} %ties_ref.15, s32[1]{0:T(128)S(6)} %copy.14.rank_ref, bf16[8,1024,1024]{2,1,0:T(8,128)(2,1)} %bitcast.33, f32[4,256,256]{2,1,0:T(8,128)} %bitcast.41, ...), custom_call_target="tpu_custom_call" | custom-call | flops 1610612736 | bytes 6291456 | tf_op jit(solution)/shard_map/back/pallas_call | solution.py:314
  84.2 3.8 %front.3 = (bf16[640,256]{1,0:T(8,128)(2,1)}, bf16[128,512]{1,0:T(8,128)(2,1)}, f32[128,512]{1,0:T(8,128)}) custom-call(s32[1]{0:T(128)} %bitcast.me_ref, s32[1]{0:T(128)S(6)} %copy.14.rank_ref, f32[1024,256]{1,0:T(8,128)} %get-tuple-element.20.v_ref, f32[1024,256]{1,0:T(8,128)} %refs_8_.3, f32[256,512]{1,0:T(8,128)} %bitcast.48), custom_call_target="tpu_custom_call" | custom-call | flops 402653184 | bytes 2097152 | tf_op jit(solution)/shard_map/front/pallas_call | solution.py:79
  89.2 1.2 collective-permute-start.32
  90.4 2.8 %collective-permute-done.23 = bf16[128,512]{1,0:T(8,128)(2,1)S(1)} collective-permute-done((bf16[128,512]{1,0:T(8,128)(2,1)}, bf16[128,512]{1,0:T(8,128)(2,1)S(1)}, u32[]{:S(2)}, u32[]{:S(2)}) %collective-permute-start.23) | collective-permute-done | bytes 131104 | tf_op jit(solution)/shard_map/ppermute | solution.py:368
  95.2 1.2 collective-permute-start.35
  97.2 2.0 %collective-permute-done.41.refs_5_ = bf16[640,256]{1,0:T(8,128)(2,1)S(1)} collective-permute-done((bf16[640,256]{1,0:T(8,128)(2,1)}, bf16[640,256]{1,0:T(8,128)(2,1)S(1)}, u32[]{:S(2)}, u32[]{:S(2)}) %collective-permute-start.41) | collective-permute-done | bytes 327712 | tf_op jit(solution)/shard_map/ppermute | solution.py:371
  99.2 2.0 %collective-permute-start.33 = (bf16[640,256]{1,0:T(8,128)(2,1)S(1)}, bf16[640,256]{1,0:T(8,128)(2,1)S(1)}, u32[]{:S(2)}, u32[]{:S(2)}) collective-permute-start(bf16[640,256]{1,0:T(8,128)(2,1)S(1)} %collective-permute-done.32.refs_2_), channel_id=1, source_target_pairs={{0,2},{2,4},{4,6},{6,7},{7,5},{5,3},{3,1},{1,0},{8,10},{10,12},{12... | collective-permute-start | bytes 983048 | tf_op jit(solution)/shard_map/ppermute | solution.py:371
  101.6 5.7 %collective-permute-done.35.refs_3_ = bf16[640,256]{1,0:T(8,128)(2,1)S(1)} collective-permute-done((bf16[640,256]{1,0:T(8,128)(2,1)}, bf16[640,256]{1,0:T(8,128)(2,1)S(1)}, u32[]{:S(2)}, u32[]{:S(2)}) %collective-permute-start.35) | collective-permute-done | bytes 327712 | tf_op jit(solution)/shard_map/ppermute | solution.py:371
  107.3 2.4 %collective-permute-start.36 = (bf16[640,256]{1,0:T(8,128)(2,1)S(1)}, bf16[640,256]{1,0:T(8,128)(2,1)S(1)}, u32[]{:S(2)}, u32[]{:S(2)}) collective-permute-start(bf16[640,256]{1,0:T(8,128)(2,1)S(1)} %collective-permute-done.35.refs_3_), channel_id=1, source_target_pairs={{0,2},{2,4},{4,6},{6,7},{7,5},{5,3},{3,1},{1,0},{8,10},{10,12},{12... | collective-permute-start | bytes 983048 | tf_op jit(solution)/shard_map/ppermute | solution.py:371
  109.7 5.0 %collective-permute-done.42.refs_3_ = bf16[640,256]{1,0:T(8,128)(2,1)S(1)} collective-permute-done((bf16[640,256]{1,0:T(8,128)(2,1)S(1)}, bf16[640,256]{1,0:T(8,128)(2,1)S(1)}, u32[]{:S(2)}, u32[]{:S(2)}) %collective-permute-start.42) | collective-permute-done | bytes 327712 | tf_op jit(solution)/shard_map/ppermute | solution.py:371
  114.9 2.5 %collective-permute-start.34 = (bf16[640,256]{1,0:T(8,128)(2,1)S(1)}, bf16[640,256]{1,0:T(8,128)(2,1)S(1)}, u32[]{:S(2)}, u32[]{:S(2)}) collective-permute-start(bf16[640,256]{1,0:T(8,128)(2,1)S(1)} %collective-permute-done.33.refs_0_), channel_id=1, source_target_pairs={{0,2},{2,4},{4,6},{6,7},{7,5},{5,3},{3,1},{1,0},{8,10},{10,12},{12... | collective-permute-start | bytes 983048 | tf_op jit(solution)/shard_map/ppermute | solution.py:371
  117.5 1.2 collective-permute-done.26.refs_1_
  119.1 3.5 %collective-permute-done.27.refs_2_ = bf16[32,512]{1,0:T(8,128)(2,1)S(1)} collective-permute-done((bf16[32,512]{1,0:T(8,128)(2,1)S(1)}, bf16[32,512]{1,0:T(8,128)(2,1)S(1)}, u32[]{:S(2)}, u32[]{:S(2)}) %collective-permute-start.27) | collective-permute-done | bytes 32800 | tf_op jit(solution)/shard_map/ppermute | solution.py:368
  122.6 3.3 %collective-permute-done.28.refs_3_ = bf16[32,512]{1,0:T(8,128)(2,1)S(1)} collective-permute-done((bf16[32,512]{1,0:T(8,128)(2,1)S(1)}, bf16[32,512]{1,0:T(8,128)(2,1)S(1)}, u32[]{:S(2)}, u32[]{:S(2)}) %collective-permute-start.28) | collective-permute-done | bytes 32800 | tf_op jit(solution)/shard_map/ppermute | solution.py:368
  126.6 3.0 %far.3.refs_0_ = bf16[32,512]{1,0:T(8,128)(2,1)} custom-call(s32[1]{0:T(128)} %bitcast.3.row_ref, s32[1,2]{1,0:T(1,128)} %links_ref.3, bf16[32,512]{1,0:T(8,128)(2,1)} %copy-done.29, bf16[32,512]{1,0:T(8,128)(2,1)} %copy-done.32, bf16[32,512]{1,0:T(8,128)(2,1)} %copy-done.34, bf16[32,512]{1,0:T(8,128)(2,1)} %copy-done.35, f32[2,512,512]{2,1,0:T(8,128)} %bitcast.51), custom_call_target="tpu_custom_call" | custom-call | flops 16777216 | bytes 2097152 | tf_op jit(solution)/shard_map/far/pallas_call | solution.py:214
  129.6 1.5 collective-permute-start.29
  131.1 3.5 %collective-permute-done.29.refs_1_ = bf16[32,512]{1,0:T(8,128)(2,1)S(1)} collective-permute-done((bf16[32,512]{1,0:T(8,128)(2,1)}, bf16[32,512]{1,0:T(8,128)(2,1)S(1)}, u32[]{:S(2)}, u32[]{:S(2)}) %collective-permute-start.29) | collective-permute-done | bytes 32800 | tf_op jit(solution)/shard_map/ppermute | solution.py:368
  135.9 1.5 collective-permute-start.37
  138.0 2.0 %collective-permute-start.45 = (bf16[640,256]{1,0:T(8,128)(2,1)S(1)}, bf16[640,256]{1,0:T(8,128)(2,1)}, u32[]{:S(2)}, u32[]{:S(2)}) collective-permute-start(bf16[640,256]{1,0:T(8,128)(2,1)S(1)} %collective-permute-done.43.refs_3_), channel_id=1, source_target_pairs={{2,0},{4,2},{6,4},{7,6},{5,7},{3,5},{1,3},{0,1},{10,8},{12,10},{14... | collective-permute-start | bytes 983048 | tf_op jit(solution)/shard_map/ppermute | solution.py:371
  140.0 6.6 %absorb.9 = (f32[1024,256]{1,0:T(8,128)}, f32[256,256]{1,0:T(8,128)}) custom-call(s32[1]{0:T(128)} %bitcast.me_ref, s32[1,8]{1,0:T(1,128)} %nears_ref.15, s32[1]{0:T(128)S(6)} %copy.13.count_ref, s32[1,4]{1,0:T(1,128)} %ties_ref.15, bf16[8,1024,1024]{2,1,0:T(8,128)(2,1)} %bitcast.34, f32[4,256,256]{2,1,0:T(8,128)} %bitcast.42, ...), custom_call_target="tpu_custom_call" | custom-call | flops 1610612736 | bytes 12582912 | tf_op jit(solution)/shard_map/absorb/pallas_call | solution.py:184
  147.1 5.7 %absorb.10 = (f32[1024,256]{1,0:T(8,128)}, f32[256,256]{1,0:T(8,128)}) custom-call(s32[1]{0:T(128)} %bitcast.me_ref, s32[1,8]{1,0:T(1,128)} %nears_ref.15, s32[1]{0:T(128)S(6)} %copy.13.count_ref, s32[1,4]{1,0:T(1,128)} %ties_ref.15, bf16[8,1024,1024]{2,1,0:T(8,128)(2,1)} %bitcast.35, f32[4,256,256]{2,1,0:T(8,128)} %bitcast.43, bf16[640,256]{1,0:T(8,128)(2,1)} %copy-done.13, ...), custom_call_target="tpu_custom_call" | custom-call | flops 1073741824 | bytes 8388608 | tf_op jit(solution)/shard_map/absorb/pallas_call | solution.py:184
  152.8 5.6 %absorb.11 = (f32[1024,256]{1,0:T(8,128)}, f32[256,256]{1,0:T(8,128)}) custom-call(s32[1]{0:T(128)} %bitcast.me_ref, s32[1,8]{1,0:T(1,128)} %nears_ref.15, s32[1]{0:T(128)S(6)} %copy.13.count_ref, s32[1,4]{1,0:T(1,128)} %ties_ref.15, bf16[8,1024,1024]{2,1,0:T(8,128)(2,1)} %bitcast.36, f32[4,256,256]{2,1,0:T(8,128)} %bitcast.44, bf16[640,256]{1,0:T(8,128)(2,1)} %copy-done.18, ...), custom_call_target="tpu_custom_call" | custom-call | flops 1073741824 | bytes 8388608 | tf_op jit(solution)/shard_map/absorb/pallas_call | solution.py:184
  159.1 6.1 %back.3 = f32[1024,256]{1,0:T(8,128)} custom-call(s32[1]{0:T(128)} %bitcast.me_ref, s32[1,8]{1,0:T(1,128)} %nears_ref.15, s32[1]{0:T(128)S(6)} %copy.13.count_ref, s32[1,4]{1,0:T(1,128)} %ties_ref.15, s32[1]{0:T(128)S(6)} %copy.14.rank_ref, bf16[8,1024,1024]{2,1,0:T(8,128)(2,1)} %bitcast.37, f32[4,256,256]{2,1,0:T(8,128)} %bitcast.45, ...), custom_call_target="tpu_custom_call" | custom-call | flops 1610612736 | bytes 6291456 | tf_op jit(solution)/shard_map/back/pallas_call | solution.py:314
  (143 shorter events, 15.4 us)
Async XLA Ops:
  5.1 5.4 %collective-permute-start = (bf16[128,512]{1,0:T(8,128)(2,1)}, bf16[128,512]{1,0:T(8,128)(2,1)S(1)}, u32[]{:S(2)}, u32[]{:S(2)}) collective-permute-start(bf16[128,512]{1,0:T(8,128)(2,1)} %get-tuple-element.23), channel_id=1, source_target_pairs={{0,1},{1,0},{2,3},{3,2},{4,5},{5,4},{6,7},{7,6},{8,9},{9,8},{10,11... | collective-permute-start | bytes 393224 | tf_op jit(solution)/shard_map/ppermute | solution.py:368
  6.6 10.8 %collective-permute-start.18 = (bf16[640,256]{1,0:T(8,128)(2,1)}, bf16[640,256]{1,0:T(8,128)(2,1)S(1)}, u32[]{:S(2)}, u32[]{:S(2)}) collective-permute-start(bf16[640,256]{1,0:T(8,128)(2,1)} %get-tuple-element.24.refs_1_), channel_id=1, source_target_pairs={{2,0},{4,2},{6,4},{7,6},{5,7},{3,5},{1,3},{0,1},{10,8},{12,10},{14... | collective-permute-start | bytes 983048 | tf_op jit(solution)/shard_map/ppermute | solution.py:371
  8.2 50.8 %copy-start = (bf16[640,256]{1,0:T(8,128)(2,1)}, bf16[640,256]{1,0:T(8,128)(2,1)S(1)}, u32[]{:S(2)}) copy-start(bf16[640,256]{1,0:T(8,128)(2,1)S(1)} %slice.7.refs_0_) | copy-start | bytes 983044
  8.2 10.6 %collective-permute-start.9 = (bf16[640,256]{1,0:T(8,128)(2,1)S(1)}, bf16[640,256]{1,0:T(8,128)(2,1)S(1)}, u32[]{:S(2)}, u32[]{:S(2)}) collective-permute-start(bf16[640,256]{1,0:T(8,128)(2,1)S(1)} %slice.7.refs_0_), channel_id=1, source_target_pairs={{0,2},{2,4},{4,6},{6,7},{7,5},{5,3},{3,1},{1,0},{8,10},{10,12},{12... | collective-permute-start | bytes 983048 | tf_op jit(solution)/shard_map/ppermute | solution.py:371
  11.6 8.8 %collective-permute-start.1 = (bf16[64,512]{1,0:T(8,128)(2,1)S(1)}, bf16[64,512]{1,0:T(8,128)(2,1)S(1)}, u32[]{:S(2)}, u32[]{:S(2)}) collective-permute-start(bf16[64,512]{1,0:T(8,128)(2,1)S(1)} %fusion), channel_id=1, source_target_pairs={{0,2},{1,3},{2,0},{3,1},{4,6},{5,7},{6,4},{7,5},{8,10},{9,11},{10,... | collective-permute-start | bytes 196616 | tf_op jit(solution)/shard_map/ppermute | solution.py:368
  14.3 12.1 %collective-permute-start.12 = (bf16[640,256]{1,0:T(8,128)(2,1)}, bf16[640,256]{1,0:T(8,128)(2,1)S(1)}, u32[]{:S(2)}, u32[]{:S(2)}) collective-permute-start(bf16[640,256]{1,0:T(8,128)(2,1)} %get-tuple-element.24.refs_1_), channel_id=1, source_target_pairs={{0,2},{2,4},{4,6},{6,7},{7,5},{5,3},{3,1},{1,0},{8,10},{10,12},{12... | collective-permute-start | bytes 983048 | tf_op jit(solution)/shard_map/ppermute | solution.py:371
  14.4 14.4 %collective-permute-start.15 = (bf16[640,256]{1,0:T(8,128)(2,1)S(1)}, bf16[640,256]{1,0:T(8,128)(2,1)S(1)}, u32[]{:S(2)}, u32[]{:S(2)}) collective-permute-start(bf16[640,256]{1,0:T(8,128)(2,1)S(1)} %slice.7.refs_0_), channel_id=1, source_target_pairs={{2,0},{4,2},{6,4},{7,6},{5,7},{3,5},{1,3},{0,1},{10,8},{12,10},{14... | collective-permute-start | bytes 983048 | tf_op jit(solution)/shard_map/ppermute | solution.py:371
  17.4 41.6 %copy-start.3 = (bf16[640,256]{1,0:T(8,128)(2,1)}, bf16[640,256]{1,0:T(8,128)(2,1)S(1)}, u32[]{:S(2)}) copy-start(bf16[640,256]{1,0:T(8,128)(2,1)S(1)} %collective-permute-done.18.refs_5_) | copy-start | bytes 983044
  17.4 15.4 %collective-permute-start.19 = (bf16[640,256]{1,0:T(8,128)(2,1)S(1)}, bf16[640,256]{1,0:T(8,128)(2,1)S(1)}, u32[]{:S(2)}, u32[]{:S(2)}) collective-permute-start(bf16[640,256]{1,0:T(8,128)(2,1)S(1)} %collective-permute-done.18.refs_5_), channel_id=1, source_target_pairs={{2,0},{4,2},{6,4},{7,6},{5,7},{3,5},{1,3},{0,1},{10,8},{12,10},{14... | collective-permute-start | bytes 983048 | tf_op jit(solution)/shard_map/ppermute | solution.py:371
  18.8 15.2 %collective-permute-start.10 = (bf16[640,256]{1,0:T(8,128)(2,1)S(1)}, bf16[640,256]{1,0:T(8,128)(2,1)S(1)}, u32[]{:S(2)}, u32[]{:S(2)}) collective-permute-start(bf16[640,256]{1,0:T(8,128)(2,1)S(1)} %collective-permute-done.9.refs_2_), channel_id=1, source_target_pairs={{0,2},{2,4},{4,6},{6,7},{7,5},{5,3},{3,1},{1,0},{8,10},{10,12},{12... | collective-permute-start | bytes 983048 | tf_op jit(solution)/shard_map/ppermute | solution.py:371
  20.4 16.1 %collective-permute-start.2 = (bf16[32,512]{1,0:T(8,128)(2,1)S(1)}, bf16[32,512]{1,0:T(8,128)(2,1)S(1)}, u32[]{:S(2)}, u32[]{:S(2)}) collective-permute-start(bf16[32,512]{1,0:T(8,128)(2,1)S(1)} %fusion.4), channel_id=1, source_target_pairs={{0,4},{1,5},{2,6},{3,7},{4,0},{5,1},{6,2},{7,3},{8,12},{9,13},{10,... | collective-permute-start | bytes 98312 | tf_op jit(solution)/shard_map/ppermute | solution.py:368
  26.4 28.4 %collective-permute-start.13 = (bf16[640,256]{1,0:T(8,128)(2,1)S(1)}, bf16[640,256]{1,0:T(8,128)(2,1)}, u32[]{:S(2)}, u32[]{:S(2)}) collective-permute-start(bf16[640,256]{1,0:T(8,128)(2,1)S(1)} %collective-permute-done.12.refs_3_), channel_id=1, source_target_pairs={{0,2},{2,4},{4,6},{6,7},{7,5},{5,3},{3,1},{1,0},{8,10},{10,12},{12... | collective-permute-start | bytes 983048 | tf_op jit(solution)/shard_map/ppermute | solution.py:371
  28.8 28.0 %collective-permute-start.16 = (bf16[640,256]{1,0:T(8,128)(2,1)S(1)}, bf16[640,256]{1,0:T(8,128)(2,1)}, u32[]{:S(2)}, u32[]{:S(2)}) collective-permute-start(bf16[640,256]{1,0:T(8,128)(2,1)S(1)} %collective-permute-done.15.refs_4_), channel_id=1, source_target_pairs={{2,0},{4,2},{6,4},{7,6},{5,7},{3,5},{1,3},{0,1},{10,8},{12,10},{14... | collective-permute-start | bytes 983048 | tf_op jit(solution)/shard_map/ppermute | solution.py:371
  32.8 24.1 %collective-permute-start.20 = (bf16[640,256]{1,0:T(8,128)(2,1)S(1)}, bf16[640,256]{1,0:T(8,128)(2,1)S(1)}, u32[]{:S(2)}, u32[]{:S(2)}) collective-permute-start(bf16[640,256]{1,0:T(8,128)(2,1)S(1)} %collective-permute-done.19.refs_3_), channel_id=1, source_target_pairs={{2,0},{4,2},{6,4},{7,6},{5,7},{3,5},{1,3},{0,1},{10,8},{12,10},{14... | collective-permute-start | bytes 983048 | tf_op jit(solution)/shard_map/ppermute | solution.py:371
  34.1 24.0 %collective-permute-start.11 = (bf16[640,256]{1,0:T(8,128)(2,1)S(1)}, bf16[640,256]{1,0:T(8,128)(2,1)S(1)}, u32[]{:S(2)}, u32[]{:S(2)}) collective-permute-start(bf16[640,256]{1,0:T(8,128)(2,1)S(1)} %collective-permute-done.10.refs_0_), channel_id=1, source_target_pairs={{0,2},{2,4},{4,6},{6,7},{7,5},{5,3},{3,1},{1,0},{8,10},{10,12},{12... | collective-permute-start | bytes 983048 | tf_op jit(solution)/shard_map/ppermute | solution.py:371
  36.6 1.3 collective-permute-start.3
  37.9 3.9 %collective-permute-start.4 = (bf16[32,512]{1,0:T(8,128)(2,1)S(1)}, bf16[32,512]{1,0:T(8,128)(2,1)S(1)}, u32[]{:S(2)}, u32[]{:S(2)}) collective-permute-start(bf16[32,512]{1,0:T(8,128)(2,1)S(1)} %fusion.3.refs_0_), channel_id=1, source_target_pairs={{0,16},{8,24},{16,0},{24,8},{1,17},{9,25},{17,1},{25,9},{2,18},{10... | collective-permute-start | bytes 98312 | tf_op jit(solution)/shard_map/ppermute | solution.py:368
  41.8 3.6 %collective-permute-start.5 = (bf16[32,512]{1,0:T(8,128)(2,1)S(1)}, bf16[32,512]{1,0:T(8,128)(2,1)S(1)}, u32[]{:S(2)}, u32[]{:S(2)}) collective-permute-start(bf16[32,512]{1,0:T(8,128)(2,1)S(1)} %fusion.3.refs_0_), channel_id=1, source_target_pairs={{0,24},{8,16},{16,8},{24,0},{1,25},{9,17},{17,9},{25,1},{2,26},{10... | collective-permute-start | bytes 98312 | tf_op jit(solution)/shard_map/ppermute | solution.py:368
  49.0 5.0 %collective-permute-start.6 = (bf16[32,512]{1,0:T(8,128)(2,1)}, bf16[32,512]{1,0:T(8,128)(2,1)S(1)}, u32[]{:S(2)}, u32[]{:S(2)}) collective-permute-start(bf16[32,512]{1,0:T(8,128)(2,1)} %far.2.refs_0_), channel_id=1, source_target_pairs={{0,4},{1,5},{2,6},{3,7},{4,0},{5,1},{6,2},{7,3},{8,12},{9,13},{10,... | collective-permute-start | bytes 98312 | tf_op jit(solution)/shard_map/ppermute | solution.py:368
  54.8 10.8 %collective-permute-start.7 = (bf16[64,512]{1,0:T(8,128)(2,1)S(1)}, bf16[64,512]{1,0:T(8,128)(2,1)S(1)}, u32[]{:S(2)}, u32[]{:S(2)}) collective-permute-start(bf16[64,512]{1,0:T(8,128)(2,1)S(1)} %pad_maximum_fusion.2), channel_id=1, source_target_pairs={{0,2},{1,3},{2,0},{3,1},{4,6},{5,7},{6,4},{7,5},{8,10},{9,11},{10,... | collective-permute-start | bytes 196616 | tf_op jit(solution)/shard_map/ppermute | solution.py:368
  54.8 16.7 %collective-permute-start.14 = (bf16[640,256]{1,0:T(8,128)(2,1)}, bf16[640,256]{1,0:T(8,128)(2,1)}, u32[]{:S(2)}, u32[]{:S(2)}) collective-permute-start(bf16[640,256]{1,0:T(8,128)(2,1)} %collective-permute-done.13.refs_1_), channel_id=1, source_target_pairs={{0,2},{2,4},{4,6},{6,7},{7,5},{5,3},{3,1},{1,0},{8,10},{10,12},{12... | collective-permute-start | bytes 983048 | tf_op jit(solution)/shard_map/ppermute | solution.py:371
  56.9 14.7 %collective-permute-start.17 = (bf16[640,256]{1,0:T(8,128)(2,1)}, bf16[640,256]{1,0:T(8,128)(2,1)}, u32[]{:S(2)}, u32[]{:S(2)}) collective-permute-start(bf16[640,256]{1,0:T(8,128)(2,1)} %collective-permute-done.16.refs_2_), channel_id=1, source_target_pairs={{2,0},{4,2},{6,4},{7,6},{5,7},{3,5},{1,3},{0,1},{10,8},{12,10},{14... | collective-permute-start | bytes 983048 | tf_op jit(solution)/shard_map/ppermute | solution.py:371
  56.9 20.2 %collective-permute-start.22 = (bf16[640,256]{1,0:T(8,128)(2,1)S(1)}, bf16[640,256]{1,0:T(8,128)(2,1)S(1)}, u32[]{:S(2)}, u32[]{:S(2)}) collective-permute-start(bf16[640,256]{1,0:T(8,128)(2,1)S(1)} %collective-permute-done.20.refs_3_), channel_id=1, source_target_pairs={{2,0},{4,2},{6,4},{7,6},{5,7},{3,5},{1,3},{0,1},{10,8},{12,10},{14... | collective-permute-start | bytes 983048 | tf_op jit(solution)/shard_map/ppermute | solution.py:371
  58.1 19.1 %collective-permute-start.21 = (bf16[640,256]{1,0:T(8,128)(2,1)S(1)}, bf16[640,256]{1,0:T(8,128)(2,1)}, u32[]{:S(2)}, u32[]{:S(2)}) collective-permute-start(bf16[640,256]{1,0:T(8,128)(2,1)S(1)} %collective-permute-done.11.refs_0_), channel_id=1, source_target_pairs={{0,2},{2,4},{4,6},{6,7},{7,5},{5,3},{3,1},{1,0},{8,10},{10,12},{12... | collective-permute-start | bytes 983048 | tf_op jit(solution)/shard_map/ppermute | solution.py:371
  65.7 11.5 %collective-permute-start.8 = (bf16[128,512]{1,0:T(8,128)(2,1)S(1)}, bf16[128,512]{1,0:T(8,128)(2,1)S(1)}, u32[]{:S(2)}, u32[]{:S(2)}) collective-permute-start(bf16[128,512]{1,0:T(8,128)(2,1)S(1)} %pad_maximum_fusion), channel_id=1, source_target_pairs={{0,1},{1,0},{2,3},{3,2},{4,5},{5,4},{6,7},{7,6},{8,9},{9,8},{10,11... | collective-permute-start | bytes 393224 | tf_op jit(solution)/shard_map/ppermute | solution.py:368
  88.1 5.2 %collective-permute-start.23 = (bf16[128,512]{1,0:T(8,128)(2,1)}, bf16[128,512]{1,0:T(8,128)(2,1)S(1)}, u32[]{:S(2)}, u32[]{:S(2)}) collective-permute-start(bf16[128,512]{1,0:T(8,128)(2,1)} %get-tuple-element.33), channel_id=1, source_target_pairs={{0,1},{1,0},{2,3},{3,2},{4,5},{5,4},{6,7},{7,6},{8,9},{9,8},{10,11... | collective-permute-start | bytes 393224 | tf_op jit(solution)/shard_map/ppermute | solution.py:368
  88.4 10.8 %collective-permute-start.41 = (bf16[640,256]{1,0:T(8,128)(2,1)}, bf16[640,256]{1,0:T(8,128)(2,1)S(1)}, u32[]{:S(2)}, u32[]{:S(2)}) collective-permute-start(bf16[640,256]{1,0:T(8,128)(2,1)} %get-tuple-element.35.refs_1_), channel_id=1, source_target_pairs={{2,0},{4,2},{6,4},{7,6},{5,7},{3,5},{1,3},{0,1},{10,8},{12,10},{14... | collective-permute-start | bytes 983048 | tf_op jit(solution)/shard_map/ppermute | solution.py:371
  89.2 10.0 %collective-permute-start.32 = (bf16[640,256]{1,0:T(8,128)(2,1)}, bf16[640,256]{1,0:T(8,128)(2,1)S(1)}, u32[]{:S(2)}, u32[]{:S(2)}) collective-permute-start(bf16[640,256]{1,0:T(8,128)(2,1)} %get-tuple-element.34.refs_0_), channel_id=1, source_target_pairs={{0,2},{2,4},{4,6},{6,7},{7,5},{5,3},{3,1},{1,0},{8,10},{10,12},{12... | collective-permute-start | bytes 983048 | tf_op jit(solution)/shard_map/ppermute | solution.py:371
  94.3 7.0 %collective-permute-start.24 = (bf16[64,512]{1,0:T(8,128)(2,1)S(1)}, bf16[64,512]{1,0:T(8,128)(2,1)S(1)}, u32[]{:S(2)}, u32[]{:S(2)}) collective-permute-start(bf16[64,512]{1,0:T(8,128)(2,1)S(1)} %fusion.1), channel_id=1, source_target_pairs={{0,2},{1,3},{2,0},{3,1},{4,6},{5,7},{6,4},{7,5},{8,10},{9,11},{10,... | collective-permute-start | bytes 196616 | tf_op jit(solution)/shard_map/ppermute | solution.py:368
  95.2 12.1 %collective-permute-start.35 = (bf16[640,256]{1,0:T(8,128)(2,1)}, bf16[640,256]{1,0:T(8,128)(2,1)S(1)}, u32[]{:S(2)}, u32[]{:S(2)}) collective-permute-start(bf16[640,256]{1,0:T(8,128)(2,1)} %get-tuple-element.35.refs_1_), channel_id=1, source_target_pairs={{0,2},{2,4},{4,6},{6,7},{7,5},{5,3},{3,1},{1,0},{8,10},{10,12},{12... | collective-permute-start | bytes 983048 | tf_op jit(solution)/shard_map/ppermute | solution.py:371
  96.4 13.3 %collective-permute-start.38 = (bf16[640,256]{1,0:T(8,128)(2,1)}, bf16[640,256]{1,0:T(8,128)(2,1)S(1)}, u32[]{:S(2)}, u32[]{:S(2)}) collective-permute-start(bf16[640,256]{1,0:T(8,128)(2,1)} %get-tuple-element.34.refs_0_), channel_id=1, source_target_pairs={{2,0},{4,2},{6,4},{7,6},{5,7},{3,5},{1,3},{0,1},{10,8},{12,10},{14... | collective-permute-start | bytes 983048 | tf_op jit(solution)/shard_map/ppermute | solution.py:371
  99.2 15.4 %collective-permute-start.42 = (bf16[640,256]{1,0:T(8,128)(2,1)S(1)}, bf16[640,256]{1,0:T(8,128)(2,1)S(1)}, u32[]{:S(2)}, u32[]{:S(2)}) collective-permute-start(bf16[640,256]{1,0:T(8,128)(2,1)S(1)} %collective-permute-done.41.refs_5_), channel_id=1, source_target_pairs={{2,0},{4,2},{6,4},{7,6},{5,7},{3,5},{1,3},{0,1},{10,8},{12,10},{14... | collective-permute-start | bytes 983048 | tf_op jit(solution)/shard_map/ppermute | solution.py:371
  99.2 15.7 %collective-permute-start.33 = (bf16[640,256]{1,0:T(8,128)(2,1)S(1)}, bf16[640,256]{1,0:T(8,128)(2,1)S(1)}, u32[]{:S(2)}, u32[]{:S(2)}) collective-permute-start(bf16[640,256]{1,0:T(8,128)(2,1)S(1)} %collective-permute-done.32.refs_2_), channel_id=1, source_target_pairs={{0,2},{2,4},{4,6},{6,7},{7,5},{5,3},{3,1},{1,0},{8,10},{10,12},{12... | collective-permute-start | bytes 983048 | tf_op jit(solution)/shard_map/ppermute | solution.py:371
  101.3 16.1 %collective-permute-start.25 = (bf16[32,512]{1,0:T(8,128)(2,1)S(1)}, bf16[32,512]{1,0:T(8,128)(2,1)S(1)}, u32[]{:S(2)}, u32[]{:S(2)}) collective-permute-start(bf16[32,512]{1,0:T(8,128)(2,1)S(1)} %fusion.5), channel_id=1, source_target_pairs={{0,4},{1,5},{2,6},{3,7},{4,0},{5,1},{6,2},{7,3},{8,12},{9,13},{10,... | collective-permute-start | bytes 98312 | tf_op jit(solution)/shard_map/ppermute | solution.py:368
  107.3 28.6 %collective-permute-start.36 = (bf16[640,256]{1,0:T(8,128)(2,1)S(1)}, bf16[640,256]{1,0:T(8,128)(2,1)S(1)}, u32[]{:S(2)}, u32[]{:S(2)}) collective-permute-start(bf16[640,256]{1,0:T(8,128)(2,1)S(1)} %collective-permute-done.35.refs_3_), channel_id=1, source_target_pairs={{0,2},{2,4},{4,6},{6,7},{7,5},{5,3},{3,1},{1,0},{8,10},{10,12},{12... | collective-permute-start | bytes 983048 | tf_op jit(solution)/shard_map/ppermute | solution.py:371
  109.7 27.8 %collective-permute-start.39 = (bf16[640,256]{1,0:T(8,128)(2,1)S(1)}, bf16[640,256]{1,0:T(8,128)(2,1)S(1)}, u32[]{:S(2)}, u32[]{:S(2)}) collective-permute-start(bf16[640,256]{1,0:T(8,128)(2,1)S(1)} %collective-permute-done.38.refs_4_), channel_id=1, source_target_pairs={{2,0},{4,2},{6,4},{7,6},{5,7},{3,5},{1,3},{0,1},{10,8},{12,10},{14... | collective-permute-start | bytes 983048 | tf_op jit(solution)/shard_map/ppermute | solution.py:371
  114.7 23.3 %collective-permute-start.43 = (bf16[640,256]{1,0:T(8,128)(2,1)S(1)}, bf16[640,256]{1,0:T(8,128)(2,1)S(1)}, u32[]{:S(2)}, u32[]{:S(2)}) collective-permute-start(bf16[640,256]{1,0:T(8,128)(2,1)S(1)} %collective-permute-done.42.refs_3_), channel_id=1, source_target_pairs={{2,0},{4,2},{6,4},{7,6},{5,7},{3,5},{1,3},{0,1},{10,8},{12,10},{14... | collective-permute-start | bytes 983048 | tf_op jit(solution)/shard_map/ppermute | solution.py:371
  114.9 25.0 %collective-permute-start.34 = (bf16[640,256]{1,0:T(8,128)(2,1)S(1)}, bf16[640,256]{1,0:T(8,128)(2,1)S(1)}, u32[]{:S(2)}, u32[]{:S(2)}) collective-permute-start(bf16[640,256]{1,0:T(8,128)(2,1)S(1)} %collective-permute-done.33.refs_0_), channel_id=1, source_target_pairs={{0,2},{2,4},{4,6},{6,7},{7,5},{5,3},{3,1},{1,0},{8,10},{10,12},{12... | collective-permute-start | bytes 983048 | tf_op jit(solution)/shard_map/ppermute | solution.py:371
  117.4 1.3 collective-permute-start.26
  118.7 3.9 %collective-permute-start.27 = (bf16[32,512]{1,0:T(8,128)(2,1)S(1)}, bf16[32,512]{1,0:T(8,128)(2,1)S(1)}, u32[]{:S(2)}, u32[]{:S(2)}) collective-permute-start(bf16[32,512]{1,0:T(8,128)(2,1)S(1)} %fusion.2.refs_0_), channel_id=1, source_target_pairs={{0,16},{8,24},{16,0},{24,8},{1,17},{9,25},{17,1},{25,9},{2,18},{10... | collective-permute-start | bytes 98312 | tf_op jit(solution)/shard_map/ppermute | solution.py:368
  122.6 3.3 %collective-permute-start.28 = (bf16[32,512]{1,0:T(8,128)(2,1)S(1)}, bf16[32,512]{1,0:T(8,128)(2,1)S(1)}, u32[]{:S(2)}, u32[]{:S(2)}) collective-permute-start(bf16[32,512]{1,0:T(8,128)(2,1)S(1)} %fusion.2.refs_0_), channel_id=1, source_target_pairs={{0,24},{8,16},{16,8},{24,0},{1,25},{9,17},{17,9},{25,1},{2,26},{10... | collective-permute-start | bytes 98312 | tf_op jit(solution)/shard_map/ppermute | solution.py:368
  129.6 5.0 %collective-permute-start.29 = (bf16[32,512]{1,0:T(8,128)(2,1)}, bf16[32,512]{1,0:T(8,128)(2,1)S(1)}, u32[]{:S(2)}, u32[]{:S(2)}) collective-permute-start(bf16[32,512]{1,0:T(8,128)(2,1)} %far.3.refs_0_), channel_id=1, source_target_pairs={{0,4},{1,5},{2,6},{3,7},{4,0},{5,1},{6,2},{7,3},{8,12},{9,13},{10,... | collective-permute-start | bytes 98312 | tf_op jit(solution)/shard_map/ppermute | solution.py:368
  135.4 11.2 %collective-permute-start.30 = (bf16[64,512]{1,0:T(8,128)(2,1)S(1)}, bf16[64,512]{1,0:T(8,128)(2,1)S(1)}, u32[]{:S(2)}, u32[]{:S(2)}) collective-permute-start(bf16[64,512]{1,0:T(8,128)(2,1)S(1)} %pad_maximum_fusion.3), channel_id=1, source_target_pairs={{0,2},{1,3},{2,0},{3,1},{4,6},{5,7},{6,4},{7,5},{8,10},{9,11},{10,... | collective-permute-start | bytes 196616 | tf_op jit(solution)/shard_map/ppermute | solution.py:368
  135.9 16.9 %collective-permute-start.37 = (bf16[640,256]{1,0:T(8,128)(2,1)S(1)}, bf16[640,256]{1,0:T(8,128)(2,1)}, u32[]{:S(2)}, u32[]{:S(2)}) collective-permute-start(bf16[640,256]{1,0:T(8,128)(2,1)S(1)} %collective-permute-done.36.refs_1_), channel_id=1, source_target_pairs={{0,2},{2,4},{4,6},{6,7},{7,5},{5,3},{3,1},{1,0},{8,10},{10,12},{12... | collective-permute-start | bytes 983048 | tf_op jit(solution)/shard_map/ppermute | solution.py:371
  137.4 15.4 %collective-permute-start.40 = (bf16[640,256]{1,0:T(8,128)(2,1)S(1)}, bf16[640,256]{1,0:T(8,128)(2,1)}, u32[]{:S(2)}, u32[]{:S(2)}) collective-permute-start(bf16[640,256]{1,0:T(8,128)(2,1)S(1)} %collective-permute-done.39.refs_2_), channel_id=1, source_target_pairs={{2,0},{4,2},{6,4},{7,6},{5,7},{3,5},{1,3},{0,1},{10,8},{12,10},{14... | collective-permute-start | bytes 983048 | tf_op jit(solution)/shard_map/ppermute | solution.py:371
  138.0 20.5 %collective-permute-start.45 = (bf16[640,256]{1,0:T(8,128)(2,1)S(1)}, bf16[640,256]{1,0:T(8,128)(2,1)}, u32[]{:S(2)}, u32[]{:S(2)}) collective-permute-start(bf16[640,256]{1,0:T(8,128)(2,1)S(1)} %collective-permute-done.43.refs_3_), channel_id=1, source_target_pairs={{2,0},{4,2},{6,4},{7,6},{5,7},{3,5},{1,3},{0,1},{10,8},{12,10},{14... | collective-permute-start | bytes 983048 | tf_op jit(solution)/shard_map/ppermute | solution.py:371
  139.9 18.6 %collective-permute-start.44 = (bf16[640,256]{1,0:T(8,128)(2,1)S(1)}, bf16[640,256]{1,0:T(8,128)(2,1)}, u32[]{:S(2)}, u32[]{:S(2)}) collective-permute-start(bf16[640,256]{1,0:T(8,128)(2,1)S(1)} %collective-permute-done.34.refs_0_), channel_id=1, source_target_pairs={{0,2},{2,4},{4,6},{6,7},{7,5},{5,3},{3,1},{1,0},{8,10},{10,12},{12... | collective-permute-start | bytes 983048 | tf_op jit(solution)/shard_map/ppermute | solution.py:371
  146.7 11.8 %collective-permute-start.31 = (bf16[128,512]{1,0:T(8,128)(2,1)S(1)}, bf16[128,512]{1,0:T(8,128)(2,1)S(1)}, u32[]{:S(2)}, u32[]{:S(2)}) collective-permute-start(bf16[128,512]{1,0:T(8,128)(2,1)S(1)} %pad_maximum_fusion.1), channel_id=1, source_target_pairs={{0,1},{1,0},{2,3},{3,2},{4,5},{5,4},{6,7},{7,6},{8,9},{9,8},{10,11... | collective-permute-start | bytes 393224 | tf_op jit(solution)/shard_map/ppermute | solution.py:368
  (34 other events, 588.2 us)

commit v2 on v1

v2 whole, which is shorter than its diff:
```python
import jax
import jax.numpy as jnp
from jax import lax
from jax.experimental import pallas as pl
from jax.experimental.pallas import tpu as pltpu
from jax.sharding import PartitionSpec as P


F32 = jnp.float32
BF16 = jnp.bfloat16
VMEM = pl.BlockSpec(memory_space=pltpu.VMEM)
SMEM = pl.BlockSpec(memory_space=pltpu.SMEM)
HBM = pl.BlockSpec(memory_space=pltpu.HBM)
ANY = pl.BlockSpec(memory_space=pl.ANY)
ROOM = pltpu.CompilerParams(vmem_limit_bytes=24 * 2**20)


def ring_order(n):
    return list(range(0, n, 2)) + list(range(n - 1, 0, -2))


def halves(x):
    high = x.astype(BF16)
    low = (x - high.astype(F32)).astype(BF16)
    return high, low


def contract(a, b, dims):
    return lax.dot_general(a, b, (dims, ((), ())), preferred_element_type=F32)


def contract3(a, b, dims):
    a_high, a_low = halves(a)
    b_high, b_low = halves(b)
    small = contract(a_low, b_high, dims) + contract(a_high, b_low, dims)
    return small + contract(a_high, b_high, dims)


def contract2(a, b, dims):
    a_high, a_low = halves(a)
    return contract(a_low, b, dims) + contract(a_high, b, dims)


NN = ((1,), (0,))
NT = ((1,), (1,))
TN = ((0,), (0,))


def cost(flops, moved):
    return pl.CostEstimate(flops=int(flops), bytes_accessed=int(moved), transcendentals=0)


def share_of(me, bits):
    share = me & 1
    for b in range(1, bits):
        share = 2 * share + ((me >> b) & 1)
    return share


DEPTH = 3


class Copies:
    def __init__(self, sems):
        self.sems = sems
        self.made = []

    def start(self, source, target, when=None):
        copy = pltpu.make_async_copy(source, target, self.sems.at[len(self.made)])
        self.made.append(copy)
        if when is None:
            copy.start()
        else:
            pl.when(when)(copy.start)
        return copy


def front(me, v, basis, transfer, rank):
    leaf_rows, probe_cols = v.shape
    rank_cols, parent_cols = transfer.shape
    part = (leaf_rows + rank_cols) // 2
    half = probe_cols // 2

    def body(me_ref, rank_ref, v_in, basis_in, transfer_in, bottom_ref, away_ref, kept_ref, v_ref, basis_ref, transfer_ref, upward_ref, sems):
        copies = Copies(sems)
        first = [copies.start(v_in, v_ref), copies.start(basis_in, basis_ref)]
        last = copies.start(transfer_in, transfer_ref)
        for copy in first:
            copy.wait()
        v = v_ref[...]
        skeleton = contract3(basis_ref[...], v, TN)
        row = lax.broadcasted_iota(jnp.int32, skeleton.shape, 0)
        skeleton = jnp.where(row < rank_ref[0], skeleton, 0.0)
        bottom_ref[: leaf_rows - part, :] = v[part:, :].astype(BF16)
        bottom_ref[leaf_rows - part :, :] = skeleton.astype(BF16)
        last.wait()
        upward_ref[...] = contract3(skeleton, transfer_ref[...], TN)
        bit = me_ref[0] & 1
        away_ref[...] = upward_ref[pl.ds(pl.multiple_of((1 - bit) * half, half), half), :].astype(BF16)
        kept_ref[...] = upward_ref[pl.ds(pl.multiple_of(bit * half, half), half), :]

    return pl.pallas_call(
        body,
        out_shape=(
            jax.ShapeDtypeStruct((part, probe_cols), BF16),
            jax.ShapeDtypeStruct((half, parent_cols), BF16),
            jax.ShapeDtypeStruct((half, parent_cols), F32),
        ),
        in_specs=[SMEM, SMEM, HBM, HBM, HBM],
        out_specs=(VMEM,) * 3,
        scratch_shapes=[
            pltpu.VMEM(v.shape, F32),
            pltpu.VMEM(basis.shape, F32),
            pltpu.VMEM(transfer.shape, F32),
            pltpu.VMEM((probe_cols, parent_cols), F32),
            pltpu.SemaphoreType.DMA((3,)),
        ],
        cost_estimate=cost(6 * v.size * rank_cols, 8 * v.size),
        compiler_params=ROOM,
        name="front",
    )(me, rank, v, basis, transfer)


def origin(me, j, n):
    place = jnp.where(me & 1 == 1, n - ((me + 1) >> 1), me >> 1)
    step = (j + 1) // 2
    place = place - step if j % 2 else place + step
    place = jnp.where(place < 0, place + n, jnp.where(place >= n, place - n, place))
    return jnp.where(place < n // 2, 2 * place, 2 * (n - place) - 1)


def named(me_ref, near_ref, count_ref, links_ref, j, n):
    leaf = origin(me_ref[0], j, n)
    slot = jnp.int32(-1)
    for k in range(near_ref.shape[1]):
        slot = jnp.where((near_ref[0, k] == leaf) & (k < count_ref[0]), k, slot)
    link = jnp.int32(-1)
    for k in range(links_ref.shape[1]):
        link = jnp.where(links_ref[0, k] == leaf, k, link)
    return slot >= 0, jnp.maximum(slot, 0), link >= 0, jnp.maximum(link, 0)


def take_all(tables, n, first, count, copies, blocks_ref, links_ref, parts, held, near_ref, coupled_ref):
    block_ref, link_ref, held_ref = held
    part = parts[0].shape[0]
    leaf_rows = near_ref.shape[0]

    def fetch(j):
        at = j % DEPTH
        live, slot, linked, link = named(*tables, first + j, n)
        got = [copies.start(parts[2 * j + c], held_ref.at[at, pl.ds(c * part, part)]) for c in (0, 1)]
        block = copies.start(blocks_ref.at[slot], block_ref.at[at], live)
        tie = copies.start(links_ref.at[link], link_ref.at[at], linked)
        return live, linked, got, block, tie

    fetched = [fetch(j) for j in range(min(count, DEPTH - 1))]
    yield
    for j in range(count):
        live, linked, got, block, tie = fetched[j]
        at = j % DEPTH
        for copy in got:
            copy.wait()
        pl.when(live)(block.wait)
        if j + DEPTH - 1 < count:
            fetched.append(fetch(j + DEPTH - 1))
        yield

        @pl.when(live)
        def _():
            near_ref[...] += contract(block_ref[at], held_ref[at, :leaf_rows, :], NN)

        @pl.when(linked)
        def _():
            tie.wait()
            coupled_ref[...] += contract2(link_ref[at], held_ref[at, leaf_rows:, :], NN)


def held_scratch(blocks, links, part):
    return [
        pltpu.VMEM((DEPTH,) + blocks.shape[1:], BF16),
        pltpu.VMEM((DEPTH,) + links.shape[1:], F32),
        pltpu.VMEM((DEPTH, 2 * part.shape[0], part.shape[1]), BF16),
    ]


def absorb(tables, n, first, blocks, links, messages, sums):
    probe_cols = messages[0][0].shape[1]
    count = len(messages)
    outs = (
        jax.ShapeDtypeStruct((blocks.shape[1], probe_cols), F32),
        jax.ShapeDtypeStruct((links.shape[1], probe_cols), F32),
    )
    operands = [p for message in messages for p in message] + list(sums)

    def body(*refs):
        tables_in, blocks_ref, links_ref, refs = refs[:4], refs[4], refs[5], refs[6:]
        near_out, coupled_out, *held, sems = refs[len(operands) :]
        copies = Copies(sems)
        base = [
            copies.start(given, out)
            for given, out in zip(refs[2 * count : len(operands)], (near_out, coupled_out))
        ]
        work = take_all(
            tables_in, n, first, count, copies, blocks_ref, links_ref, refs[: 2 * count], held,
            near_out, coupled_out,
        )
        next(work)
        if sums:
            for copy in base:
                copy.wait()
        else:
            near_out[...] = jnp.zeros_like(near_out)
            coupled_out[...] = jnp.zeros_like(coupled_out)
        for _ in work:
            pass

    return pl.pallas_call(
        body,
        out_shape=outs,
        in_specs=[SMEM] * 4 + [HBM] * 2 + [ANY] * len(operands),
        out_specs=(VMEM, VMEM),
        scratch_shapes=held_scratch(blocks, links, messages[0][0])
        + [pltpu.SemaphoreType.DMA((4 * count + 2,))],
        cost_estimate=cost(2 * count * (blocks.shape[1] ** 2) * probe_cols, 4 * count * (blocks.shape[1] ** 2)),
        compiler_params=ROOM,
        name="absorb",
    )(*tables, blocks, links, *operands)


def far_share(row, links, parents, blocks):
    count = len(parents)
    slots = blocks.shape[0]

    def body(row_ref, links_ref, *refs):
        blocks_in, out_ref, blocks_ref, parents_ref, sems = refs[count:]
        copies = Copies(sems)
        brought = [copies.start(refs[e], parents_ref.at[e]) for e in range(count)]
        fetched = [copies.start(blocks_in.at[k], blocks_ref.at[k]) for k in range(slots)]
        for copy in brought:
            copy.wait()
        total = jnp.zeros(out_ref.shape, F32)
        for k in range(slots):
            away = jnp.bitwise_xor(links_ref[0, k], row_ref[0])
            chosen = parents_ref[away]
            fetched[k].wait()
            high, low = halves(blocks_ref[k])
            total += contract(chosen, low, NT) + contract(chosen, high, NT)
        out_ref[...] = total.astype(BF16)

    return pl.pallas_call(
        body,
        out_shape=jax.ShapeDtypeStruct(parents[0].shape, BF16),
        in_specs=[SMEM, SMEM] + [ANY] * count + [HBM],
        out_specs=VMEM,
        scratch_shapes=[
            pltpu.VMEM(blocks.shape, F32),
            pltpu.VMEM((count,) + parents[0].shape, BF16),
            pltpu.SemaphoreType.DMA((count + slots,)),
        ],
        cost_estimate=cost(2**24, blocks.size * 4),
        compiler_params=ROOM,
        name="far",
    )(row, links, *parents, blocks)


def far_bits(far):
    total = sum(piece.shape[0] for piece in far) // far[0].shape[0]
    return total.bit_length() - 1


def reversed_bits(at, bits):
    return sum(((at >> b) & 1) << (bits - 1 - b) for b in range(bits))


def back(tables, n, first, rank, blocks, links, messages, near, coupled, far, transfer, basis, start):
    final = start is not None
    arrived = len(messages)
    parts = [p for message in messages for p in message]
    part = parts[0].shape[0]
    count = len(far)
    bits = far_bits(far)
    operands = parts + [near, coupled, transfer, basis] + list(far) + ([start] if final else [])

    def body(*refs):
        tables_in, rank_ref, blocks_ref, links_ref, refs = refs[:4], refs[4], refs[5], refs[6], refs[7:]
        near_in, coupled_in, transfer_in, basis_in = refs[2 * arrived : 2 * arrived + 4]
        far_refs = refs[2 * arrived + 4 : 2 * arrived + 4 + count]
        out_ref, *rest = refs[len(operands) :]
        if final:
            past_ref = rest.pop(-2)
        else:
            top_ref = rest.pop(0)
        *held, transfer_ref, basis_ref, spread_ref, combined_ref, sems = rest
        copies = Copies(sems)
        base = [copies.start(near_in, out_ref), copies.start(coupled_in, combined_ref)]
        work = take_all(
            tables_in, n, first, arrived, copies, blocks_ref, links_ref, refs[: 2 * arrived], held,
            out_ref, combined_ref,
        )
        next(work)
        rows = far_refs[0].shape[0]
        late = []
        at = 0
        for ref in far_refs:
            for piece in range(ref.shape[0] // rows):
                share = share_of(jnp.bitwise_xor(tables_in[0][0], reversed_bits(at, bits)), bits)
                late.append(
                    copies.start(
                        ref.at[pl.ds(piece * rows, rows)],
                        spread_ref.at[pl.ds(pl.multiple_of(share * rows, rows), rows)],
                    )
                )
                at += 1
        late.append(copies.start(transfer_in, transfer_ref))
        late.append(copies.start(basis_in, basis_ref))
        if final:
            late.append(copies.start(refs[len(operands) - 1], past_ref))
        for copy in base:
            copy.wait()
        for _ in work:
            pass

        for copy in late:
            copy.wait()
        combined_ref[...] += contract2(transfer_ref[...], spread_ref[...], NT)
        row = lax.broadcasted_iota(jnp.int32, combined_ref.shape, 0)
        combined = jnp.where(row < rank_ref[0], combined_ref[...], 0.0)
        value = out_ref[...] + contract3(basis_ref[...], combined, NN)
        if final:
            out_ref[...] = 2.0 * value - past_ref[...]
        else:
            out_ref[...] = value
            top_ref[...] = value[:part, :].astype(BF16)

    out = jax.ShapeDtypeStruct(near.shape, F32)
    outs = (out,) if final else (out, jax.ShapeDtypeStruct(parts[0].shape, BF16))
    return pl.pallas_call(
        body,
        out_shape=outs,
        in_specs=[SMEM] * 5
        + [HBM] * 2
        + [ANY] * (2 * arrived + 2)
        + [HBM] * 2
        + [ANY] * count
        + ([HBM] if final else []),
        out_specs=(VMEM,) * len(outs),
        scratch_shapes=held_scratch(blocks, links, parts[0])
        + [
            pltpu.VMEM(transfer.shape, F32),
            pltpu.VMEM(basis.shape, F32),
            pltpu.VMEM((near.shape[1], transfer.shape[1]), BF16),
            pltpu.VMEM(coupled.shape, F32),
        ]
        + ([pltpu.VMEM(near.shape, F32)] if final else [])
        + [pltpu.SemaphoreType.DMA((4 * arrived + 5 + (1 << bits),))],
        cost_estimate=cost(6 * (blocks.shape[1] ** 2) * near.shape[1], 6 * (blocks.shape[1] ** 2)),
        compiler_params=ROOM,
        name="back",
    )(*tables, rank, blocks, links, *operands)


def local(
    probes,
    near_blocks,
    near_leaves,
    near_count,
    leaf_rank,
    leaf_basis,
    leaf_transfer,
    leaf_links,
    leaf_link_blocks,
    parent_links,
    parent_link_blocks,
):
    n = lax.axis_size("col")
    span_row = lax.axis_size("row")
    me = lax.axis_index("col")
    my_row = lax.axis_index("row")
    leaf_rows, _ = probes.shape
    keep = lambda a: pltpu.with_memory_space_constraint(a, pltpu.HBM)
    transfer = keep(leaf_transfer[0])
    blocks = keep(near_blocks[0])
    link_blocks = keep(leaf_link_blocks[0])
    parent_blocks = keep(parent_link_blocks[0])
    leaf_basis = keep(leaf_basis)
    past = keep(probes)
    bits = n.bit_length() - 1
    assert 1 << bits == n

    order = ring_order(n)
    to_right = [(order[i], order[(i + 1) % n]) for i in range(n)]
    to_left = [(b, a) for a, b in to_right]
    steps = n // 2 - 1

    mine = jnp.reshape(me, (1,))
    tables = (mine, near_leaves, near_count, leaf_links)

    def swap(value, axis, size, distance):
        return lax.ppermute(value, axis, [(i, i ^ distance) for i in range(size)])

    def pass_on(value, perm):
        return lax.ppermute(value, "col", perm)

    def multiply(vector, top, start):
        bottom, away, kept = front(mine, keep(vector), leaf_basis, transfer, leaf_rank)

        for b in range(bits):
            if b:
                pair = total.reshape(2, total.shape[0] // 2, total.shape[1])
                bit = (me >> b) & 1
                away = lax.dynamic_index_in_dim(pair, 1 - bit, 0, False).astype(BF16)
                kept = lax.dynamic_index_in_dim(pair, bit, 0, False)
            came = swap(away, "col", n, 1 << b)
            total = kept + came.astype(F32)
        share = total.astype(BF16)
        parents = [share] + [swap(share, "row", span_row, e) for e in range(1, span_row)]
        far = [far_share(jnp.reshape(my_row, (1,)), parent_links, parents, parent_blocks)]
        for b in reversed(range(bits)):
            held = far[0] if len(far) == 1 else jnp.concatenate(far)
            far.append(swap(held, "col", n, 1 << b))

        messages = [(top, bottom)]
        right = left = (top, bottom)
        for _ in range(1, steps + 1):
            right = tuple(pass_on(right[c], to_right) for c in (0, 1))
            left = tuple(pass_on(left[c], to_left) for c in (0, 1))
            messages += [right, left]
        opposite = (pass_on(right[0], to_right), pass_on(left[1], to_left))
        sums = absorb(tables, n, 0, blocks, link_blocks, [(top, keep(bottom))], ())
        first = 1
        for s in range(1, steps + 1):
            taken = messages[first : 2 * s + 1]
            sums = absorb(tables, n, first, blocks, link_blocks, taken, sums)
            first = 2 * s + 1
        return back(
            tables, n, first, leaf_rank, blocks, link_blocks, messages[first:] + [opposite],
            *sums, far, transfer, leaf_basis, start,
        )

    part = (leaf_rows + leaf_basis.shape[1]) // 2
    term_one, top = multiply(probes, probes[:part].astype(BF16), None)
    (term_two,) = multiply(term_one, top, past)
    return (term_one, term_two)


def solution(mesh):
    in_specs = (
        P(("row", "col"), None),
        P(("row", "col"), None, None, None),
        P(("row", "col"), None),
        P(("row", "col")),
        P(("row", "col")),
        P(("row", "col"), None),
        P(("row", "col"), None, None),
        P(("row", "col"), None),
        P(("row", "col"), None, None, None),
        P("row", None),
        P("row", None, None, None),
    )
    out_specs = (P(("row", "col"), None), P(("row", "col"), None))
    return jax.shard_map(local, mesh=mesh, in_specs=in_specs, out_specs=out_specs, check_vma=False)
```

time: 169 us -> 159 us (0.941)
  Pallas kernels: 61.9 us -> 54.8 us
  starting transfers between devices: 42 us -> 46.8 us
  other arithmetic: 3.59 us -> 0.14 us
  waiting for transfers between devices: 51.3 us -> 48.9 us
    pallas_call x12 -> x14, Pallas kernels: 61.9 us -> 54.8 us  [the longest x8 31.8 us: absorb(): pl.pallas_call(body, out_shape=outs, in_specs=[SMEM] * 4 + [HBM] * 2 + [A...]
    ppermute x18, starting transfers between devices: 11.4 us -> 16.1 us  [swap(): return lax.ppermute(value, axis, [(i, i ^ distance) for i in range(size)])]
    ppermute x18, waiting for transfers between devices: 26.1 us -> 22.7 us  [swap(): return lax.ppermute(value, axis, [(i, i ^ distance) for i in range(size)])]
    add x4, other arithmetic: 1.99 us -> 0.09 us  [multiply(): total = kept + came.astype(F32)]
  transfers between devices with their start and end apart: 46 -> 46, of which waited for: 19 -> 19; matrix products, arithmetic and copies ran while one was open for 3% -> 1% of each run, Pallas kernels for 25% -> 24%
where the time goes in v2:
time: 159 us; the launch traced here: 156 us
  Pallas kernels  54.8 us (34%)
  waiting for transfers between devices  48.9 us (31%)
  starting transfers between devices  46.8 us (29%)
  local copies, waits for them, and re-layouts  3.18 us (2%)
  between operations  2.5 us (2%)
    pallas_call x8, Pallas kernels, absorb(): pl.pallas_call(body, out_shape=outs, in_specs=[SMEM] * 4 + [HBM] * 2 + [A...  31.8 us
    ppermute x28, starting transfers between devices, pass_on(): return lax.ppermute(value, 'col', perm)  30.7 us
    ppermute x28, waiting for transfers between devices, pass_on(): return lax.ppermute(value, 'col', perm)  26.2 us
    ppermute x18, waiting for transfers between devices, swap(): return lax.ppermute(value, axis, [(i, i ^ distance) for i in range(size)])  22.7 us
    ppermute x18, starting transfers between devices, swap(): return lax.ppermute(value, axis, [(i, i ^ distance) for i in range(size)])  16.1 us
    pallas_call x2, Pallas kernels, back(): pl.pallas_call(body, out_shape=outs, in_specs=[SMEM] * 5 + [HBM] * 2 + [A...  11.6 us
    pallas_call x2, Pallas kernels, front(): pl.pallas_call(body, out_shape=(jax.ShapeDtypeStruct((part, probe_cols),...  6 us
    pallas_call x2, Pallas kernels, far_share(): pl.pallas_call(body, out_shape=jax.ShapeDtypeStruct(parents[0].shape, BF1...  5.47 us
  transfers between devices with their start and end apart: 46, of which 19 were waited for; matrix products, arithmetic and copies ran while one was open for 1% of the time, Pallas kernels for 24%

profile of v2, /device:TPU:16, one launch (start us, length us, event | category | flops | bytes accessed | tf_op | source)
XLA Modules:
  0.0 156.3 jit_solution(9246569449706123752)
XLA Ops:
  1.3 3.0 %front.2 = (bf16[640,256]{1,0:T(8,128)(2,1)S(1)}, bf16[128,512]{1,0:T(8,128)(2,1)S(1)}, f32[128,512]{1,0:T(8,128)S(1)}) custom-call(s32[1]{0:T(128)} %bitcast.me_ref.refs_0_, s32[1]{0:T(128)S(6)} %copy.14.rank_ref.refs_4_, f32[1024,256]{1,0:T(8,128)} %refs_17_.1, f32[1024,256]{1,0:T(8,128)} %refs_12_.3, f32[256,512]{1,0:T(8,128)} %bitcast.50), custom_call_target="tpu_custom_call" | custom-call | flops 402653184 | bytes 2097152 | tf_op jit(solution)/shard_map/front/pallas_call | solution.py:102
  4.3 1.6 collective-permute-start.14
  7.4 1.6 %collective-permute-start = (bf16[640,256]{1,0:T(8,128)(2,1)S(1)}, bf16[640,256]{1,0:T(8,128)(2,1)S(1)}, u32[]{:S(2)}, u32[]{:S(2)}) collective-permute-start(bf16[640,256]{1,0:T(8,128)(2,1)S(1)} %slice.7.refs_6_), channel_id=1, source_target_pairs={{0,2},{2,4},{4,6},{6,7},{7,5},{5,3},{3,1},{1,0},{8,10},{10,12},{12... | collective-permute-start | bytes 983048 | tf_op jit(solution)/shard_map/ppermute | solution.py:402
  9.7 2.8 %collective-permute-start.15 = (bf16[64,512]{1,0:T(8,128)(2,1)S(1)}, bf16[64,512]{1,0:T(8,128)(2,1)S(1)}, u32[]{:S(2)}, u32[]{:S(2)}) collective-permute-start(bf16[64,512]{1,0:T(8,128)(2,1)S(1)} %fusion), channel_id=1, source_target_pairs={{0,2},{1,3},{2,0},{3,1},{4,6},{5,7},{6,4},{7,5},{8,10},{9,11},{10,... | collective-permute-start | bytes 196616 | tf_op jit(solution)/shard_map/ppermute | solution.py:399
  12.5 2.0 %collective-permute-start.11 = (bf16[640,256]{1,0:T(8,128)(2,1)S(1)}, bf16[640,256]{1,0:T(8,128)(2,1)S(1)}, u32[]{:S(2)}, u32[]{:S(2)}) collective-permute-start(bf16[640,256]{1,0:T(8,128)(2,1)S(1)} %slice.7.refs_6_), channel_id=1, source_target_pairs={{2,0},{4,2},{6,4},{7,6},{5,7},{3,5},{1,3},{0,1},{10,8},{12,10},{14... | collective-permute-start | bytes 983048 | tf_op jit(solution)/shard_map/ppermute | solution.py:402
  14.5 2.0 %collective-permute-done.4.refs_9_ = bf16[640,256]{1,0:T(8,128)(2,1)S(1)} collective-permute-done((bf16[640,256]{1,0:T(8,128)(2,1)S(1)}, bf16[640,256]{1,0:T(8,128)(2,1)S(1)}, u32[]{:S(2)}, u32[]{:S(2)}) %collective-permute-start.4) | collective-permute-done | bytes 327712 | tf_op jit(solution)/shard_map/ppermute | solution.py:402
  16.6 1.5 collective-permute-done.refs_6_
  18.1 1.6 %collective-permute-start.1 = (bf16[640,256]{1,0:T(8,128)(2,1)S(1)}, bf16[640,256]{1,0:T(8,128)(2,1)S(1)}, u32[]{:S(2)}, u32[]{:S(2)}) collective-permute-start(bf16[640,256]{1,0:T(8,128)(2,1)S(1)} %collective-permute-done.refs_6_), channel_id=1, source_target_pairs={{0,2},{2,4},{4,6},{6,7},{7,5},{5,3},{3,1},{1,0},{8,10},{10,12},{12... | collective-permute-start | bytes 983048 | tf_op jit(solution)/shard_map/ppermute | solution.py:402
  20.1 5.5 %collective-permute-done.8.refs_7_ = bf16[640,256]{1,0:T(8,128)(2,1)S(1)} collective-permute-done((bf16[640,256]{1,0:T(8,128)(2,1)S(1)}, bf16[640,256]{1,0:T(8,128)(2,1)S(1)}, u32[]{:S(2)}, u32[]{:S(2)}) %collective-permute-start.8) | collective-permute-done | bytes 327712 | tf_op jit(solution)/shard_map/ppermute | solution.py:402
  25.6 2.5 %collective-permute-start.9 = (bf16[640,256]{1,0:T(8,128)(2,1)S(1)}, bf16[640,256]{1,0:T(8,128)(2,1)}, u32[]{:S(2)}, u32[]{:S(2)}) collective-permute-start(bf16[640,256]{1,0:T(8,128)(2,1)S(1)} %collective-permute-done.8.refs_7_), channel_id=1, source_target_pairs={{0,2},{2,4},{4,6},{6,7},{7,5},{5,3},{3,1},{1,0},{8,10},{10,12},{12... | collective-permute-start | bytes 983048 | tf_op jit(solution)/shard_map/ppermute | solution.py:402
  28.1 3.8 %collective-permute-done.5.refs_9_ = bf16[640,256]{1,0:T(8,128)(2,1)S(1)} collective-permute-done((bf16[640,256]{1,0:T(8,128)(2,1)S(1)}, bf16[640,256]{1,0:T(8,128)(2,1)S(1)}, u32[]{:S(2)}, u32[]{:S(2)}) %collective-permute-start.5) | collective-permute-done | bytes 327712 | tf_op jit(solution)/shard_map/ppermute | solution.py:402
  33.3 2.5 %collective-permute-start.2 = (bf16[640,256]{1,0:T(8,128)(2,1)S(1)}, bf16[640,256]{1,0:T(8,128)(2,1)S(1)}, u32[]{:S(2)}, u32[]{:S(2)}) collective-permute-start(bf16[640,256]{1,0:T(8,128)(2,1)S(1)} %collective-permute-done.1.refs_6_), channel_id=1, source_target_pairs={{0,2},{2,4},{4,6},{6,7},{7,5},{5,3},{3,1},{1,0},{8,10},{10,12},{12... | collective-permute-start | bytes 983048 | tf_op jit(solution)/shard_map/ppermute | solution.py:402
  35.9 1.2 collective-permute-done.17.refs_1_
  37.1 1.5 collective-permute-start.18
  38.6 2.4 %collective-permute-done.18.refs_2_ = bf16[32,512]{1,0:T(8,128)(2,1)S(1)} collective-permute-done((bf16[32,512]{1,0:T(8,128)(2,1)S(1)}, bf16[32,512]{1,0:T(8,128)(2,1)S(1)}, u32[]{:S(2)}, u32[]{:S(2)}) %collective-permute-start.18) | collective-permute-done | bytes 32800 | tf_op jit(solution)/shard_map/ppermute | solution.py:399
  42.2 2.4 %collective-permute-done.19.refs_3_ = bf16[32,512]{1,0:T(8,128)(2,1)S(1)} collective-permute-done((bf16[32,512]{1,0:T(8,128)(2,1)S(1)}, bf16[32,512]{1,0:T(8,128)(2,1)S(1)}, u32[]{:S(2)}, u32[]{:S(2)}) %collective-permute-start.19) | collective-permute-done | bytes 32800 | tf_op jit(solution)/shard_map/ppermute | solution.py:399
  45.3 2.7 %far.2.refs_13_ = bf16[32,512]{1,0:T(8,128)(2,1)S(1)} custom-call(s32[1]{0:T(128)} %bitcast.4.row_ref, s32[1,2]{1,0:T(1,128)S(1)} %copy-done.5, bf16[32,512]{1,0:T(8,128)(2,1)S(1)} %fusion.3.refs_0_, bf16[32,512]{1,0:T(8,128)(2,1)S(1)} %collective-permute-done.17.refs_1_, bf16[32,512]{1,0:T(8,128)(2,1)S(1)} %collective-permute-done.18.refs_2_, ...), custom_call_target="tpu_custom_call" | custom-call | flops 16777216 | bytes 2097152 | tf_op jit(solution)/shard_map/far/pallas_call | solution.py:250
  49.4 3.2 %absorb.8 = (f32[1024,256]{1,0:T(8,128)S(1)}, f32[256,256]{1,0:T(8,128)S(1)}) custom-call(s32[1]{0:T(128)} %bitcast.me_ref.refs_0_, s32[1,8]{1,0:T(1,128)S(1)} %copy-done.2, s32[1]{0:T(128)S(6)} %copy.13.refs_2_, s32[1,4]{1,0:T(1,128)S(1)} %copy-done.4, bf16[8,1024,1024]{2,1,0:T(8,128)(2,1)} %bitcast.30, f32[4,256,256]{2,1,0:T(8,128)} %bitcast.40, ...), custom_call_target="tpu_custom_call" | custom-call | flops 536870912 | bytes 4194304 | tf_op jit(solution)/shard_map/absorb/pallas_call | solution.py:217
  55.7 2.5 %collective-permute-start.7 = (bf16[640,256]{1,0:T(8,128)(2,1)S(1)}, bf16[640,256]{1,0:T(8,128)(2,1)S(1)}, u32[]{:S(2)}, u32[]{:S(2)}) collective-permute-start(bf16[640,256]{1,0:T(8,128)(2,1)S(1)} %collective-permute-done.6.refs_9_), channel_id=1, source_target_pairs={{2,0},{4,2},{6,4},{7,6},{5,7},{3,5},{1,3},{0,1},{10,8},{12,10},{14... | collective-permute-start | bytes 983048 | tf_op jit(solution)/shard_map/ppermute | solution.py:402
  58.2 4.5 %absorb.9 = (f32[1024,256]{1,0:T(8,128)S(1)}, f32[256,256]{1,0:T(8,128)S(1)}) custom-call(s32[1]{0:T(128)} %bitcast.me_ref.refs_0_, s32[1,8]{1,0:T(1,128)S(1)} %copy-done.2, s32[1]{0:T(128)S(6)} %copy.13.refs_2_, s32[1,4]{1,0:T(1,128)S(1)} %copy-done.4, bf16[8,1024,1024]{2,1,0:T(8,128)(2,1)} %bitcast.31, f32[4,256,256]{2,1,0:T(8,128)} %bitcast.41, ...), custom_call_target="tpu_custom_call" | custom-call | flops 1073741824 | bytes 8388608 | tf_op jit(solution)/shard_map/absorb/pallas_call | solution.py:217
  62.7 3.1 %collective-permute-done.21.refs_15_ = bf16[64,512]{1,0:T(8,128)(2,1)S(1)} collective-permute-done((bf16[64,512]{1,0:T(8,128)(2,1)S(1)}, bf16[64,512]{1,0:T(8,128)(2,1)S(1)}, u32[]{:S(2)}, u32[]{:S(2)}) %collective-permute-start.21) | collective-permute-done | bytes 65568 | tf_op jit(solution)/shard_map/ppermute | solution.py:399
  65.9 4.3 %absorb.10 = (f32[1024,256]{1,0:T(8,128)S(1)}, f32[256,256]{1,0:T(8,128)S(1)}) custom-call(s32[1]{0:T(128)} %bitcast.me_ref.refs_0_, s32[1,8]{1,0:T(1,128)S(1)} %copy-done.2, s32[1]{0:T(128)S(6)} %copy.13.refs_2_, s32[1,4]{1,0:T(1,128)S(1)} %copy-done.4, bf16[8,1024,1024]{2,1,0:T(8,128)(2,1)} %bitcast.32, f32[4,256,256]{2,1,0:T(8,128)} %bitcast.42, ...), custom_call_target="tpu_custom_call" | custom-call | flops 1073741824 | bytes 8388608 | tf_op jit(solution)/shard_map/absorb/pallas_call | solution.py:217
  70.2 4.0 %absorb.11 = (f32[1024,256]{1,0:T(8,128)S(1)}, f32[256,256]{1,0:T(8,128)S(1)}) custom-call(s32[1]{0:T(128)} %bitcast.me_ref.refs_0_, s32[1,8]{1,0:T(1,128)S(1)} %copy-done.2, s32[1]{0:T(128)S(6)} %copy.13.refs_2_, s32[1,4]{1,0:T(1,128)S(1)} %copy-done.4, bf16[8,1024,1024]{2,1,0:T(8,128)(2,1)} %bitcast.33, f32[4,256,256]{2,1,0:T(8,128)} %bitcast.43, ...), custom_call_target="tpu_custom_call" | custom-call | flops 1073741824 | bytes 8388608 | tf_op jit(solution)/shard_map/absorb/pallas_call | solution.py:217
  74.3 5.9 %back.2 = (f32[1024,256]{1,0:T(8,128)}, bf16[640,256]{1,0:T(8,128)(2,1)S(1)}) custom-call(s32[1]{0:T(128)} %bitcast.me_ref.refs_0_, s32[1,8]{1,0:T(1,128)S(1)} %copy-done.2, s32[1]{0:T(128)S(6)} %copy.13.refs_2_, s32[1,4]{1,0:T(1,128)S(1)} %copy-done.4, s32[1]{0:T(128)S(6)} %copy.14.rank_ref.refs_4_, bf16[8,1024,1024]{2,1,0:T(8,128)(2,1)} %bitcast.34, ...), custom_call_target="tpu_custom_call" | custom-call | flops 1610612736 | bytes 6291456 | tf_op jit(solution)/shard_map/back/pallas_call | solution.py:337
  80.2 3.0 %front.3 = (bf16[640,256]{1,0:T(8,128)(2,1)S(1)}, bf16[128,512]{1,0:T(8,128)(2,1)S(1)}, f32[128,512]{1,0:T(8,128)S(1)}) custom-call(s32[1]{0:T(128)} %bitcast.me_ref.refs_0_, s32[1]{0:T(128)S(6)} %copy.14.rank_ref.refs_4_, f32[1024,256]{1,0:T(8,128)} %get-tuple-element.24.v_in, f32[1024,256]{1,0:T(8,128)} %refs_12_.3, f32[256,512]{1,0:T(8,128)} %bitcast.52), custom_call_target="tpu_custom_call" | custom-call | flops 402653184 | bytes 2097152 | tf_op jit(solution)/shard_map/front/pallas_call | solution.py:102
  85.0 1.4 collective-permute-start.23
  86.4 1.9 %collective-permute-done.37 = bf16[128,512]{1,0:T(8,128)(2,1)S(1)} collective-permute-done((bf16[128,512]{1,0:T(8,128)(2,1)S(1)}, bf16[128,512]{1,0:T(8,128)(2,1)S(1)}, u32[]{:S(2)}, u32[]{:S(2)}) %collective-permute-start.37) | collective-permute-done | bytes 131104 | tf_op jit(solution)/shard_map/ppermute | solution.py:399
  88.3 1.2 collective-permute-start.38
  91.5 3.4 %collective-permute-done.27.refs_9_ = bf16[640,256]{1,0:T(8,128)(2,1)S(1)} collective-permute-done((bf16[640,256]{1,0:T(8,128)(2,1)S(1)}, bf16[640,256]{1,0:T(8,128)(2,1)S(1)}, u32[]{:S(2)}, u32[]{:S(2)}) %collective-permute-start.27) | collective-permute-done | bytes 327712 | tf_op jit(solution)/shard_map/ppermute | solution.py:402
  95.6 1.4 collective-permute-start.24
  97.0 2.4 %collective-permute-start.39 = (bf16[32,512]{1,0:T(8,128)(2,1)S(1)}, bf16[32,512]{1,0:T(8,128)(2,1)S(1)}, u32[]{:S(2)}, u32[]{:S(2)}) collective-permute-start(bf16[32,512]{1,0:T(8,128)(2,1)S(1)} %fusion.5), channel_id=1, source_target_pairs={{0,4},{1,5},{2,6},{3,7},{4,0},{5,1},{6,2},{7,3},{8,12},{9,13},{10,... | collective-permute-start | bytes 98312 | tf_op jit(solution)/shard_map/ppermute | solution.py:399
  99.4 3.5 %collective-permute-done.31.refs_7_ = bf16[640,256]{1,0:T(8,128)(2,1)S(1)} collective-permute-done((bf16[640,256]{1,0:T(8,128)(2,1)S(1)}, bf16[640,256]{1,0:T(8,128)(2,1)S(1)}, u32[]{:S(2)}, u32[]{:S(2)}) %collective-permute-start.31) | collective-permute-done | bytes 327712 | tf_op jit(solution)/shard_map/ppermute | solution.py:402
  102.9 2.5 %collective-permute-start.32 = (bf16[640,256]{1,0:T(8,128)(2,1)S(1)}, bf16[640,256]{1,0:T(8,128)(2,1)S(1)}, u32[]{:S(2)}, u32[]{:S(2)}) collective-permute-start(bf16[640,256]{1,0:T(8,128)(2,1)S(1)} %collective-permute-done.31.refs_7_), channel_id=1, source_target_pairs={{0,2},{2,4},{4,6},{6,7},{7,5},{5,3},{3,1},{1,0},{8,10},{10,12},{12... | collective-permute-start | bytes 983048 | tf_op jit(solution)/shard_map/ppermute | solution.py:402
  105.4 4.9 %collective-permute-done.28.refs_9_ = bf16[640,256]{1,0:T(8,128)(2,1)S(1)} collective-permute-done((bf16[640,256]{1,0:T(8,128)(2,1)S(1)}, bf16[640,256]{1,0:T(8,128)(2,1)S(1)}, u32[]{:S(2)}, u32[]{:S(2)}) %collective-permute-start.28) | collective-permute-done | bytes 327712 | tf_op jit(solution)/shard_map/ppermute | solution.py:402
  110.7 2.4 %collective-permute-start.25 = (bf16[640,256]{1,0:T(8,128)(2,1)S(1)}, bf16[640,256]{1,0:T(8,128)(2,1)S(1)}, u32[]{:S(2)}, u32[]{:S(2)}) collective-permute-start(bf16[640,256]{1,0:T(8,128)(2,1)S(1)} %collective-permute-done.24.refs_6_), channel_id=1, source_target_pairs={{0,2},{2,4},{4,6},{6,7},{7,5},{5,3},{3,1},{1,0},{8,10},{10,12},{12... | collective-permute-start | bytes 983048 | tf_op jit(solution)/shard_map/ppermute | solution.py:402
  113.2 1.2 collective-permute-done.40.refs_1_
  115.1 3.2 %collective-permute-done.41.refs_2_ = bf16[32,512]{1,0:T(8,128)(2,1)S(1)} collective-permute-done((bf16[32,512]{1,0:T(8,128)(2,1)S(1)}, bf16[32,512]{1,0:T(8,128)(2,1)S(1)}, u32[]{:S(2)}, u32[]{:S(2)}) %collective-permute-start.41) | collective-permute-done | bytes 32800 | tf_op jit(solution)/shard_map/ppermute | solution.py:399
  118.3 3.3 %collective-permute-done.42.refs_3_ = bf16[32,512]{1,0:T(8,128)(2,1)S(1)} collective-permute-done((bf16[32,512]{1,0:T(8,128)(2,1)S(1)}, bf16[32,512]{1,0:T(8,128)(2,1)S(1)}, u32[]{:S(2)}, u32[]{:S(2)}) %collective-permute-start.42) | collective-permute-done | bytes 32800 | tf_op jit(solution)/shard_map/ppermute | solution.py:399
  121.6 2.7 %far.3.refs_13_ = bf16[32,512]{1,0:T(8,128)(2,1)S(1)} custom-call(s32[1]{0:T(128)} %bitcast.4.row_ref, s32[1,2]{1,0:T(1,128)S(1)} %copy-done.6, bf16[32,512]{1,0:T(8,128)(2,1)S(1)} %fusion.2.refs_0_, bf16[32,512]{1,0:T(8,128)(2,1)S(1)} %collective-permute-done.40.refs_1_, bf16[32,512]{1,0:T(8,128)(2,1)S(1)} %collective-permute-done.41.refs_2_, ...), custom_call_target="tpu_custom_call" | custom-call | flops 16777216 | bytes 2097152 | tf_op jit(solution)/shard_map/far/pallas_call | solution.py:250
  124.4 1.6 %collective-permute-start.43 = (bf16[32,512]{1,0:T(8,128)(2,1)S(1)}, bf16[32,512]{1,0:T(8,128)(2,1)S(1)}, u32[]{:S(2)}, u32[]{:S(2)}) collective-permute-start(bf16[32,512]{1,0:T(8,128)(2,1)S(1)} %far.3.refs_13_), channel_id=1, source_target_pairs={{0,4},{1,5},{2,6},{3,7},{4,0},{5,1},{6,2},{7,3},{8,12},{9,13},{10,... | collective-permute-start | bytes 98312 | tf_op jit(solution)/shard_map/ppermute | solution.py:399
  126.0 3.2 %absorb.12 = (f32[1024,256]{1,0:T(8,128)S(1)}, f32[256,256]{1,0:T(8,128)S(1)}) custom-call(s32[1]{0:T(128)} %bitcast.me_ref.refs_0_, s32[1,8]{1,0:T(1,128)S(1)} %copy-done.3, s32[1]{0:T(128)S(6)} %copy.13.refs_2_, s32[1,4]{1,0:T(1,128)S(1)} %copy-done.4, bf16[8,1024,1024]{2,1,0:T(8,128)(2,1)} %bitcast.35, f32[4,256,256]{2,1,0:T(8,128)} %bitcast.45, ...), custom_call_target="tpu_custom_call" | custom-call | flops 536870912 | bytes 4194304 | tf_op jit(solution)/shard_map/absorb/pallas_call | solution.py:217
  129.2 2.0 %collective-permute-start.36 = (bf16[640,256]{1,0:T(8,128)(2,1)S(1)}, bf16[640,256]{1,0:T(8,128)(2,1)S(1)}, u32[]{:S(2)}, u32[]{:S(2)}) collective-permute-start(bf16[640,256]{1,0:T(8,128)(2,1)S(1)} %collective-permute-done.35.refs_8_), channel_id=1, source_target_pairs={{2,0},{4,2},{6,4},{7,6},{5,7},{3,5},{1,3},{0,1},{10,8},{12,10},{14... | collective-permute-start | bytes 983048 | tf_op jit(solution)/shard_map/ppermute | solution.py:402
  132.1 1.2 collective-permute-start.30
  134.1 4.5 %absorb.13 = (f32[1024,256]{1,0:T(8,128)S(1)}, f32[256,256]{1,0:T(8,128)S(1)}) custom-call(s32[1]{0:T(128)} %bitcast.me_ref.refs_0_, s32[1,8]{1,0:T(1,128)S(1)} %copy-done.3, s32[1]{0:T(128)S(6)} %copy.13.refs_2_, s32[1,4]{1,0:T(1,128)S(1)} %copy-done.4, bf16[8,1024,1024]{2,1,0:T(8,128)(2,1)} %bitcast.36, f32[4,256,256]{2,1,0:T(8,128)} %bitcast.46, ...), custom_call_target="tpu_custom_call" | custom-call | flops 1073741824 | bytes 8388608 | tf_op jit(solution)/shard_map/absorb/pallas_call | solution.py:217
  138.6 3.4 %collective-permute-done.44.refs_15_ = bf16[64,512]{1,0:T(8,128)(2,1)S(1)} collective-permute-done((bf16[64,512]{1,0:T(8,128)(2,1)S(1)}, bf16[64,512]{1,0:T(8,128)(2,1)S(1)}, u32[]{:S(2)}, u32[]{:S(2)}) %collective-permute-start.44) | collective-permute-done | bytes 65568 | tf_op jit(solution)/shard_map/ppermute | solution.py:399
  142.1 4.2 %absorb.14 = (f32[1024,256]{1,0:T(8,128)S(1)}, f32[256,256]{1,0:T(8,128)S(1)}) custom-call(s32[1]{0:T(128)} %bitcast.me_ref.refs_0_, s32[1,8]{1,0:T(1,128)S(1)} %copy-done.3, s32[1]{0:T(128)S(6)} %copy.13.refs_2_, s32[1,4]{1,0:T(1,128)S(1)} %copy-done.4, bf16[8,1024,1024]{2,1,0:T(8,128)(2,1)} %bitcast.37, f32[4,256,256]{2,1,0:T(8,128)} %bitcast.47, ...), custom_call_target="tpu_custom_call" | custom-call | flops 1073741824 | bytes 8388608 | tf_op jit(solution)/shard_map/absorb/pallas_call | solution.py:217
  146.3 4.0 %absorb.15 = (f32[1024,256]{1,0:T(8,128)S(1)}, f32[256,256]{1,0:T(8,128)S(1)}) custom-call(s32[1]{0:T(128)} %bitcast.me_ref.refs_0_, s32[1,8]{1,0:T(1,128)S(1)} %copy-done.3, s32[1]{0:T(128)S(6)} %copy.13.refs_2_, s32[1,4]{1,0:T(1,128)S(1)} %copy-done.4, bf16[8,1024,1024]{2,1,0:T(8,128)(2,1)} %bitcast.38, f32[4,256,256]{2,1,0:T(8,128)} %bitcast.48, ...), custom_call_target="tpu_custom_call" | custom-call | flops 1073741824 | bytes 8388608 | tf_op jit(solution)/shard_map/absorb/pallas_call | solution.py:217
  150.4 5.7 %back.3 = f32[1024,256]{1,0:T(8,128)} custom-call(s32[1]{0:T(128)} %bitcast.me_ref.refs_0_, s32[1,8]{1,0:T(1,128)S(1)} %copy-done.3, s32[1]{0:T(128)S(6)} %copy.13.refs_2_, s32[1,4]{1,0:T(1,128)S(1)} %copy-done.4, s32[1]{0:T(128)S(6)} %copy.14.rank_ref.refs_4_, bf16[8,1024,1024]{2,1,0:T(8,128)(2,1)} %bitcast.39, f32[4,256,256]{2,1,0:T(8,128)} %bitcast.49, ...), custom_call_target="tpu_custom_call" | custom-call | flops 1610612736 | bytes 6291456 | tf_op jit(solution)/shard_map/back/pallas_call | solution.py:337
  (87 shorter events, 17.8 us)
Async XLA Ops:
  4.3 5.3 %collective-permute-start.14 = (bf16[128,512]{1,0:T(8,128)(2,1)S(1)}, bf16[128,512]{1,0:T(8,128)(2,1)S(1)}, u32[]{:S(2)}, u32[]{:S(2)}) collective-permute-start(bf16[128,512]{1,0:T(8,128)(2,1)S(1)} %get-tuple-element.36), channel_id=1, source_target_pairs={{0,1},{1,0},{2,3},{3,2},{4,5},{5,4},{6,7},{7,6},{8,9},{9,8},{10,11... | collective-permute-start | bytes 393224 | tf_op jit(solution)/shard_map/ppermute | solution.py:399
  5.9 10.6 %collective-permute-start.4 = (bf16[640,256]{1,0:T(8,128)(2,1)S(1)}, bf16[640,256]{1,0:T(8,128)(2,1)S(1)}, u32[]{:S(2)}, u32[]{:S(2)}) collective-permute-start(bf16[640,256]{1,0:T(8,128)(2,1)S(1)} %get-tuple-element.26.refs_7_), channel_id=1, source_target_pairs={{2,0},{4,2},{6,4},{7,6},{5,7},{3,5},{1,3},{0,1},{10,8},{12,10},{14... | collective-permute-start | bytes 983048 | tf_op jit(solution)/shard_map/ppermute | solution.py:402
  7.4 10.6 %collective-permute-start = (bf16[640,256]{1,0:T(8,128)(2,1)S(1)}, bf16[640,256]{1,0:T(8,128)(2,1)S(1)}, u32[]{:S(2)}, u32[]{:S(2)}) collective-permute-start(bf16[640,256]{1,0:T(8,128)(2,1)S(1)} %slice.7.refs_6_), channel_id=1, source_target_pairs={{0,2},{2,4},{4,6},{6,7},{7,5},{5,3},{3,1},{1,0},{8,10},{10,12},{12... | collective-permute-start | bytes 983048 | tf_op jit(solution)/shard_map/ppermute | solution.py:402
  9.7 10.0 %collective-permute-start.15 = (bf16[64,512]{1,0:T(8,128)(2,1)S(1)}, bf16[64,512]{1,0:T(8,128)(2,1)S(1)}, u32[]{:S(2)}, u32[]{:S(2)}) collective-permute-start(bf16[64,512]{1,0:T(8,128)(2,1)S(1)} %fusion), channel_id=1, source_target_pairs={{0,2},{1,3},{2,0},{3,1},{4,6},{5,7},{6,4},{7,5},{8,10},{9,11},{10,... | collective-permute-start | bytes 196616 | tf_op jit(solution)/shard_map/ppermute | solution.py:399
  12.4 13.1 %collective-permute-start.8 = (bf16[640,256]{1,0:T(8,128)(2,1)S(1)}, bf16[640,256]{1,0:T(8,128)(2,1)S(1)}, u32[]{:S(2)}, u32[]{:S(2)}) collective-permute-start(bf16[640,256]{1,0:T(8,128)(2,1)S(1)} %get-tuple-element.26.refs_7_), channel_id=1, source_target_pairs={{0,2},{2,4},{4,6},{6,7},{7,5},{5,3},{3,1},{1,0},{8,10},{10,12},{12... | collective-permute-start | bytes 983048 | tf_op jit(solution)/shard_map/ppermute | solution.py:402
  12.5 15.6 %collective-permute-start.11 = (bf16[640,256]{1,0:T(8,128)(2,1)S(1)}, bf16[640,256]{1,0:T(8,128)(2,1)S(1)}, u32[]{:S(2)}, u32[]{:S(2)}) collective-permute-start(bf16[640,256]{1,0:T(8,128)(2,1)S(1)} %slice.7.refs_6_), channel_id=1, source_target_pairs={{2,0},{4,2},{6,4},{7,6},{5,7},{3,5},{1,3},{0,1},{10,8},{12,10},{14... | collective-permute-start | bytes 983048 | tf_op jit(solution)/shard_map/ppermute | solution.py:402
  16.4 15.4 %collective-permute-start.5 = (bf16[640,256]{1,0:T(8,128)(2,1)S(1)}, bf16[640,256]{1,0:T(8,128)(2,1)S(1)}, u32[]{:S(2)}, u32[]{:S(2)}) collective-permute-start(bf16[640,256]{1,0:T(8,128)(2,1)S(1)} %collective-permute-done.4.refs_9_), channel_id=1, source_target_pairs={{2,0},{4,2},{6,4},{7,6},{5,7},{3,5},{1,3},{0,1},{10,8},{12,10},{14... | collective-permute-start | bytes 983048 | tf_op jit(solution)/shard_map/ppermute | solution.py:402
  18.1 15.2 %collective-permute-start.1 = (bf16[640,256]{1,0:T(8,128)(2,1)S(1)}, bf16[640,256]{1,0:T(8,128)(2,1)S(1)}, u32[]{:S(2)}, u32[]{:S(2)}) collective-permute-start(bf16[640,256]{1,0:T(8,128)(2,1)S(1)} %collective-permute-done.refs_6_), channel_id=1, source_target_pairs={{0,2},{2,4},{4,6},{6,7},{7,5},{5,3},{3,1},{1,0},{8,10},{10,12},{12... | collective-permute-start | bytes 983048 | tf_op jit(solution)/shard_map/ppermute | solution.py:402
  19.7 16.1 %collective-permute-start.16 = (bf16[32,512]{1,0:T(8,128)(2,1)S(1)}, bf16[32,512]{1,0:T(8,128)(2,1)S(1)}, u32[]{:S(2)}, u32[]{:S(2)}) collective-permute-start(bf16[32,512]{1,0:T(8,128)(2,1)S(1)} %fusion.4), channel_id=1, source_target_pairs={{0,4},{1,5},{2,6},{3,7},{4,0},{5,1},{6,2},{7,3},{8,12},{9,13},{10,... | collective-permute-start | bytes 98312 | tf_op jit(solution)/shard_map/ppermute | solution.py:399
  25.6 27.0 %collective-permute-start.9 = (bf16[640,256]{1,0:T(8,128)(2,1)S(1)}, bf16[640,256]{1,0:T(8,128)(2,1)}, u32[]{:S(2)}, u32[]{:S(2)}) collective-permute-start(bf16[640,256]{1,0:T(8,128)(2,1)S(1)} %collective-permute-done.8.refs_7_), channel_id=1, source_target_pairs={{0,2},{2,4},{4,6},{6,7},{7,5},{5,3},{3,1},{1,0},{8,10},{10,12},{12... | collective-permute-start | bytes 983048 | tf_op jit(solution)/shard_map/ppermute | solution.py:402
  28.1 25.6 %collective-permute-start.12 = (bf16[640,256]{1,0:T(8,128)(2,1)S(1)}, bf16[640,256]{1,0:T(8,128)(2,1)}, u32[]{:S(2)}, u32[]{:S(2)}) collective-permute-start(bf16[640,256]{1,0:T(8,128)(2,1)S(1)} %collective-permute-done.11.refs_8_), channel_id=1, source_target_pairs={{2,0},{4,2},{6,4},{7,6},{5,7},{3,5},{1,3},{0,1},{10,8},{12,10},{14... | collective-permute-start | bytes 983048 | tf_op jit(solution)/shard_map/ppermute | solution.py:402
  31.9 23.9 %collective-permute-start.6 = (bf16[640,256]{1,0:T(8,128)(2,1)S(1)}, bf16[640,256]{1,0:T(8,128)(2,1)S(1)}, u32[]{:S(2)}, u32[]{:S(2)}) collective-permute-start(bf16[640,256]{1,0:T(8,128)(2,1)S(1)} %collective-permute-done.5.refs_9_), channel_id=1, source_target_pairs={{2,0},{4,2},{6,4},{7,6},{5,7},{3,5},{1,3},{0,1},{10,8},{12,10},{14... | collective-permute-start | bytes 983048 | tf_op jit(solution)/shard_map/ppermute | solution.py:402
  33.3 24.9 %collective-permute-start.2 = (bf16[640,256]{1,0:T(8,128)(2,1)S(1)}, bf16[640,256]{1,0:T(8,128)(2,1)S(1)}, u32[]{:S(2)}, u32[]{:S(2)}) collective-permute-start(bf16[640,256]{1,0:T(8,128)(2,1)S(1)} %collective-permute-done.1.refs_6_), channel_id=1, source_target_pairs={{0,2},{2,4},{4,6},{6,7},{7,5},{5,3},{3,1},{1,0},{8,10},{10,12},{12... | collective-permute-start | bytes 983048 | tf_op jit(solution)/shard_map/ppermute | solution.py:402
  35.8 1.3 collective-permute-start.17
  37.1 3.9 %collective-permute-start.18 = (bf16[32,512]{1,0:T(8,128)(2,1)S(1)}, bf16[32,512]{1,0:T(8,128)(2,1)S(1)}, u32[]{:S(2)}, u32[]{:S(2)}) collective-permute-start(bf16[32,512]{1,0:T(8,128)(2,1)S(1)} %fusion.3.refs_0_), channel_id=1, source_target_pairs={{0,16},{8,24},{16,0},{24,8},{1,17},{9,25},{17,1},{25,9},{2,18},{10... | collective-permute-start | bytes 98312 | tf_op jit(solution)/shard_map/ppermute | solution.py:399
  41.0 3.6 %collective-permute-start.19 = (bf16[32,512]{1,0:T(8,128)(2,1)S(1)}, bf16[32,512]{1,0:T(8,128)(2,1)S(1)}, u32[]{:S(2)}, u32[]{:S(2)}) collective-permute-start(bf16[32,512]{1,0:T(8,128)(2,1)S(1)} %fusion.3.refs_0_), channel_id=1, source_target_pairs={{0,24},{8,16},{16,8},{24,0},{1,25},{9,17},{17,9},{25,1},{2,26},{10... | collective-permute-start | bytes 98312 | tf_op jit(solution)/shard_map/ppermute | solution.py:399
  48.0 6.7 %collective-permute-start.20 = (bf16[32,512]{1,0:T(8,128)(2,1)S(1)}, bf16[32,512]{1,0:T(8,128)(2,1)S(1)}, u32[]{:S(2)}, u32[]{:S(2)}) collective-permute-start(bf16[32,512]{1,0:T(8,128)(2,1)S(1)} %far.2.refs_13_), channel_id=1, source_target_pairs={{0,4},{1,5},{2,6},{3,7},{4,0},{5,1},{6,2},{7,3},{8,12},{9,13},{10,... | collective-permute-start | bytes 98312 | tf_op jit(solution)/shard_map/ppermute | solution.py:399
  52.6 17.6 %collective-permute-start.10 = (bf16[640,256]{1,0:T(8,128)(2,1)}, bf16[640,256]{1,0:T(8,128)(2,1)S(1)}, u32[]{:S(2)}, u32[]{:S(2)}) collective-permute-start(bf16[640,256]{1,0:T(8,128)(2,1)} %collective-permute-done.9.refs_7_), channel_id=1, source_target_pairs={{0,2},{2,4},{4,6},{6,7},{7,5},{5,3},{3,1},{1,0},{8,10},{10,12},{12... | collective-permute-start | bytes 983048 | tf_op jit(solution)/shard_map/ppermute | solution.py:402
  53.6 16.6 %collective-permute-start.13 = (bf16[640,256]{1,0:T(8,128)(2,1)}, bf16[640,256]{1,0:T(8,128)(2,1)S(1)}, u32[]{:S(2)}, u32[]{:S(2)}) collective-permute-start(bf16[640,256]{1,0:T(8,128)(2,1)} %collective-permute-done.12.refs_8_), channel_id=1, source_target_pairs={{2,0},{4,2},{6,4},{7,6},{5,7},{3,5},{1,3},{0,1},{10,8},{12,10},{14... | collective-permute-start | bytes 983048 | tf_op jit(solution)/shard_map/ppermute | solution.py:402
  54.7 11.1 %collective-permute-start.21 = (bf16[64,512]{1,0:T(8,128)(2,1)S(1)}, bf16[64,512]{1,0:T(8,128)(2,1)S(1)}, u32[]{:S(2)}, u32[]{:S(2)}) collective-permute-start(bf16[64,512]{1,0:T(8,128)(2,1)S(1)} %pad_maximum_fusion.2), channel_id=1, source_target_pairs={{0,2},{1,3},{2,0},{3,1},{4,6},{5,7},{6,4},{7,5},{8,10},{9,11},{10,... | collective-permute-start | bytes 196616 | tf_op jit(solution)/shard_map/ppermute | solution.py:399
  55.7 18.5 %collective-permute-start.7 = (bf16[640,256]{1,0:T(8,128)(2,1)S(1)}, bf16[640,256]{1,0:T(8,128)(2,1)S(1)}, u32[]{:S(2)}, u32[]{:S(2)}) collective-permute-start(bf16[640,256]{1,0:T(8,128)(2,1)S(1)} %collective-permute-done.6.refs_9_), channel_id=1, source_target_pairs={{2,0},{4,2},{6,4},{7,6},{5,7},{3,5},{1,3},{0,1},{10,8},{12,10},{14... | collective-permute-start | bytes 983048 | tf_op jit(solution)/shard_map/ppermute | solution.py:402
  58.2 16.1 %collective-permute-start.3 = (bf16[640,256]{1,0:T(8,128)(2,1)S(1)}, bf16[640,256]{1,0:T(8,128)(2,1)S(1)}, u32[]{:S(2)}, u32[]{:S(2)}) collective-permute-start(bf16[640,256]{1,0:T(8,128)(2,1)S(1)} %collective-permute-done.2.refs_6_), channel_id=1, source_target_pairs={{0,2},{2,4},{4,6},{6,7},{7,5},{5,3},{3,1},{1,0},{8,10},{10,12},{12... | collective-permute-start | bytes 983048 | tf_op jit(solution)/shard_map/ppermute | solution.py:402
  65.8 8.4 %collective-permute-start.22 = (bf16[128,512]{1,0:T(8,128)(2,1)S(1)}, bf16[128,512]{1,0:T(8,128)(2,1)S(1)}, u32[]{:S(2)}, u32[]{:S(2)}) collective-permute-start(bf16[128,512]{1,0:T(8,128)(2,1)S(1)} %pad_maximum_fusion), channel_id=1, source_target_pairs={{0,1},{1,0},{2,3},{3,2},{4,5},{5,4},{6,7},{7,6},{8,9},{9,8},{10,11... | collective-permute-start | bytes 393224 | tf_op jit(solution)/shard_map/ppermute | solution.py:399
  74.2 47.4 %copy-start.6 = (s32[1,2]{1,0:T(1,128)S(1)}, s32[1,2]{1,0:T(1,128)}, u32[]{:S(2)}) copy-start(s32[1,2]{1,0:T(1,128)} %links_ref.3) | copy-start | bytes 28
  74.2 51.7 %copy-start.3 = (s32[1,8]{1,0:T(1,128)S(1)}, s32[1,8]{1,0:T(1,128)}, u32[]{:S(2)}) copy-start(s32[1,8]{1,0:T(1,128)} %refs_1_.19) | copy-start | bytes 100
  83.2 5.0 %collective-permute-start.37 = (bf16[128,512]{1,0:T(8,128)(2,1)S(1)}, bf16[128,512]{1,0:T(8,128)(2,1)S(1)}, u32[]{:S(2)}, u32[]{:S(2)}) collective-permute-start(bf16[128,512]{1,0:T(8,128)(2,1)S(1)} %get-tuple-element.49), channel_id=1, source_target_pairs={{0,1},{1,0},{2,3},{3,2},{4,5},{5,4},{6,7},{7,6},{8,9},{9,8},{10,11... | collective-permute-start | bytes 393224 | tf_op jit(solution)/shard_map/ppermute | solution.py:399
  84.3 10.6 %collective-permute-start.27 = (bf16[640,256]{1,0:T(8,128)(2,1)S(1)}, bf16[640,256]{1,0:T(8,128)(2,1)S(1)}, u32[]{:S(2)}, u32[]{:S(2)}) collective-permute-start(bf16[640,256]{1,0:T(8,128)(2,1)S(1)} %get-tuple-element.39.refs_7_), channel_id=1, source_target_pairs={{2,0},{4,2},{6,4},{7,6},{5,7},{3,5},{1,3},{0,1},{10,8},{12,10},{14... | collective-permute-start | bytes 983048 | tf_op jit(solution)/shard_map/ppermute | solution.py:402
  85.0 10.6 %collective-permute-start.23 = (bf16[640,256]{1,0:T(8,128)(2,1)S(1)}, bf16[640,256]{1,0:T(8,128)(2,1)S(1)}, u32[]{:S(2)}, u32[]{:S(2)}) collective-permute-start(bf16[640,256]{1,0:T(8,128)(2,1)S(1)} %get-tuple-element.38.refs_6_), channel_id=1, source_target_pairs={{0,2},{2,4},{4,6},{6,7},{7,5},{5,3},{3,1},{1,0},{8,10},{10,12},{12... | collective-permute-start | bytes 983048 | tf_op jit(solution)/shard_map/ppermute | solution.py:402
  88.3 8.7 %collective-permute-start.38 = (bf16[64,512]{1,0:T(8,128)(2,1)S(1)}, bf16[64,512]{1,0:T(8,128)(2,1)S(1)}, u32[]{:S(2)}, u32[]{:S(2)}) collective-permute-start(bf16[64,512]{1,0:T(8,128)(2,1)S(1)} %fusion.1), channel_id=1, source_target_pairs={{0,2},{1,3},{2,0},{3,1},{4,6},{5,7},{6,4},{7,5},{8,10},{9,11},{10,... | collective-permute-start | bytes 196616 | tf_op jit(solution)/shard_map/ppermute | solution.py:399
  89.5 13.4 %collective-permute-start.31 = (bf16[640,256]{1,0:T(8,128)(2,1)S(1)}, bf16[640,256]{1,0:T(8,128)(2,1)S(1)}, u32[]{:S(2)}, u32[]{:S(2)}) collective-permute-start(bf16[640,256]{1,0:T(8,128)(2,1)S(1)} %get-tuple-element.39.refs_7_), channel_id=1, source_target_pairs={{0,2},{2,4},{4,6},{6,7},{7,5},{5,3},{3,1},{1,0},{8,10},{10,12},{12... | collective-permute-start | bytes 983048 | tf_op jit(solution)/shard_map/ppermute | solution.py:402
  90.4 15.0 %collective-permute-start.34 = (bf16[640,256]{1,0:T(8,128)(2,1)S(1)}, bf16[640,256]{1,0:T(8,128)(2,1)S(1)}, u32[]{:S(2)}, u32[]{:S(2)}) collective-permute-start(bf16[640,256]{1,0:T(8,128)(2,1)S(1)} %get-tuple-element.38.refs_6_), channel_id=1, source_target_pairs={{2,0},{4,2},{6,4},{7,6},{5,7},{3,5},{1,3},{0,1},{10,8},{12,10},{14... | collective-permute-start | bytes 983048 | tf_op jit(solution)/shard_map/ppermute | solution.py:402
  94.9 15.4 %collective-permute-start.28 = (bf16[640,256]{1,0:T(8,128)(2,1)S(1)}, bf16[640,256]{1,0:T(8,128)(2,1)S(1)}, u32[]{:S(2)}, u32[]{:S(2)}) collective-permute-start(bf16[640,256]{1,0:T(8,128)(2,1)S(1)} %collective-permute-done.27.refs_9_), channel_id=1, source_target_pairs={{2,0},{4,2},{6,4},{7,6},{5,7},{3,5},{1,3},{0,1},{10,8},{12,10},{14... | collective-permute-start | bytes 983048 | tf_op jit(solution)/shard_map/ppermute | solution.py:402
  95.6 15.1 %collective-permute-start.24 = (bf16[640,256]{1,0:T(8,128)(2,1)S(1)}, bf16[640,256]{1,0:T(8,128)(2,1)S(1)}, u32[]{:S(2)}, u32[]{:S(2)}) collective-permute-start(bf16[640,256]{1,0:T(8,128)(2,1)S(1)} %collective-permute-done.23.refs_6_), channel_id=1, source_target_pairs={{0,2},{2,4},{4,6},{6,7},{7,5},{5,3},{3,1},{1,0},{8,10},{10,12},{12... | collective-permute-start | bytes 983048 | tf_op jit(solution)/shard_map/ppermute | solution.py:402
  97.0 16.1 %collective-permute-start.39 = (bf16[32,512]{1,0:T(8,128)(2,1)S(1)}, bf16[32,512]{1,0:T(8,128)(2,1)S(1)}, u32[]{:S(2)}, u32[]{:S(2)}) collective-permute-start(bf16[32,512]{1,0:T(8,128)(2,1)S(1)} %fusion.5), channel_id=1, source_target_pairs={{0,4},{1,5},{2,6},{3,7},{4,0},{5,1},{6,2},{7,3},{8,12},{9,13},{10,... | collective-permute-start | bytes 98312 | tf_op jit(solution)/shard_map/ppermute | solution.py:399
  102.9 26.2 %collective-permute-start.32 = (bf16[640,256]{1,0:T(8,128)(2,1)S(1)}, bf16[640,256]{1,0:T(8,128)(2,1)S(1)}, u32[]{:S(2)}, u32[]{:S(2)}) collective-permute-start(bf16[640,256]{1,0:T(8,128)(2,1)S(1)} %collective-permute-done.31.refs_7_), channel_id=1, source_target_pairs={{0,2},{2,4},{4,6},{6,7},{7,5},{5,3},{3,1},{1,0},{8,10},{10,12},{12... | collective-permute-start | bytes 983048 | tf_op jit(solution)/shard_map/ppermute | solution.py:402
  105.4 23.9 %collective-permute-start.35 = (bf16[640,256]{1,0:T(8,128)(2,1)S(1)}, bf16[640,256]{1,0:T(8,128)(2,1)S(1)}, u32[]{:S(2)}, u32[]{:S(2)}) collective-permute-start(bf16[640,256]{1,0:T(8,128)(2,1)S(1)} %collective-permute-done.34.refs_8_), channel_id=1, source_target_pairs={{2,0},{4,2},{6,4},{7,6},{5,7},{3,5},{1,3},{0,1},{10,8},{12,10},{14... | collective-permute-start | bytes 983048 | tf_op jit(solution)/shard_map/ppermute | solution.py:402
  110.4 21.7 %collective-permute-start.29 = (bf16[640,256]{1,0:T(8,128)(2,1)S(1)}, bf16[640,256]{1,0:T(8,128)(2,1)S(1)}, u32[]{:S(2)}, u32[]{:S(2)}) collective-permute-start(bf16[640,256]{1,0:T(8,128)(2,1)S(1)} %collective-permute-done.28.refs_9_), channel_id=1, source_target_pairs={{2,0},{4,2},{6,4},{7,6},{5,7},{3,5},{1,3},{0,1},{10,8},{12,10},{14... | collective-permute-start | bytes 983048 | tf_op jit(solution)/shard_map/ppermute | solution.py:402
  110.7 22.6 %collective-permute-start.25 = (bf16[640,256]{1,0:T(8,128)(2,1)S(1)}, bf16[640,256]{1,0:T(8,128)(2,1)S(1)}, u32[]{:S(2)}, u32[]{:S(2)}) collective-permute-start(bf16[640,256]{1,0:T(8,128)(2,1)S(1)} %collective-permute-done.24.refs_6_), channel_id=1, source_target_pairs={{0,2},{2,4},{4,6},{6,7},{7,5},{5,3},{3,1},{1,0},{8,10},{10,12},{12... | collective-permute-start | bytes 983048 | tf_op jit(solution)/shard_map/ppermute | solution.py:402
  113.1 1.3 collective-permute-start.40
  114.4 3.9 %collective-permute-start.41 = (bf16[32,512]{1,0:T(8,128)(2,1)S(1)}, bf16[32,512]{1,0:T(8,128)(2,1)S(1)}, u32[]{:S(2)}, u32[]{:S(2)}) collective-permute-start(bf16[32,512]{1,0:T(8,128)(2,1)S(1)} %fusion.2.refs_0_), channel_id=1, source_target_pairs={{0,16},{8,24},{16,0},{24,8},{1,17},{9,25},{17,1},{25,9},{2,18},{10... | collective-permute-start | bytes 98312 | tf_op jit(solution)/shard_map/ppermute | solution.py:399
  118.3 3.3 %collective-permute-start.42 = (bf16[32,512]{1,0:T(8,128)(2,1)S(1)}, bf16[32,512]{1,0:T(8,128)(2,1)S(1)}, u32[]{:S(2)}, u32[]{:S(2)}) collective-permute-start(bf16[32,512]{1,0:T(8,128)(2,1)S(1)} %fusion.2.refs_0_), channel_id=1, source_target_pairs={{0,24},{8,16},{16,8},{24,0},{1,25},{9,17},{17,9},{25,1},{2,26},{10... | collective-permute-start | bytes 98312 | tf_op jit(solution)/shard_map/ppermute | solution.py:399
  124.4 6.8 %collective-permute-start.43 = (bf16[32,512]{1,0:T(8,128)(2,1)S(1)}, bf16[32,512]{1,0:T(8,128)(2,1)S(1)}, u32[]{:S(2)}, u32[]{:S(2)}) collective-permute-start(bf16[32,512]{1,0:T(8,128)(2,1)S(1)} %far.3.refs_13_), channel_id=1, source_target_pairs={{0,4},{1,5},{2,6},{3,7},{4,0},{5,1},{6,2},{7,3},{8,12},{9,13},{10,... | collective-permute-start | bytes 98312 | tf_op jit(solution)/shard_map/ppermute | solution.py:399
  129.1 17.2 %collective-permute-start.33 = (bf16[640,256]{1,0:T(8,128)(2,1)S(1)}, bf16[640,256]{1,0:T(8,128)(2,1)S(1)}, u32[]{:S(2)}, u32[]{:S(2)}) collective-permute-start(bf16[640,256]{1,0:T(8,128)(2,1)S(1)} %collective-permute-done.32.refs_7_), channel_id=1, source_target_pairs={{0,2},{2,4},{4,6},{6,7},{7,5},{5,3},{3,1},{1,0},{8,10},{10,12},{12... | collective-permute-start | bytes 983048 | tf_op jit(solution)/shard_map/ppermute | solution.py:402
  129.2 17.1 %collective-permute-start.36 = (bf16[640,256]{1,0:T(8,128)(2,1)S(1)}, bf16[640,256]{1,0:T(8,128)(2,1)S(1)}, u32[]{:S(2)}, u32[]{:S(2)}) collective-permute-start(bf16[640,256]{1,0:T(8,128)(2,1)S(1)} %collective-permute-done.35.refs_8_), channel_id=1, source_target_pairs={{2,0},{4,2},{6,4},{7,6},{5,7},{3,5},{1,3},{0,1},{10,8},{12,10},{14... | collective-permute-start | bytes 983048 | tf_op jit(solution)/shard_map/ppermute | solution.py:402
  131.2 10.7 %collective-permute-start.44 = (bf16[64,512]{1,0:T(8,128)(2,1)S(1)}, bf16[64,512]{1,0:T(8,128)(2,1)S(1)}, u32[]{:S(2)}, u32[]{:S(2)}) collective-permute-start(bf16[64,512]{1,0:T(8,128)(2,1)S(1)} %pad_maximum_fusion.3), channel_id=1, source_target_pairs={{0,2},{1,3},{2,0},{3,1},{4,6},{5,7},{6,4},{7,5},{8,10},{9,11},{10,... | collective-permute-start | bytes 196616 | tf_op jit(solution)/shard_map/ppermute | solution.py:399
  132.1 18.3 %collective-permute-start.30 = (bf16[640,256]{1,0:T(8,128)(2,1)S(1)}, bf16[640,256]{1,0:T(8,128)(2,1)S(1)}, u32[]{:S(2)}, u32[]{:S(2)}) collective-permute-start(bf16[640,256]{1,0:T(8,128)(2,1)S(1)} %collective-permute-done.29.refs_9_), channel_id=1, source_target_pairs={{2,0},{4,2},{6,4},{7,6},{5,7},{3,5},{1,3},{0,1},{10,8},{12,10},{14... | collective-permute-start | bytes 983048 | tf_op jit(solution)/shard_map/ppermute | solution.py:402
  133.3 17.1 %collective-permute-start.26 = (bf16[640,256]{1,0:T(8,128)(2,1)S(1)}, bf16[640,256]{1,0:T(8,128)(2,1)S(1)}, u32[]{:S(2)}, u32[]{:S(2)}) collective-permute-start(bf16[640,256]{1,0:T(8,128)(2,1)S(1)} %collective-permute-done.25.refs_6_), channel_id=1, source_target_pairs={{0,2},{2,4},{4,6},{6,7},{7,5},{5,3},{3,1},{1,0},{8,10},{10,12},{12... | collective-permute-start | bytes 983048 | tf_op jit(solution)/shard_map/ppermute | solution.py:402
  142.0 8.4 %collective-permute-start.45 = (bf16[128,512]{1,0:T(8,128)(2,1)S(1)}, bf16[128,512]{1,0:T(8,128)(2,1)S(1)}, u32[]{:S(2)}, u32[]{:S(2)}) collective-permute-start(bf16[128,512]{1,0:T(8,128)(2,1)S(1)} %pad_maximum_fusion.1), channel_id=1, source_target_pairs={{0,1},{1,0},{2,3},{3,2},{4,5},{5,4},{6,7},{7,6},{8,9},{9,8},{10,11... | collective-permute-start | bytes 393224 | tf_op jit(solution)/shard_map/ppermute | solution.py:399
  (5 other events, 88.6 us)

commit v3 on v2

--- a/solution.py
+++ b/solution.py
@@ -57,6 +57,7 @@
     return share
 
 
+SHARE = 5
 DEPTH = 3
 
 
@@ -75,10 +76,9 @@
         return copy
 
 
-def front(me, v, basis, transfer, rank):
+def front(me, v, basis, transfer, rank, split):
     leaf_rows, probe_cols = v.shape
     rank_cols, parent_cols = transfer.shape
-    part = (leaf_rows + rank_cols) // 2
     half = probe_cols // 2
 
     def body(me_ref, rank_ref, v_in, basis_in, transfer_in, bottom_ref, away_ref, kept_ref, v_ref, basis_ref, transfer_ref, upward_ref, sems):
@@ -91,8 +91,8 @@
         skeleton = contract3(basis_ref[...], v, TN)
         row = lax.broadcasted_iota(jnp.int32, skeleton.shape, 0)
         skeleton = jnp.where(row < rank_ref[0], skeleton, 0.0)
-        bottom_ref[: leaf_rows - part, :] = v[part:, :].astype(BF16)
-        bottom_ref[leaf_rows - part :, :] = skeleton.astype(BF16)
+        bottom_ref[: leaf_rows - split, :] = v[split:, :].astype(BF16)
+        bottom_ref[leaf_rows - split :, :] = skeleton.astype(BF16)
         last.wait()
         upward_ref[...] = contract3(skeleton, transfer_ref[...], TN)
         bit = me_ref[0] & 1
@@ -102,7 +102,7 @@
     return pl.pallas_call(
         body,
         out_shape=(
-            jax.ShapeDtypeStruct((part, probe_cols), BF16),
+            jax.ShapeDtypeStruct((leaf_rows + rank_cols - split, probe_cols), BF16),
             jax.ShapeDtypeStruct((half, parent_cols), BF16),
             jax.ShapeDtypeStruct((half, parent_cols), F32),
         ),
@@ -142,13 +142,14 @@
 
 def take_all(tables, n, first, count, copies, blocks_ref, links_ref, parts, held, near_ref, coupled_ref):
     block_ref, link_ref, held_ref = held
-    part = parts[0].shape[0]
+    split = parts[0].shape[0]
+    rows = (pl.ds(0, split), pl.ds(split, parts[1].shape[0]))
     leaf_rows = near_ref.shape[0]
 
     def fetch(j):
         at = j % DEPTH
         live, slot, linked, link = named(*tables, first + j, n)
-        got = [copies.start(parts[2 * j + c], held_ref.at[at, pl.ds(c * part, part)]) for c in (0, 1)]
+        got = [copies.start(parts[2 * j + c], held_ref.at[at, rows[c]]) for c in (0, 1)]
         block = copies.start(blocks_ref.at[slot], block_ref.at[at], live)
         tie = copies.start(links_ref.at[link], link_ref.at[at], linked)
         return live, linked, got, block, tie
@@ -175,11 +176,11 @@
             coupled_ref[...] += contract2(link_ref[at], held_ref[at, leaf_rows:, :], NN)
 
 
-def held_scratch(blocks, links, part):
+def held_scratch(blocks, links, message):
     return [
         pltpu.VMEM((DEPTH,) + blocks.shape[1:], BF16),
         pltpu.VMEM((DEPTH,) + links.shape[1:], F32),
-        pltpu.VMEM((DEPTH, 2 * part.shape[0], part.shape[1]), BF16),
+        pltpu.VMEM((DEPTH, sum(part.shape[0] for part in message), message[0].shape[1]), BF16),
     ]
 
 
@@ -219,7 +220,7 @@
         out_shape=outs,
         in_specs=[SMEM] * 4 + [HBM] * 2 + [ANY] * len(operands),
         out_specs=(VMEM, VMEM),
-        scratch_shapes=held_scratch(blocks, links, messages[0][0])
+        scratch_shapes=held_scratch(blocks, links, messages[0])
         + [pltpu.SemaphoreType.DMA((4 * count + 2,))],
         cost_estimate=cost(2 * count * (blocks.shape[1] ** 2) * probe_cols, 4 * count * (blocks.shape[1] ** 2)),
         compiler_params=ROOM,
@@ -344,7 +345,7 @@
         + [ANY] * count
         + ([HBM] if final else []),
         out_specs=(VMEM,) * len(outs),
-        scratch_shapes=held_scratch(blocks, links, parts[0])
+        scratch_shapes=held_scratch(blocks, links, messages[0])
         + [
             pltpu.VMEM(transfer.shape, F32),
             pltpu.VMEM(basis.shape, F32),
@@ -402,7 +403,7 @@
         return lax.ppermute(value, "col", perm)
 
     def multiply(vector, top, start):
-        bottom, away, kept = front(mine, keep(vector), leaf_basis, transfer, leaf_rank)
+        bottom, away, kept = front(mine, keep(vector), leaf_basis, transfer, leaf_rank, top.shape[0])
 
         for b in range(bits):
             if b:
@@ -427,18 +428,16 @@
             messages += [right, left]
         opposite = (pass_on(right[0], to_right), pass_on(left[1], to_left))
         sums = absorb(tables, n, 0, blocks, link_blocks, [(top, keep(bottom))], ())
-        first = 1
-        for s in range(1, steps + 1):
-            taken = messages[first : 2 * s + 1]
-            sums = absorb(tables, n, first, blocks, link_blocks, taken, sums)
-            first = 2 * s + 1
+        sums = absorb(tables, n, 1, blocks, link_blocks, messages[1:-2], sums)
+        sums = absorb(tables, n, n - 3, blocks, link_blocks, messages[-2:], sums)
+        first = n - 1
         return back(
             tables, n, first, leaf_rank, blocks, link_blocks, messages[first:] + [opposite],
             *sums, far, transfer, leaf_basis, start,
         )
 
-    part = (leaf_rows + leaf_basis.shape[1]) // 2
-    term_one, top = multiply(probes, probes[:part].astype(BF16), None)
+    split = (leaf_rows + leaf_basis.shape[1]) * SHARE // 10 // 128 * 128
+    term_one, top = multiply(probes, probes[:split].astype(BF16), None)
     (term_two,) = multiply(term_one, top, past)
     return (term_one, term_two)
 

time: 159 us -> 156 us (0.981)
  waiting for transfers between devices: 48.9 us -> 53.9 us
  Pallas kernels: 54.8 us -> 50.6 us
  starting transfers between devices: 46.8 us -> 44.1 us
    pallas_call x8 -> x6, Pallas kernels: 31.8 us -> 27.5 us  [absorb(): pl.pallas_call(body, out_shape=outs, in_specs=[SMEM] * 4 + [HBM] * 2 + [A...]
    ppermute x18, waiting for transfers between devices: 22.7 us -> 26.5 us  [swap(): return lax.ppermute(value, axis, [(i, i ^ distance) for i in range(size)])]
    ppermute x18, starting transfers between devices: 16.1 us -> 13.5 us  [swap(): return lax.ppermute(value, axis, [(i, i ^ distance) for i in range(size)])]
  transfers between devices with their start and end apart: 46 -> 46, of which waited for: 19 -> 20; matrix products, arithmetic and copies ran while one was open for 1% -> 1% of each run, Pallas kernels for 24% -> 21%
where the time goes in v3:
time: 156 us; the launch traced here: 154 us
  waiting for transfers between devices  53.9 us (35%)
  Pallas kernels  50.6 us (32%)
  starting transfers between devices  44.1 us (28%)
  local copies, waits for them, and re-layouts  3.18 us (2%)
  between operations  2.47 us (2%)
    ppermute x28, starting transfers between devices, pass_on(): return lax.ppermute(value, 'col', perm)  30.6 us
    pallas_call x6, Pallas kernels, absorb(): pl.pallas_call(body, out_shape=outs, in_specs=[SMEM] * 4 + [HBM] * 2 + [A...  27.5 us
    ppermute x28, waiting for transfers between devices, pass_on(): return lax.ppermute(value, 'col', perm)  27.3 us
    ppermute x18, waiting for transfers between devices, swap(): return lax.ppermute(value, axis, [(i, i ^ distance) for i in range(size)])  26.5 us
    ppermute x18, starting transfers between devices, swap(): return lax.ppermute(value, axis, [(i, i ^ distance) for i in range(size)])  13.5 us
    pallas_call x2, Pallas kernels, back(): pl.pallas_call(body, out_shape=outs, in_specs=[SMEM] * 5 + [HBM] * 2 + [A...  11.6 us
    pallas_call x2, Pallas kernels, front(): pl.pallas_call(body, out_shape=(jax.ShapeDtypeStruct((leaf_rows + rank_co...  6 us
    pallas_call x2, Pallas kernels, far_share(): pl.pallas_call(body, out_shape=jax.ShapeDtypeStruct(parents[0].shape, BF1...  5.47 us
  transfers between devices with their start and end apart: 46, of which 20 were waited for; matrix products, arithmetic and copies ran while one was open for 1% of the time, Pallas kernels for 21%

profile of v3, /device:TPU:16, one launch (start us, length us, event | category | flops | bytes accessed | tf_op | source)
XLA Modules:
  0.0 154.3 jit_solution(17266282386903043554)
XLA Ops:
  1.3 3.0 %front.2 = (bf16[640,256]{1,0:T(8,128)(2,1)S(1)}, bf16[128,512]{1,0:T(8,128)(2,1)S(1)}, f32[128,512]{1,0:T(8,128)S(1)}) custom-call(s32[1]{0:T(128)} %bitcast.me_ref.refs_0_, s32[1]{0:T(128)S(6)} %copy.14.rank_ref.refs_4_, f32[1024,256]{1,0:T(8,128)} %refs_17_.1, f32[1024,256]{1,0:T(8,128)} %refs_12_.3, f32[256,512]{1,0:T(8,128)} %bitcast.46), custom_call_target="tpu_custom_call" | custom-call | flops 402653184 | bytes 2097152 | tf_op jit(solution)/shard_map/front/pallas_call | solution.py:102
  4.3 1.6 %collective-permute-start.14 = (bf16[128,512]{1,0:T(8,128)(2,1)S(1)}, bf16[128,512]{1,0:T(8,128)(2,1)S(1)}, u32[]{:S(2)}, u32[]{:S(2)}) collective-permute-start(bf16[128,512]{1,0:T(8,128)(2,1)S(1)} %get-tuple-element.30), channel_id=1, source_target_pairs={{0,1},{1,0},{2,3},{3,2},{4,5},{5,4},{6,7},{7,6},{8,9},{9,8},{10,11... | collective-permute-start | bytes 393224 | tf_op jit(solution)/shard_map/ppermute | solution.py:400
  6.3 1.1 slice.7.refs_6_
  7.4 1.6 %collective-permute-start = (bf16[640,256]{1,0:T(8,128)(2,1)S(1)}, bf16[640,256]{1,0:T(8,128)(2,1)S(1)}, u32[]{:S(2)}, u32[]{:S(2)}) collective-permute-start(bf16[640,256]{1,0:T(8,128)(2,1)S(1)} %slice.7.refs_6_), channel_id=1, source_target_pairs={{0,2},{2,4},{4,6},{6,7},{7,5},{5,3},{3,1},{1,0},{8,10},{10,12},{12... | collective-permute-start | bytes 983048 | tf_op jit(solution)/shard_map/ppermute | solution.py:403
  9.7 2.8 %collective-permute-start.15 = (bf16[64,512]{1,0:T(8,128)(2,1)S(1)}, bf16[64,512]{1,0:T(8,128)(2,1)S(1)}, u32[]{:S(2)}, u32[]{:S(2)}) collective-permute-start(bf16[64,512]{1,0:T(8,128)(2,1)S(1)} %fusion), channel_id=1, source_target_pairs={{0,2},{1,3},{2,0},{3,1},{4,6},{5,7},{6,4},{7,5},{8,10},{9,11},{10,... | collective-permute-start | bytes 196616 | tf_op jit(solution)/shard_map/ppermute | solution.py:400
  12.5 2.0 %collective-permute-start.11 = (bf16[640,256]{1,0:T(8,128)(2,1)S(1)}, bf16[640,256]{1,0:T(8,128)(2,1)S(1)}, u32[]{:S(2)}, u32[]{:S(2)}) collective-permute-start(bf16[640,256]{1,0:T(8,128)(2,1)S(1)} %slice.7.refs_6_), channel_id=1, source_target_pairs={{2,0},{4,2},{6,4},{7,6},{5,7},{3,5},{1,3},{0,1},{10,8},{12,10},{14... | collective-permute-start | bytes 983048 | tf_op jit(solution)/shard_map/ppermute | solution.py:403
  14.5 2.0 %collective-permute-done.4.refs_9_ = bf16[640,256]{1,0:T(8,128)(2,1)S(1)} collective-permute-done((bf16[640,256]{1,0:T(8,128)(2,1)S(1)}, bf16[640,256]{1,0:T(8,128)(2,1)S(1)}, u32[]{:S(2)}, u32[]{:S(2)}) %collective-permute-start.4) | collective-permute-done | bytes 327712 | tf_op jit(solution)/shard_map/ppermute | solution.py:403
  16.6 1.5 collective-permute-done.refs_6_
  18.1 1.6 %collective-permute-start.1 = (bf16[640,256]{1,0:T(8,128)(2,1)S(1)}, bf16[640,256]{1,0:T(8,128)(2,1)S(1)}, u32[]{:S(2)}, u32[]{:S(2)}) collective-permute-start(bf16[640,256]{1,0:T(8,128)(2,1)S(1)} %collective-permute-done.refs_6_), channel_id=1, source_target_pairs={{0,2},{2,4},{4,6},{6,7},{7,5},{5,3},{3,1},{1,0},{8,10},{10,12},{12... | collective-permute-start | bytes 983048 | tf_op jit(solution)/shard_map/ppermute | solution.py:403
  20.1 5.5 %collective-permute-done.8.refs_7_ = bf16[640,256]{1,0:T(8,128)(2,1)S(1)} collective-permute-done((bf16[640,256]{1,0:T(8,128)(2,1)S(1)}, bf16[640,256]{1,0:T(8,128)(2,1)S(1)}, u32[]{:S(2)}, u32[]{:S(2)}) %collective-permute-start.8) | collective-permute-done | bytes 327712 | tf_op jit(solution)/shard_map/ppermute | solution.py:403
  25.6 2.5 %collective-permute-start.9 = (bf16[640,256]{1,0:T(8,128)(2,1)S(1)}, bf16[640,256]{1,0:T(8,128)(2,1)}, u32[]{:S(2)}, u32[]{:S(2)}) collective-permute-start(bf16[640,256]{1,0:T(8,128)(2,1)S(1)} %collective-permute-done.8.refs_7_), channel_id=1, source_target_pairs={{0,2},{2,4},{4,6},{6,7},{7,5},{5,3},{3,1},{1,0},{8,10},{10,12},{12... | collective-permute-start | bytes 983048 | tf_op jit(solution)/shard_map/ppermute | solution.py:403
  28.1 3.8 %collective-permute-done.5.refs_13_ = bf16[640,256]{1,0:T(8,128)(2,1)S(1)} collective-permute-done((bf16[640,256]{1,0:T(8,128)(2,1)S(1)}, bf16[640,256]{1,0:T(8,128)(2,1)S(1)}, u32[]{:S(2)}, u32[]{:S(2)}) %collective-permute-start.5) | collective-permute-done | bytes 327712 | tf_op jit(solution)/shard_map/ppermute | solution.py:403
  33.3 2.5 %collective-permute-start.2 = (bf16[640,256]{1,0:T(8,128)(2,1)S(1)}, bf16[640,256]{1,0:T(8,128)(2,1)S(1)}, u32[]{:S(2)}, u32[]{:S(2)}) collective-permute-start(bf16[640,256]{1,0:T(8,128)(2,1)S(1)} %collective-permute-done.1.refs_10_), channel_id=1, source_target_pairs={{0,2},{2,4},{4,6},{6,7},{7,5},{5,3},{3,1},{1,0},{8,10},{10,12},{12... | collective-permute-start | bytes 983048 | tf_op jit(solution)/shard_map/ppermute | solution.py:403
  35.9 1.2 collective-permute-done.17.refs_1_
  37.1 1.5 collective-permute-start.18
  38.6 2.4 %collective-permute-done.18.refs_2_ = bf16[32,512]{1,0:T(8,128)(2,1)S(1)} collective-permute-done((bf16[32,512]{1,0:T(8,128)(2,1)S(1)}, bf16[32,512]{1,0:T(8,128)(2,1)S(1)}, u32[]{:S(2)}, u32[]{:S(2)}) %collective-permute-start.18) | collective-permute-done | bytes 32800 | tf_op jit(solution)/shard_map/ppermute | solution.py:400
  41.5 3.1 %collective-permute-done.19.refs_3_ = bf16[32,512]{1,0:T(8,128)(2,1)S(1)} collective-permute-done((bf16[32,512]{1,0:T(8,128)(2,1)S(1)}, bf16[32,512]{1,0:T(8,128)(2,1)S(1)}, u32[]{:S(2)}, u32[]{:S(2)}) %collective-permute-start.19) | collective-permute-done | bytes 32800 | tf_op jit(solution)/shard_map/ppermute | solution.py:400
  45.3 2.7 %far.2.refs_13_ = bf16[32,512]{1,0:T(8,128)(2,1)S(1)} custom-call(s32[1]{0:T(128)} %bitcast.4.row_ref, s32[1,2]{1,0:T(1,128)S(1)} %copy-done.5, bf16[32,512]{1,0:T(8,128)(2,1)S(1)} %fusion.3.refs_0_, bf16[32,512]{1,0:T(8,128)(2,1)S(1)} %collective-permute-done.17.refs_1_, bf16[32,512]{1,0:T(8,128)(2,1)S(1)} %collective-permute-done.18.refs_2_, ...), custom_call_target="tpu_custom_call" | custom-call | flops 16777216 | bytes 2097152 | tf_op jit(solution)/shard_map/far/pallas_call | solution.py:251
  48.1 4.8 %collective-permute-done.20.refs_14_ = bf16[32,512]{1,0:T(8,128)(2,1)S(1)} collective-permute-done((bf16[32,512]{1,0:T(8,128)(2,1)S(1)}, bf16[32,512]{1,0:T(8,128)(2,1)S(1)}, u32[]{:S(2)}, u32[]{:S(2)}) %collective-permute-start.20) | collective-permute-done | bytes 32800 | tf_op jit(solution)/shard_map/ppermute | solution.py:400
  53.6 2.1 %collective-permute-start.10 = (bf16[640,256]{1,0:T(8,128)(2,1)}, bf16[640,256]{1,0:T(8,128)(2,1)S(1)}, u32[]{:S(2)}, u32[]{:S(2)}) collective-permute-start(bf16[640,256]{1,0:T(8,128)(2,1)} %collective-permute-done.9.refs_11_), channel_id=1, source_target_pairs={{0,2},{2,4},{4,6},{6,7},{7,5},{5,3},{3,1},{1,0},{8,10},{10,12},{12... | collective-permute-start | bytes 983048 | tf_op jit(solution)/shard_map/ppermute | solution.py:403
  57.0 3.2 %absorb.6 = (f32[1024,256]{1,0:T(8,128)S(1)}, f32[256,256]{1,0:T(8,128)S(1)}) custom-call(s32[1]{0:T(128)} %bitcast.me_ref.refs_0_, s32[1,8]{1,0:T(1,128)S(1)} %copy-done.2, s32[1]{0:T(128)S(6)} %copy.13.refs_2_, s32[1,4]{1,0:T(1,128)S(1)} %copy-done.4, bf16[8,1024,1024]{2,1,0:T(8,128)(2,1)} %bitcast.30, f32[4,256,256]{2,1,0:T(8,128)} %bitcast.38, ...), custom_call_target="tpu_custom_call" | custom-call | flops 536870912 | bytes 4194304 | tf_op jit(solution)/shard_map/absorb/pallas_call | solution.py:218
  60.1 1.2 collective-permute-start.7
  62.3 1.4 collective-permute-start.22
  63.7 6.5 %absorb.7 = (f32[1024,256]{1,0:T(8,128)S(1)}, f32[256,256]{1,0:T(8,128)S(1)}) custom-call(s32[1]{0:T(128)} %bitcast.me_ref.refs_0_, s32[1,8]{1,0:T(1,128)S(1)} %copy-done.2, s32[1]{0:T(128)S(6)} %copy.13.refs_2_, s32[1,4]{1,0:T(1,128)S(1)} %copy-done.4, bf16[8,1024,1024]{2,1,0:T(8,128)(2,1)} %bitcast.31, f32[4,256,256]{2,1,0:T(8,128)} %bitcast.39, ...), custom_call_target="tpu_custom_call" | custom-call | flops 2147483648 | bytes 16777216 | tf_op jit(solution)/shard_map/absorb/pallas_call | solution.py:218
  70.2 4.0 %absorb.8 = (f32[1024,256]{1,0:T(8,128)S(1)}, f32[256,256]{1,0:T(8,128)S(1)}) custom-call(s32[1]{0:T(128)} %bitcast.me_ref.refs_0_, s32[1,8]{1,0:T(1,128)S(1)} %copy-done.2, s32[1]{0:T(128)S(6)} %copy.13.refs_2_, s32[1,4]{1,0:T(1,128)S(1)} %copy-done.4, bf16[8,1024,1024]{2,1,0:T(8,128)(2,1)} %bitcast.32, f32[4,256,256]{2,1,0:T(8,128)} %bitcast.40, ...), custom_call_target="tpu_custom_call" | custom-call | flops 1073741824 | bytes 8388608 | tf_op jit(solution)/shard_map/absorb/pallas_call | solution.py:218
  74.3 5.9 %back.2 = (f32[1024,256]{1,0:T(8,128)}, bf16[640,256]{1,0:T(8,128)(2,1)S(1)}) custom-call(s32[1]{0:T(128)} %bitcast.me_ref.refs_0_, s32[1,8]{1,0:T(1,128)S(1)} %copy-done.2, s32[1]{0:T(128)S(6)} %copy.13.refs_2_, s32[1,4]{1,0:T(1,128)S(1)} %copy-done.4, s32[1]{0:T(128)S(6)} %copy.14.rank_ref.refs_4_, bf16[8,1024,1024]{2,1,0:T(8,128)(2,1)} %bitcast.33, ...), custom_call_target="tpu_custom_call" | custom-call | flops 1610612736 | bytes 6291456 | tf_op jit(solution)/shard_map/back/pallas_call | solution.py:338
  80.2 3.0 %front.3 = (bf16[640,256]{1,0:T(8,128)(2,1)S(1)}, bf16[128,512]{1,0:T(8,128)(2,1)S(1)}, f32[128,512]{1,0:T(8,128)S(1)}) custom-call(s32[1]{0:T(128)} %bitcast.me_ref.refs_0_, s32[1]{0:T(128)S(6)} %copy.14.rank_ref.refs_4_, f32[1024,256]{1,0:T(8,128)} %get-tuple-element.20.v_in, f32[1024,256]{1,0:T(8,128)} %refs_12_.3, f32[256,512]{1,0:T(8,128)} %bitcast.48), custom_call_target="tpu_custom_call" | custom-call | flops 402653184 | bytes 2097152 | tf_op jit(solution)/shard_map/front/pallas_call | solution.py:102
  83.3 1.4 collective-permute-start.27
  85.4 2.9 %collective-permute-done.37 = bf16[128,512]{1,0:T(8,128)(2,1)S(1)} collective-permute-done((bf16[128,512]{1,0:T(8,128)(2,1)S(1)}, bf16[128,512]{1,0:T(8,128)(2,1)S(1)}, u32[]{:S(2)}, u32[]{:S(2)}) %collective-permute-start.37) | collective-permute-done | bytes 131104 | tf_op jit(solution)/shard_map/ppermute | solution.py:400
  88.7 1.7 %collective-permute-start.31 = (bf16[640,256]{1,0:T(8,128)(2,1)S(1)}, bf16[640,256]{1,0:T(8,128)(2,1)S(1)}, u32[]{:S(2)}, u32[]{:S(2)}) collective-permute-start(bf16[640,256]{1,0:T(8,128)(2,1)S(1)} %get-tuple-element.33.refs_7_), channel_id=1, source_target_pairs={{0,2},{2,4},{4,6},{6,7},{7,5},{5,3},{3,1},{1,0},{8,10},{10,12},{12... | collective-permute-start | bytes 983048 | tf_op jit(solution)/shard_map/ppermute | solution.py:403
  90.7 2.8 %collective-permute-done.27.refs_9_ = bf16[640,256]{1,0:T(8,128)(2,1)S(1)} collective-permute-done((bf16[640,256]{1,0:T(8,128)(2,1)S(1)}, bf16[640,256]{1,0:T(8,128)(2,1)S(1)}, u32[]{:S(2)}, u32[]{:S(2)}) %collective-permute-start.27) | collective-permute-done | bytes 327712 | tf_op jit(solution)/shard_map/ppermute | solution.py:403
  93.5 1.1 collective-permute-start.28
  96.8 5.4 %collective-permute-done.31.refs_7_ = bf16[640,256]{1,0:T(8,128)(2,1)S(1)} collective-permute-done((bf16[640,256]{1,0:T(8,128)(2,1)S(1)}, bf16[640,256]{1,0:T(8,128)(2,1)S(1)}, u32[]{:S(2)}, u32[]{:S(2)}) %collective-permute-start.31) | collective-permute-done | bytes 327712 | tf_op jit(solution)/shard_map/ppermute | solution.py:403
  102.3 2.4 %collective-permute-start.32 = (bf16[640,256]{1,0:T(8,128)(2,1)S(1)}, bf16[640,256]{1,0:T(8,128)(2,1)S(1)}, u32[]{:S(2)}, u32[]{:S(2)}) collective-permute-start(bf16[640,256]{1,0:T(8,128)(2,1)S(1)} %collective-permute-done.31.refs_7_), channel_id=1, source_target_pairs={{0,2},{2,4},{4,6},{6,7},{7,5},{5,3},{3,1},{1,0},{8,10},{10,12},{12... | collective-permute-start | bytes 983048 | tf_op jit(solution)/shard_map/ppermute | solution.py:403
  104.7 4.2 %collective-permute-done.28.refs_13_ = bf16[640,256]{1,0:T(8,128)(2,1)S(1)} collective-permute-done((bf16[640,256]{1,0:T(8,128)(2,1)S(1)}, bf16[640,256]{1,0:T(8,128)(2,1)S(1)}, u32[]{:S(2)}, u32[]{:S(2)}) %collective-permute-start.28) | collective-permute-done | bytes 327712 | tf_op jit(solution)/shard_map/ppermute | solution.py:403
  109.7 2.4 %collective-permute-start.25 = (bf16[640,256]{1,0:T(8,128)(2,1)S(1)}, bf16[640,256]{1,0:T(8,128)(2,1)S(1)}, u32[]{:S(2)}, u32[]{:S(2)}) collective-permute-start(bf16[640,256]{1,0:T(8,128)(2,1)S(1)} %collective-permute-done.24.refs_10_), channel_id=1, source_target_pairs={{0,2},{2,4},{4,6},{6,7},{7,5},{5,3},{3,1},{1,0},{8,10},{10,12},{12... | collective-permute-start | bytes 983048 | tf_op jit(solution)/shard_map/ppermute | solution.py:403
  112.2 1.2 collective-permute-done.40.refs_1_
  114.3 3.1 %collective-permute-done.41.refs_2_ = bf16[32,512]{1,0:T(8,128)(2,1)S(1)} collective-permute-done((bf16[32,512]{1,0:T(8,128)(2,1)S(1)}, bf16[32,512]{1,0:T(8,128)(2,1)S(1)}, u32[]{:S(2)}, u32[]{:S(2)}) %collective-permute-start.41) | collective-permute-done | bytes 32800 | tf_op jit(solution)/shard_map/ppermute | solution.py:400
  117.3 3.3 %collective-permute-done.42.refs_3_ = bf16[32,512]{1,0:T(8,128)(2,1)S(1)} collective-permute-done((bf16[32,512]{1,0:T(8,128)(2,1)S(1)}, bf16[32,512]{1,0:T(8,128)(2,1)S(1)}, u32[]{:S(2)}, u32[]{:S(2)}) %collective-permute-start.42) | collective-permute-done | bytes 32800 | tf_op jit(solution)/shard_map/ppermute | solution.py:400
  120.7 2.7 %far.3.refs_13_ = bf16[32,512]{1,0:T(8,128)(2,1)S(1)} custom-call(s32[1]{0:T(128)} %bitcast.4.row_ref, s32[1,2]{1,0:T(1,128)S(1)} %copy-done.6, bf16[32,512]{1,0:T(8,128)(2,1)S(1)} %fusion.2.refs_0_, bf16[32,512]{1,0:T(8,128)(2,1)S(1)} %collective-permute-done.40.refs_1_, bf16[32,512]{1,0:T(8,128)(2,1)S(1)} %collective-permute-done.41.refs_2_, ...), custom_call_target="tpu_custom_call" | custom-call | flops 16777216 | bytes 2097152 | tf_op jit(solution)/shard_map/far/pallas_call | solution.py:251
  124.2 4.0 %collective-permute-done.43.refs_14_ = bf16[32,512]{1,0:T(8,128)(2,1)S(1)} collective-permute-done((bf16[32,512]{1,0:T(8,128)(2,1)S(1)}, bf16[32,512]{1,0:T(8,128)(2,1)S(1)}, u32[]{:S(2)}, u32[]{:S(2)}) %collective-permute-start.43) | collective-permute-done | bytes 32800 | tf_op jit(solution)/shard_map/ppermute | solution.py:400
  128.7 1.7 %collective-permute-start.33 = (bf16[640,256]{1,0:T(8,128)(2,1)S(1)}, bf16[640,256]{1,0:T(8,128)(2,1)S(1)}, u32[]{:S(2)}, u32[]{:S(2)}) collective-permute-start(bf16[640,256]{1,0:T(8,128)(2,1)S(1)} %collective-permute-done.32.refs_11_), channel_id=1, source_target_pairs={{0,2},{2,4},{4,6},{6,7},{7,5},{5,3},{3,1},{1,0},{8,10},{10,12},{12... | collective-permute-start | bytes 983048 | tf_op jit(solution)/shard_map/ppermute | solution.py:403
  130.7 3.2 %absorb.9 = (f32[1024,256]{1,0:T(8,128)S(1)}, f32[256,256]{1,0:T(8,128)S(1)}) custom-call(s32[1]{0:T(128)} %bitcast.me_ref.refs_0_, s32[1,8]{1,0:T(1,128)S(1)} %copy-done.3, s32[1]{0:T(128)S(6)} %copy.13.refs_2_, s32[1,4]{1,0:T(1,128)S(1)} %copy-done.4, bf16[8,1024,1024]{2,1,0:T(8,128)(2,1)} %bitcast.34, f32[4,256,256]{2,1,0:T(8,128)} %bitcast.42, ...), custom_call_target="tpu_custom_call" | custom-call | flops 536870912 | bytes 4194304 | tf_op jit(solution)/shard_map/absorb/pallas_call | solution.py:218
  133.9 1.4 collective-permute-start.30
  136.0 1.7 %collective-permute-start.45 = (bf16[128,512]{1,0:T(8,128)(2,1)S(1)}, bf16[128,512]{1,0:T(8,128)(2,1)S(1)}, u32[]{:S(2)}, u32[]{:S(2)}) collective-permute-start(bf16[128,512]{1,0:T(8,128)(2,1)S(1)} %pad_maximum_fusion.1), channel_id=1, source_target_pairs={{0,1},{1,0},{2,3},{3,2},{4,5},{5,4},{6,7},{7,6},{8,9},{9,8},{10,11... | collective-permute-start | bytes 393224 | tf_op jit(solution)/shard_map/ppermute | solution.py:400
  137.7 6.7 %absorb.10 = (f32[1024,256]{1,0:T(8,128)S(1)}, f32[256,256]{1,0:T(8,128)S(1)}) custom-call(s32[1]{0:T(128)} %bitcast.me_ref.refs_0_, s32[1,8]{1,0:T(1,128)S(1)} %copy-done.3, s32[1]{0:T(128)S(6)} %copy.13.refs_2_, s32[1,4]{1,0:T(1,128)S(1)} %copy-done.4, bf16[8,1024,1024]{2,1,0:T(8,128)(2,1)} %bitcast.35, f32[4,256,256]{2,1,0:T(8,128)} %bitcast.43, ...), custom_call_target="tpu_custom_call" | custom-call | flops 2147483648 | bytes 16777216 | tf_op jit(solution)/shard_map/absorb/pallas_call | solution.py:218
  144.4 4.0 %absorb.11 = (f32[1024,256]{1,0:T(8,128)S(1)}, f32[256,256]{1,0:T(8,128)S(1)}) custom-call(s32[1]{0:T(128)} %bitcast.me_ref.refs_0_, s32[1,8]{1,0:T(1,128)S(1)} %copy-done.3, s32[1]{0:T(128)S(6)} %copy.13.refs_2_, s32[1,4]{1,0:T(1,128)S(1)} %copy-done.4, bf16[8,1024,1024]{2,1,0:T(8,128)(2,1)} %bitcast.36, f32[4,256,256]{2,1,0:T(8,128)} %bitcast.44, ...), custom_call_target="tpu_custom_call" | custom-call | flops 1073741824 | bytes 8388608 | tf_op jit(solution)/shard_map/absorb/pallas_call | solution.py:218
  148.5 5.7 %back.3 = f32[1024,256]{1,0:T(8,128)} custom-call(s32[1]{0:T(128)} %bitcast.me_ref.refs_0_, s32[1,8]{1,0:T(1,128)S(1)} %copy-done.3, s32[1]{0:T(128)S(6)} %copy.13.refs_2_, s32[1,4]{1,0:T(1,128)S(1)} %copy-done.4, s32[1]{0:T(128)S(6)} %copy.14.rank_ref.refs_4_, bf16[8,1024,1024]{2,1,0:T(8,128)(2,1)} %bitcast.37, f32[4,256,256]{2,1,0:T(8,128)} %bitcast.45, ...), custom_call_target="tpu_custom_call" | custom-call | flops 1610612736 | bytes 6291456 | tf_op jit(solution)/shard_map/back/pallas_call | solution.py:338
  (85 shorter events, 14.5 us)
Async XLA Ops:
  4.3 51.4 %copy-start = (bf16[640,256]{1,0:T(8,128)(2,1)}, bf16[640,256]{1,0:T(8,128)(2,1)S(1)}, u32[]{:S(2)}) copy-start(bf16[640,256]{1,0:T(8,128)(2,1)S(1)} %get-tuple-element.22.refs_7_) | copy-start | bytes 983044
  4.3 5.3 %collective-permute-start.14 = (bf16[128,512]{1,0:T(8,128)(2,1)S(1)}, bf16[128,512]{1,0:T(8,128)(2,1)S(1)}, u32[]{:S(2)}, u32[]{:S(2)}) collective-permute-start(bf16[128,512]{1,0:T(8,128)(2,1)S(1)} %get-tuple-element.30), channel_id=1, source_target_pairs={{0,1},{1,0},{2,3},{3,2},{4,5},{5,4},{6,7},{7,6},{8,9},{9,8},{10,11... | collective-permute-start | bytes 393224 | tf_op jit(solution)/shard_map/ppermute | solution.py:400
  5.9 10.6 %collective-permute-start.4 = (bf16[640,256]{1,0:T(8,128)(2,1)S(1)}, bf16[640,256]{1,0:T(8,128)(2,1)S(1)}, u32[]{:S(2)}, u32[]{:S(2)}) collective-permute-start(bf16[640,256]{1,0:T(8,128)(2,1)S(1)} %get-tuple-element.22.refs_7_), channel_id=1, source_target_pairs={{2,0},{4,2},{6,4},{7,6},{5,7},{3,5},{1,3},{0,1},{10,8},{12,10},{14... | collective-permute-start | bytes 983048 | tf_op jit(solution)/shard_map/ppermute | solution.py:403
  7.4 10.6 %collective-permute-start = (bf16[640,256]{1,0:T(8,128)(2,1)S(1)}, bf16[640,256]{1,0:T(8,128)(2,1)S(1)}, u32[]{:S(2)}, u32[]{:S(2)}) collective-permute-start(bf16[640,256]{1,0:T(8,128)(2,1)S(1)} %slice.7.refs_6_), channel_id=1, source_target_pairs={{0,2},{2,4},{4,6},{6,7},{7,5},{5,3},{3,1},{1,0},{8,10},{10,12},{12... | collective-permute-start | bytes 983048 | tf_op jit(solution)/shard_map/ppermute | solution.py:403
  9.7 10.0 %collective-permute-start.15 = (bf16[64,512]{1,0:T(8,128)(2,1)S(1)}, bf16[64,512]{1,0:T(8,128)(2,1)S(1)}, u32[]{:S(2)}, u32[]{:S(2)}) collective-permute-start(bf16[64,512]{1,0:T(8,128)(2,1)S(1)} %fusion), channel_id=1, source_target_pairs={{0,2},{1,3},{2,0},{3,1},{4,6},{5,7},{6,4},{7,5},{8,10},{9,11},{10,... | collective-permute-start | bytes 196616 | tf_op jit(solution)/shard_map/ppermute | solution.py:400
  12.4 13.1 %collective-permute-start.8 = (bf16[640,256]{1,0:T(8,128)(2,1)S(1)}, bf16[640,256]{1,0:T(8,128)(2,1)S(1)}, u32[]{:S(2)}, u32[]{:S(2)}) collective-permute-start(bf16[640,256]{1,0:T(8,128)(2,1)S(1)} %get-tuple-element.22.refs_7_), channel_id=1, source_target_pairs={{0,2},{2,4},{4,6},{6,7},{7,5},{5,3},{3,1},{1,0},{8,10},{10,12},{12... | collective-permute-start | bytes 983048 | tf_op jit(solution)/shard_map/ppermute | solution.py:403
  12.5 15.6 %collective-permute-start.11 = (bf16[640,256]{1,0:T(8,128)(2,1)S(1)}, bf16[640,256]{1,0:T(8,128)(2,1)S(1)}, u32[]{:S(2)}, u32[]{:S(2)}) collective-permute-start(bf16[640,256]{1,0:T(8,128)(2,1)S(1)} %slice.7.refs_6_), channel_id=1, source_target_pairs={{2,0},{4,2},{6,4},{7,6},{5,7},{3,5},{1,3},{0,1},{10,8},{12,10},{14... | collective-permute-start | bytes 983048 | tf_op jit(solution)/shard_map/ppermute | solution.py:403
  16.4 15.4 %collective-permute-start.5 = (bf16[640,256]{1,0:T(8,128)(2,1)S(1)}, bf16[640,256]{1,0:T(8,128)(2,1)S(1)}, u32[]{:S(2)}, u32[]{:S(2)}) collective-permute-start(bf16[640,256]{1,0:T(8,128)(2,1)S(1)} %collective-permute-done.4.refs_9_), channel_id=1, source_target_pairs={{2,0},{4,2},{6,4},{7,6},{5,7},{3,5},{1,3},{0,1},{10,8},{12,10},{14... | collective-permute-start | bytes 983048 | tf_op jit(solution)/shard_map/ppermute | solution.py:403
  18.1 15.2 %collective-permute-start.1 = (bf16[640,256]{1,0:T(8,128)(2,1)S(1)}, bf16[640,256]{1,0:T(8,128)(2,1)S(1)}, u32[]{:S(2)}, u32[]{:S(2)}) collective-permute-start(bf16[640,256]{1,0:T(8,128)(2,1)S(1)} %collective-permute-done.refs_6_), channel_id=1, source_target_pairs={{0,2},{2,4},{4,6},{6,7},{7,5},{5,3},{3,1},{1,0},{8,10},{10,12},{12... | collective-permute-start | bytes 983048 | tf_op jit(solution)/shard_map/ppermute | solution.py:403
  19.7 16.1 %collective-permute-start.16 = (bf16[32,512]{1,0:T(8,128)(2,1)S(1)}, bf16[32,512]{1,0:T(8,128)(2,1)S(1)}, u32[]{:S(2)}, u32[]{:S(2)}) collective-permute-start(bf16[32,512]{1,0:T(8,128)(2,1)S(1)} %fusion.4), channel_id=1, source_target_pairs={{0,4},{1,5},{2,6},{3,7},{4,0},{5,1},{6,2},{7,3},{8,12},{9,13},{10,... | collective-permute-start | bytes 98312 | tf_op jit(solution)/shard_map/ppermute | solution.py:400
  25.6 28.0 %collective-permute-start.9 = (bf16[640,256]{1,0:T(8,128)(2,1)S(1)}, bf16[640,256]{1,0:T(8,128)(2,1)}, u32[]{:S(2)}, u32[]{:S(2)}) collective-permute-start(bf16[640,256]{1,0:T(8,128)(2,1)S(1)} %collective-permute-done.8.refs_7_), channel_id=1, source_target_pairs={{0,2},{2,4},{4,6},{6,7},{7,5},{5,3},{3,1},{1,0},{8,10},{10,12},{12... | collective-permute-start | bytes 983048 | tf_op jit(solution)/shard_map/ppermute | solution.py:403
  28.1 27.6 %collective-permute-start.12 = (bf16[640,256]{1,0:T(8,128)(2,1)S(1)}, bf16[640,256]{1,0:T(8,128)(2,1)}, u32[]{:S(2)}, u32[]{:S(2)}) collective-permute-start(bf16[640,256]{1,0:T(8,128)(2,1)S(1)} %collective-permute-done.11.refs_8_), channel_id=1, source_target_pairs={{2,0},{4,2},{6,4},{7,6},{5,7},{3,5},{1,3},{0,1},{10,8},{12,10},{14... | collective-permute-start | bytes 983048 | tf_op jit(solution)/shard_map/ppermute | solution.py:403
  31.9 28.2 %collective-permute-start.6 = (bf16[640,256]{1,0:T(8,128)(2,1)S(1)}, bf16[640,256]{1,0:T(8,128)(2,1)S(1)}, u32[]{:S(2)}, u32[]{:S(2)}) collective-permute-start(bf16[640,256]{1,0:T(8,128)(2,1)S(1)} %collective-permute-done.5.refs_13_), channel_id=1, source_target_pairs={{2,0},{4,2},{6,4},{7,6},{5,7},{3,5},{1,3},{0,1},{10,8},{12,10},{14... | collective-permute-start | bytes 983048 | tf_op jit(solution)/shard_map/ppermute | solution.py:403
  33.3 28.0 %collective-permute-start.2 = (bf16[640,256]{1,0:T(8,128)(2,1)S(1)}, bf16[640,256]{1,0:T(8,128)(2,1)S(1)}, u32[]{:S(2)}, u32[]{:S(2)}) collective-permute-start(bf16[640,256]{1,0:T(8,128)(2,1)S(1)} %collective-permute-done.1.refs_10_), channel_id=1, source_target_pairs={{0,2},{2,4},{4,6},{6,7},{7,5},{5,3},{3,1},{1,0},{8,10},{10,12},{12... | collective-permute-start | bytes 983048 | tf_op jit(solution)/shard_map/ppermute | solution.py:403
  35.8 1.3 collective-permute-start.17
  37.1 3.9 %collective-permute-start.18 = (bf16[32,512]{1,0:T(8,128)(2,1)S(1)}, bf16[32,512]{1,0:T(8,128)(2,1)S(1)}, u32[]{:S(2)}, u32[]{:S(2)}) collective-permute-start(bf16[32,512]{1,0:T(8,128)(2,1)S(1)} %fusion.3.refs_0_), channel_id=1, source_target_pairs={{0,16},{8,24},{16,0},{24,8},{1,17},{9,25},{17,1},{25,9},{2,18},{10... | collective-permute-start | bytes 98312 | tf_op jit(solution)/shard_map/ppermute | solution.py:400
  41.0 3.6 %collective-permute-start.19 = (bf16[32,512]{1,0:T(8,128)(2,1)S(1)}, bf16[32,512]{1,0:T(8,128)(2,1)S(1)}, u32[]{:S(2)}, u32[]{:S(2)}) collective-permute-start(bf16[32,512]{1,0:T(8,128)(2,1)S(1)} %fusion.3.refs_0_), channel_id=1, source_target_pairs={{0,24},{8,16},{16,8},{24,0},{1,25},{9,17},{17,9},{25,1},{2,26},{10... | collective-permute-start | bytes 98312 | tf_op jit(solution)/shard_map/ppermute | solution.py:400
  48.0 4.9 %collective-permute-start.20 = (bf16[32,512]{1,0:T(8,128)(2,1)S(1)}, bf16[32,512]{1,0:T(8,128)(2,1)S(1)}, u32[]{:S(2)}, u32[]{:S(2)}) collective-permute-start(bf16[32,512]{1,0:T(8,128)(2,1)S(1)} %far.2.refs_13_), channel_id=1, source_target_pairs={{0,4},{1,5},{2,6},{3,7},{4,0},{5,1},{6,2},{7,3},{8,12},{9,13},{10,... | collective-permute-start | bytes 98312 | tf_op jit(solution)/shard_map/ppermute | solution.py:400
  52.9 9.4 %collective-permute-start.21 = (bf16[64,512]{1,0:T(8,128)(2,1)S(1)}, bf16[64,512]{1,0:T(8,128)(2,1)S(1)}, u32[]{:S(2)}, u32[]{:S(2)}) collective-permute-start(bf16[64,512]{1,0:T(8,128)(2,1)S(1)} %pad_maximum_fusion.2), channel_id=1, source_target_pairs={{0,2},{1,3},{2,0},{3,1},{4,6},{5,7},{6,4},{7,5},{8,10},{9,11},{10,... | collective-permute-start | bytes 196616 | tf_op jit(solution)/shard_map/ppermute | solution.py:400
  53.6 16.7 %collective-permute-start.10 = (bf16[640,256]{1,0:T(8,128)(2,1)}, bf16[640,256]{1,0:T(8,128)(2,1)S(1)}, u32[]{:S(2)}, u32[]{:S(2)}) collective-permute-start(bf16[640,256]{1,0:T(8,128)(2,1)} %collective-permute-done.9.refs_11_), channel_id=1, source_target_pairs={{0,2},{2,4},{4,6},{6,7},{7,5},{5,3},{3,1},{1,0},{8,10},{10,12},{12... | collective-permute-start | bytes 983048 | tf_op jit(solution)/shard_map/ppermute | solution.py:403
  55.6 14.6 %collective-permute-start.13 = (bf16[640,256]{1,0:T(8,128)(2,1)}, bf16[640,256]{1,0:T(8,128)(2,1)S(1)}, u32[]{:S(2)}, u32[]{:S(2)}) collective-permute-start(bf16[640,256]{1,0:T(8,128)(2,1)} %collective-permute-done.12.refs_12_), channel_id=1, source_target_pairs={{2,0},{4,2},{6,4},{7,6},{5,7},{3,5},{1,3},{0,1},{10,8},{12,10},{14... | collective-permute-start | bytes 983048 | tf_op jit(solution)/shard_map/ppermute | solution.py:403
  60.1 14.2 %collective-permute-start.7 = (bf16[640,256]{1,0:T(8,128)(2,1)S(1)}, bf16[640,256]{1,0:T(8,128)(2,1)S(1)}, u32[]{:S(2)}, u32[]{:S(2)}) collective-permute-start(bf16[640,256]{1,0:T(8,128)(2,1)S(1)} %collective-permute-done.6.refs_9_), channel_id=1, source_target_pairs={{2,0},{4,2},{6,4},{7,6},{5,7},{3,5},{1,3},{0,1},{10,8},{12,10},{14... | collective-permute-start | bytes 983048 | tf_op jit(solution)/shard_map/ppermute | solution.py:403
  61.3 13.0 %collective-permute-start.3 = (bf16[640,256]{1,0:T(8,128)(2,1)S(1)}, bf16[640,256]{1,0:T(8,128)(2,1)S(1)}, u32[]{:S(2)}, u32[]{:S(2)}) collective-permute-start(bf16[640,256]{1,0:T(8,128)(2,1)S(1)} %collective-permute-done.2.refs_6_), channel_id=1, source_target_pairs={{0,2},{2,4},{4,6},{6,7},{7,5},{5,3},{3,1},{1,0},{8,10},{10,12},{12... | collective-permute-start | bytes 983048 | tf_op jit(solution)/shard_map/ppermute | solution.py:403
  62.3 12.0 %collective-permute-start.22 = (bf16[128,512]{1,0:T(8,128)(2,1)S(1)}, bf16[128,512]{1,0:T(8,128)(2,1)S(1)}, u32[]{:S(2)}, u32[]{:S(2)}) collective-permute-start(bf16[128,512]{1,0:T(8,128)(2,1)S(1)} %pad_maximum_fusion), channel_id=1, source_target_pairs={{0,1},{1,0},{2,3},{3,2},{4,5},{5,4},{6,7},{7,6},{8,9},{9,8},{10,11... | collective-permute-start | bytes 393224 | tf_op jit(solution)/shard_map/ppermute | solution.py:400
  74.3 56.4 %copy-start.3 = (s32[1,8]{1,0:T(1,128)S(1)}, s32[1,8]{1,0:T(1,128)}, u32[]{:S(2)}) copy-start(s32[1,8]{1,0:T(1,128)} %refs_1_.15) | copy-start | bytes 100
  83.2 5.0 %collective-permute-start.37 = (bf16[128,512]{1,0:T(8,128)(2,1)S(1)}, bf16[128,512]{1,0:T(8,128)(2,1)S(1)}, u32[]{:S(2)}, u32[]{:S(2)}) collective-permute-start(bf16[128,512]{1,0:T(8,128)(2,1)S(1)} %get-tuple-element.41), channel_id=1, source_target_pairs={{0,1},{1,0},{2,3},{3,2},{4,5},{5,4},{6,7},{7,6},{8,9},{9,8},{10,11... | collective-permute-start | bytes 393224 | tf_op jit(solution)/shard_map/ppermute | solution.py:400
  83.3 10.2 %collective-permute-start.27 = (bf16[640,256]{1,0:T(8,128)(2,1)S(1)}, bf16[640,256]{1,0:T(8,128)(2,1)S(1)}, u32[]{:S(2)}, u32[]{:S(2)}) collective-permute-start(bf16[640,256]{1,0:T(8,128)(2,1)S(1)} %get-tuple-element.33.refs_7_), channel_id=1, source_target_pairs={{2,0},{4,2},{6,4},{7,6},{5,7},{3,5},{1,3},{0,1},{10,8},{12,10},{14... | collective-permute-start | bytes 983048 | tf_op jit(solution)/shard_map/ppermute | solution.py:403
  84.7 10.6 %collective-permute-start.23 = (bf16[640,256]{1,0:T(8,128)(2,1)S(1)}, bf16[640,256]{1,0:T(8,128)(2,1)S(1)}, u32[]{:S(2)}, u32[]{:S(2)}) collective-permute-start(bf16[640,256]{1,0:T(8,128)(2,1)S(1)} %get-tuple-element.32.refs_6_), channel_id=1, source_target_pairs={{0,2},{2,4},{4,6},{6,7},{7,5},{5,3},{3,1},{1,0},{8,10},{10,12},{12... | collective-permute-start | bytes 983048 | tf_op jit(solution)/shard_map/ppermute | solution.py:403
  88.3 7.6 %collective-permute-start.38 = (bf16[64,512]{1,0:T(8,128)(2,1)S(1)}, bf16[64,512]{1,0:T(8,128)(2,1)S(1)}, u32[]{:S(2)}, u32[]{:S(2)}) collective-permute-start(bf16[64,512]{1,0:T(8,128)(2,1)S(1)} %fusion.1), channel_id=1, source_target_pairs={{0,2},{1,3},{2,0},{3,1},{4,6},{5,7},{6,4},{7,5},{8,10},{9,11},{10,... | collective-permute-start | bytes 196616 | tf_op jit(solution)/shard_map/ppermute | solution.py:400
  88.7 13.6 %collective-permute-start.31 = (bf16[640,256]{1,0:T(8,128)(2,1)S(1)}, bf16[640,256]{1,0:T(8,128)(2,1)S(1)}, u32[]{:S(2)}, u32[]{:S(2)}) collective-permute-start(bf16[640,256]{1,0:T(8,128)(2,1)S(1)} %get-tuple-element.33.refs_7_), channel_id=1, source_target_pairs={{0,2},{2,4},{4,6},{6,7},{7,5},{5,3},{3,1},{1,0},{8,10},{10,12},{12... | collective-permute-start | bytes 983048 | tf_op jit(solution)/shard_map/ppermute | solution.py:403
  90.4 14.3 %collective-permute-start.34 = (bf16[640,256]{1,0:T(8,128)(2,1)S(1)}, bf16[640,256]{1,0:T(8,128)(2,1)S(1)}, u32[]{:S(2)}, u32[]{:S(2)}) collective-permute-start(bf16[640,256]{1,0:T(8,128)(2,1)S(1)} %get-tuple-element.32.refs_6_), channel_id=1, source_target_pairs={{2,0},{4,2},{6,4},{7,6},{5,7},{3,5},{1,3},{0,1},{10,8},{12,10},{14... | collective-permute-start | bytes 983048 | tf_op jit(solution)/shard_map/ppermute | solution.py:403
  93.5 15.4 %collective-permute-start.28 = (bf16[640,256]{1,0:T(8,128)(2,1)S(1)}, bf16[640,256]{1,0:T(8,128)(2,1)S(1)}, u32[]{:S(2)}, u32[]{:S(2)}) collective-permute-start(bf16[640,256]{1,0:T(8,128)(2,1)S(1)} %collective-permute-done.27.refs_9_), channel_id=1, source_target_pairs={{2,0},{4,2},{6,4},{7,6},{5,7},{3,5},{1,3},{0,1},{10,8},{12,10},{14... | collective-permute-start | bytes 983048 | tf_op jit(solution)/shard_map/ppermute | solution.py:403
  95.3 14.4 %collective-permute-start.24 = (bf16[640,256]{1,0:T(8,128)(2,1)S(1)}, bf16[640,256]{1,0:T(8,128)(2,1)S(1)}, u32[]{:S(2)}, u32[]{:S(2)}) collective-permute-start(bf16[640,256]{1,0:T(8,128)(2,1)S(1)} %collective-permute-done.23.refs_6_), channel_id=1, source_target_pairs={{0,2},{2,4},{4,6},{6,7},{7,5},{5,3},{3,1},{1,0},{8,10},{10,12},{12... | collective-permute-start | bytes 983048 | tf_op jit(solution)/shard_map/ppermute | solution.py:403
  96.0 16.1 %collective-permute-start.39 = (bf16[32,512]{1,0:T(8,128)(2,1)S(1)}, bf16[32,512]{1,0:T(8,128)(2,1)S(1)}, u32[]{:S(2)}, u32[]{:S(2)}) collective-permute-start(bf16[32,512]{1,0:T(8,128)(2,1)S(1)} %fusion.5), channel_id=1, source_target_pairs={{0,4},{1,5},{2,6},{3,7},{4,0},{5,1},{6,2},{7,3},{8,12},{9,13},{10,... | collective-permute-start | bytes 98312 | tf_op jit(solution)/shard_map/ppermute | solution.py:400
  102.3 26.4 %collective-permute-start.32 = (bf16[640,256]{1,0:T(8,128)(2,1)S(1)}, bf16[640,256]{1,0:T(8,128)(2,1)S(1)}, u32[]{:S(2)}, u32[]{:S(2)}) collective-permute-start(bf16[640,256]{1,0:T(8,128)(2,1)S(1)} %collective-permute-done.31.refs_7_), channel_id=1, source_target_pairs={{0,2},{2,4},{4,6},{6,7},{7,5},{5,3},{3,1},{1,0},{8,10},{10,12},{12... | collective-permute-start | bytes 983048 | tf_op jit(solution)/shard_map/ppermute | solution.py:403
  104.7 25.6 %collective-permute-start.35 = (bf16[640,256]{1,0:T(8,128)(2,1)S(1)}, bf16[640,256]{1,0:T(8,128)(2,1)S(1)}, u32[]{:S(2)}, u32[]{:S(2)}) collective-permute-start(bf16[640,256]{1,0:T(8,128)(2,1)S(1)} %collective-permute-done.34.refs_8_), channel_id=1, source_target_pairs={{2,0},{4,2},{6,4},{7,6},{5,7},{3,5},{1,3},{0,1},{10,8},{12,10},{14... | collective-permute-start | bytes 983048 | tf_op jit(solution)/shard_map/ppermute | solution.py:403
  109.0 24.9 %collective-permute-start.29 = (bf16[640,256]{1,0:T(8,128)(2,1)S(1)}, bf16[640,256]{1,0:T(8,128)(2,1)S(1)}, u32[]{:S(2)}, u32[]{:S(2)}) collective-permute-start(bf16[640,256]{1,0:T(8,128)(2,1)S(1)} %collective-permute-done.28.refs_13_), channel_id=1, source_target_pairs={{2,0},{4,2},{6,4},{7,6},{5,7},{3,5},{1,3},{0,1},{10,8},{12,10},{14... | collective-permute-start | bytes 983048 | tf_op jit(solution)/shard_map/ppermute | solution.py:403
  109.7 25.6 %collective-permute-start.25 = (bf16[640,256]{1,0:T(8,128)(2,1)S(1)}, bf16[640,256]{1,0:T(8,128)(2,1)S(1)}, u32[]{:S(2)}, u32[]{:S(2)}) collective-permute-start(bf16[640,256]{1,0:T(8,128)(2,1)S(1)} %collective-permute-done.24.refs_10_), channel_id=1, source_target_pairs={{0,2},{2,4},{4,6},{6,7},{7,5},{5,3},{3,1},{1,0},{8,10},{10,12},{12... | collective-permute-start | bytes 983048 | tf_op jit(solution)/shard_map/ppermute | solution.py:403
  112.1 1.3 collective-permute-start.40
  113.4 3.9 %collective-permute-start.41 = (bf16[32,512]{1,0:T(8,128)(2,1)S(1)}, bf16[32,512]{1,0:T(8,128)(2,1)S(1)}, u32[]{:S(2)}, u32[]{:S(2)}) collective-permute-start(bf16[32,512]{1,0:T(8,128)(2,1)S(1)} %fusion.2.refs_0_), channel_id=1, source_target_pairs={{0,16},{8,24},{16,0},{24,8},{1,17},{9,25},{17,1},{25,9},{2,18},{10... | collective-permute-start | bytes 98312 | tf_op jit(solution)/shard_map/ppermute | solution.py:400
  117.3 3.3 %collective-permute-start.42 = (bf16[32,512]{1,0:T(8,128)(2,1)S(1)}, bf16[32,512]{1,0:T(8,128)(2,1)S(1)}, u32[]{:S(2)}, u32[]{:S(2)}) collective-permute-start(bf16[32,512]{1,0:T(8,128)(2,1)S(1)} %fusion.2.refs_0_), channel_id=1, source_target_pairs={{0,24},{8,16},{16,8},{24,0},{1,25},{9,17},{17,9},{25,1},{2,26},{10... | collective-permute-start | bytes 98312 | tf_op jit(solution)/shard_map/ppermute | solution.py:400
  123.4 4.9 %collective-permute-start.43 = (bf16[32,512]{1,0:T(8,128)(2,1)S(1)}, bf16[32,512]{1,0:T(8,128)(2,1)S(1)}, u32[]{:S(2)}, u32[]{:S(2)}) collective-permute-start(bf16[32,512]{1,0:T(8,128)(2,1)S(1)} %far.3.refs_13_), channel_id=1, source_target_pairs={{0,4},{1,5},{2,6},{3,7},{4,0},{5,1},{6,2},{7,3},{8,12},{9,13},{10,... | collective-permute-start | bytes 98312 | tf_op jit(solution)/shard_map/ppermute | solution.py:400
  128.3 7.7 %collective-permute-start.44 = (bf16[64,512]{1,0:T(8,128)(2,1)S(1)}, bf16[64,512]{1,0:T(8,128)(2,1)S(1)}, u32[]{:S(2)}, u32[]{:S(2)}) collective-permute-start(bf16[64,512]{1,0:T(8,128)(2,1)S(1)} %pad_maximum_fusion.3), channel_id=1, source_target_pairs={{0,2},{1,3},{2,0},{3,1},{4,6},{5,7},{6,4},{7,5},{8,10},{9,11},{10,... | collective-permute-start | bytes 196616 | tf_op jit(solution)/shard_map/ppermute | solution.py:400
  128.7 15.8 %collective-permute-start.33 = (bf16[640,256]{1,0:T(8,128)(2,1)S(1)}, bf16[640,256]{1,0:T(8,128)(2,1)S(1)}, u32[]{:S(2)}, u32[]{:S(2)}) collective-permute-start(bf16[640,256]{1,0:T(8,128)(2,1)S(1)} %collective-permute-done.32.refs_11_), channel_id=1, source_target_pairs={{0,2},{2,4},{4,6},{6,7},{7,5},{5,3},{3,1},{1,0},{8,10},{10,12},{12... | collective-permute-start | bytes 983048 | tf_op jit(solution)/shard_map/ppermute | solution.py:403
  130.3 14.1 %collective-permute-start.36 = (bf16[640,256]{1,0:T(8,128)(2,1)S(1)}, bf16[640,256]{1,0:T(8,128)(2,1)S(1)}, u32[]{:S(2)}, u32[]{:S(2)}) collective-permute-start(bf16[640,256]{1,0:T(8,128)(2,1)S(1)} %collective-permute-done.35.refs_12_), channel_id=1, source_target_pairs={{2,0},{4,2},{6,4},{7,6},{5,7},{3,5},{1,3},{0,1},{10,8},{12,10},{14... | collective-permute-start | bytes 983048 | tf_op jit(solution)/shard_map/ppermute | solution.py:403
  133.9 14.6 %collective-permute-start.30 = (bf16[640,256]{1,0:T(8,128)(2,1)S(1)}, bf16[640,256]{1,0:T(8,128)(2,1)S(1)}, u32[]{:S(2)}, u32[]{:S(2)}) collective-permute-start(bf16[640,256]{1,0:T(8,128)(2,1)S(1)} %collective-permute-done.29.refs_9_), channel_id=1, source_target_pairs={{2,0},{4,2},{6,4},{7,6},{5,7},{3,5},{1,3},{0,1},{10,8},{12,10},{14... | collective-permute-start | bytes 983048 | tf_op jit(solution)/shard_map/ppermute | solution.py:403
  135.3 13.2 %collective-permute-start.26 = (bf16[640,256]{1,0:T(8,128)(2,1)S(1)}, bf16[640,256]{1,0:T(8,128)(2,1)S(1)}, u32[]{:S(2)}, u32[]{:S(2)}) collective-permute-start(bf16[640,256]{1,0:T(8,128)(2,1)S(1)} %collective-permute-done.25.refs_6_), channel_id=1, source_target_pairs={{0,2},{2,4},{4,6},{6,7},{7,5},{5,3},{3,1},{1,0},{8,10},{10,12},{12... | collective-permute-start | bytes 983048 | tf_op jit(solution)/shard_map/ppermute | solution.py:403
  136.0 12.5 %collective-permute-start.45 = (bf16[128,512]{1,0:T(8,128)(2,1)S(1)}, bf16[128,512]{1,0:T(8,128)(2,1)S(1)}, u32[]{:S(2)}, u32[]{:S(2)}) collective-permute-start(bf16[128,512]{1,0:T(8,128)(2,1)S(1)} %pad_maximum_fusion.1), channel_id=1, source_target_pairs={{0,1},{1,0},{2,3},{3,2},{4,5},{5,4},{6,7},{7,6},{8,9},{9,8},{10,11... | collective-permute-start | bytes 393224 | tf_op jit(solution)/shard_map/ppermute | solution.py:400
  (5 other events, 95.9 us)

commit v4 on v3

--- a/solution.py
+++ b/solution.py
@@ -151,7 +151,7 @@
         live, slot, linked, link = named(*tables, first + j, n)
         got = [copies.start(parts[2 * j + c], held_ref.at[at, rows[c]]) for c in (0, 1)]
         block = copies.start(blocks_ref.at[slot], block_ref.at[at], live)
-        tie = copies.start(links_ref.at[link], link_ref.at[at], linked)
+        tie = coupled_ref is not None and copies.start(links_ref.at[link], link_ref.at[at], linked)
         return live, linked, got, block, tie
 
     fetched = [fetch(j) for j in range(min(count, DEPTH - 1))]
@@ -169,6 +169,9 @@
         @pl.when(live)
         def _():
             near_ref[...] += contract(block_ref[at], held_ref[at, :leaf_rows, :], NN)
+
+        if coupled_ref is None:
+            continue
 
         @pl.when(linked)
         def _():
@@ -195,7 +198,9 @@
 
     def body(*refs):
         tables_in, blocks_ref, links_ref, refs = refs[:4], refs[4], refs[5], refs[6:]
-        near_out, coupled_out, *held, sems = refs[len(operands) :]
+        near_out, *rest = refs[len(operands) :]
+        coupled_out = rest.pop(0) if sums else None
+        *held, sems = rest
         copies = Copies(sems)
         base = [
             copies.start(given, out)
@@ -206,20 +211,20 @@
             near_out, coupled_out,
         )
         next(work)
-        if sums:
-            for copy in base:
-                copy.wait()
-        else:
+        for copy in base:
+            copy.wait()
+        if len(sums) < 1:
             near_out[...] = jnp.zeros_like(near_out)
+        elif len(sums) < 2:
             coupled_out[...] = jnp.zeros_like(coupled_out)
         for _ in work:
             pass
 
     return pl.pallas_call(
         body,
-        out_shape=outs,
+        out_shape=outs if sums else outs[:1],
         in_specs=[SMEM] * 4 + [HBM] * 2 + [ANY] * len(operands),
-        out_specs=(VMEM, VMEM),
+        out_specs=(VMEM, VMEM) if sums else (VMEM,),
         scratch_shapes=held_scratch(blocks, links, messages[0])
         + [pltpu.SemaphoreType.DMA((4 * count + 2,))],
         cost_estimate=cost(2 * count * (blocks.shape[1] ** 2) * probe_cols, 4 * count * (blocks.shape[1] ** 2)),
@@ -394,7 +399,7 @@
     steps = n // 2 - 1
 
     mine = jnp.reshape(me, (1,))
-    tables = (mine, near_leaves, near_count, leaf_links)
+    tables = (mine, keep(near_leaves), near_count, keep(leaf_links))
 
     def swap(value, axis, size, distance):
         return lax.ppermute(value, axis, [(i, i ^ distance) for i in range(size)])

time: 156 us -> 156 us (level)
  starting transfers between devices: 44.1 us -> 46.6 us
  waiting for transfers between devices: 53.9 us -> 51.4 us
    ppermute x28, waiting for transfers between devices: 27.3 us -> 24.9 us  [pass_on(): return lax.ppermute(value, 'col', perm)]
  transfers between devices with their start and end apart: 46 -> 46, of which waited for: 20 -> 19; matrix products, arithmetic and copies ran while one was open for 1% -> 1% of each run, Pallas kernels for 21% -> 22%
where the time goes in v4:
time: 156 us; the launch traced here: 154 us
  Pallas kernels  51.4 us (33%)
  waiting for transfers between devices  51.4 us (33%)
  starting transfers between devices  46.6 us (30%)
  between operations  2.45 us (2%)
  local copies, waits for them, and re-layouts  1.87 us (1%)
    ppermute x28, starting transfers between devices, pass_on(): return lax.ppermute(value, 'col', perm)  31.8 us
    pallas_call x6, Pallas kernels, absorb(): pl.pallas_call(body, out_shape=outs if sums else outs[:1], in_specs=[SMEM...  28.1 us
    ppermute x18, waiting for transfers between devices, swap(): return lax.ppermute(value, axis, [(i, i ^ distance) for i in range(size)])  26.5 us
    ppermute x28, waiting for transfers between devices, pass_on(): return lax.ppermute(value, 'col', perm)  24.9 us
    ppermute x18, starting transfers between devices, swap(): return lax.ppermute(value, axis, [(i, i ^ distance) for i in range(size)])  14.8 us
    pallas_call x2, Pallas kernels, back(): pl.pallas_call(body, out_shape=outs, in_specs=[SMEM] * 5 + [HBM] * 2 + [A...  11.8 us
    pallas_call x2, Pallas kernels, front(): pl.pallas_call(body, out_shape=(jax.ShapeDtypeStruct((leaf_rows + rank_co...  6 us
    pallas_call x2, Pallas kernels, far_share(): pl.pallas_call(body, out_shape=jax.ShapeDtypeStruct(parents[0].shape, BF1...  5.47 us
  transfers between devices with their start and end apart: 46, of which 19 were waited for; matrix products, arithmetic and copies ran while one was open for 1% of the time, Pallas kernels for 22%

profile of v4, /device:TPU:16, one launch (start us, length us, event | category | flops | bytes accessed | tf_op | source)
XLA Modules:
  0.0 153.8 jit_solution(3375309182686072860)
XLA Ops:
  1.3 3.0 %front.2 = (bf16[640,256]{1,0:T(8,128)(2,1)S(1)}, bf16[128,512]{1,0:T(8,128)(2,1)S(1)}, f32[128,512]{1,0:T(8,128)S(1)}) custom-call(s32[1]{0:T(128)} %bitcast.me_ref.refs_0_, s32[1]{0:T(128)S(6)} %copy.14.rank_ref.refs_4_, f32[1024,256]{1,0:T(8,128)} %refs_17_.1, f32[1024,256]{1,0:T(8,128)} %refs_12_.3, f32[256,512]{1,0:T(8,128)} %bitcast.46), custom_call_target="tpu_custom_call" | custom-call | flops 402653184 | bytes 2097152 | tf_op jit(solution)/shard_map/front/pallas_call | solution.py:102
  4.3 1.6 %collective-permute-start.14 = (bf16[128,512]{1,0:T(8,128)(2,1)S(1)}, bf16[128,512]{1,0:T(8,128)(2,1)S(1)}, u32[]{:S(2)}, u32[]{:S(2)}) collective-permute-start(bf16[128,512]{1,0:T(8,128)(2,1)S(1)} %get-tuple-element.24), channel_id=1, source_target_pairs={{0,1},{1,0},{2,3},{3,2},{4,5},{5,4},{6,7},{7,6},{8,9},{9,8},{10,11... | collective-permute-start | bytes 393224 | tf_op jit(solution)/shard_map/ppermute | solution.py:405
  7.4 1.6 %collective-permute-start = (bf16[640,256]{1,0:T(8,128)(2,1)S(1)}, bf16[640,256]{1,0:T(8,128)(2,1)S(1)}, u32[]{:S(2)}, u32[]{:S(2)}) collective-permute-start(bf16[640,256]{1,0:T(8,128)(2,1)S(1)} %slice.7.refs_6_), channel_id=1, source_target_pairs={{0,2},{2,4},{4,6},{6,7},{7,5},{5,3},{3,1},{1,0},{8,10},{10,12},{12... | collective-permute-start | bytes 983048 | tf_op jit(solution)/shard_map/ppermute | solution.py:408
  9.7 2.8 %collective-permute-start.15 = (bf16[64,512]{1,0:T(8,128)(2,1)S(1)}, bf16[64,512]{1,0:T(8,128)(2,1)S(1)}, u32[]{:S(2)}, u32[]{:S(2)}) collective-permute-start(bf16[64,512]{1,0:T(8,128)(2,1)S(1)} %fusion), channel_id=1, source_target_pairs={{0,2},{1,3},{2,0},{3,1},{4,6},{5,7},{6,4},{7,5},{8,10},{9,11},{10,... | collective-permute-start | bytes 196616 | tf_op jit(solution)/shard_map/ppermute | solution.py:405
  12.5 2.0 %collective-permute-start.11 = (bf16[640,256]{1,0:T(8,128)(2,1)S(1)}, bf16[640,256]{1,0:T(8,128)(2,1)S(1)}, u32[]{:S(2)}, u32[]{:S(2)}) collective-permute-start(bf16[640,256]{1,0:T(8,128)(2,1)S(1)} %slice.7.refs_6_), channel_id=1, source_target_pairs={{2,0},{4,2},{6,4},{7,6},{5,7},{3,5},{1,3},{0,1},{10,8},{12,10},{14... | collective-permute-start | bytes 983048 | tf_op jit(solution)/shard_map/ppermute | solution.py:408
  14.5 2.0 %collective-permute-done.4.refs_9_ = bf16[640,256]{1,0:T(8,128)(2,1)S(1)} collective-permute-done((bf16[640,256]{1,0:T(8,128)(2,1)S(1)}, bf16[640,256]{1,0:T(8,128)(2,1)S(1)}, u32[]{:S(2)}, u32[]{:S(2)}) %collective-permute-start.4) | collective-permute-done | bytes 327712 | tf_op jit(solution)/shard_map/ppermute | solution.py:408
  16.6 1.5 collective-permute-done.refs_6_
  18.1 1.6 %collective-permute-start.1 = (bf16[640,256]{1,0:T(8,128)(2,1)S(1)}, bf16[640,256]{1,0:T(8,128)(2,1)S(1)}, u32[]{:S(2)}, u32[]{:S(2)}) collective-permute-start(bf16[640,256]{1,0:T(8,128)(2,1)S(1)} %collective-permute-done.refs_6_), channel_id=1, source_target_pairs={{0,2},{2,4},{4,6},{6,7},{7,5},{5,3},{3,1},{1,0},{8,10},{10,12},{12... | collective-permute-start | bytes 983048 | tf_op jit(solution)/shard_map/ppermute | solution.py:408
  20.1 5.5 %collective-permute-done.8.refs_7_ = bf16[640,256]{1,0:T(8,128)(2,1)S(1)} collective-permute-done((bf16[640,256]{1,0:T(8,128)(2,1)S(1)}, bf16[640,256]{1,0:T(8,128)(2,1)S(1)}, u32[]{:S(2)}, u32[]{:S(2)}) %collective-permute-start.8) | collective-permute-done | bytes 327712 | tf_op jit(solution)/shard_map/ppermute | solution.py:408
  25.6 2.5 %collective-permute-start.9 = (bf16[640,256]{1,0:T(8,128)(2,1)S(1)}, bf16[640,256]{1,0:T(8,128)(2,1)}, u32[]{:S(2)}, u32[]{:S(2)}) collective-permute-start(bf16[640,256]{1,0:T(8,128)(2,1)S(1)} %collective-permute-done.8.refs_7_), channel_id=1, source_target_pairs={{0,2},{2,4},{4,6},{6,7},{7,5},{5,3},{3,1},{1,0},{8,10},{10,12},{12... | collective-permute-start | bytes 983048 | tf_op jit(solution)/shard_map/ppermute | solution.py:408
  28.1 3.8 %collective-permute-done.5.refs_13_ = bf16[640,256]{1,0:T(8,128)(2,1)S(1)} collective-permute-done((bf16[640,256]{1,0:T(8,128)(2,1)S(1)}, bf16[640,256]{1,0:T(8,128)(2,1)S(1)}, u32[]{:S(2)}, u32[]{:S(2)}) %collective-permute-start.5) | collective-permute-done | bytes 327712 | tf_op jit(solution)/shard_map/ppermute | solution.py:408
  33.3 2.5 %collective-permute-start.2 = (bf16[640,256]{1,0:T(8,128)(2,1)S(1)}, bf16[640,256]{1,0:T(8,128)(2,1)S(1)}, u32[]{:S(2)}, u32[]{:S(2)}) collective-permute-start(bf16[640,256]{1,0:T(8,128)(2,1)S(1)} %collective-permute-done.1.refs_10_), channel_id=1, source_target_pairs={{0,2},{2,4},{4,6},{6,7},{7,5},{5,3},{3,1},{1,0},{8,10},{10,12},{12... | collective-permute-start | bytes 983048 | tf_op jit(solution)/shard_map/ppermute | solution.py:408
  35.9 1.2 collective-permute-done.17.refs_1_
  37.1 1.5 collective-permute-start.18
  38.6 2.4 %collective-permute-done.18.refs_2_ = bf16[32,512]{1,0:T(8,128)(2,1)S(1)} collective-permute-done((bf16[32,512]{1,0:T(8,128)(2,1)S(1)}, bf16[32,512]{1,0:T(8,128)(2,1)S(1)}, u32[]{:S(2)}, u32[]{:S(2)}) %collective-permute-start.18) | collective-permute-done | bytes 32800 | tf_op jit(solution)/shard_map/ppermute | solution.py:405
  41.5 3.1 %collective-permute-done.19.refs_3_ = bf16[32,512]{1,0:T(8,128)(2,1)S(1)} collective-permute-done((bf16[32,512]{1,0:T(8,128)(2,1)S(1)}, bf16[32,512]{1,0:T(8,128)(2,1)S(1)}, u32[]{:S(2)}, u32[]{:S(2)}) %collective-permute-start.19) | collective-permute-done | bytes 32800 | tf_op jit(solution)/shard_map/ppermute | solution.py:405
  45.3 2.7 %far.2.refs_13_ = bf16[32,512]{1,0:T(8,128)(2,1)S(1)} custom-call(s32[1]{0:T(128)} %bitcast.4.row_ref, s32[1,2]{1,0:T(1,128)S(1)} %copy-done.2, bf16[32,512]{1,0:T(8,128)(2,1)S(1)} %fusion.3.refs_0_, bf16[32,512]{1,0:T(8,128)(2,1)S(1)} %collective-permute-done.17.refs_1_, bf16[32,512]{1,0:T(8,128)(2,1)S(1)} %collective-permute-done.18.refs_2_, ...), custom_call_target="tpu_custom_call" | custom-call | flops 16777216 | bytes 2097152 | tf_op jit(solution)/shard_map/far/pallas_call | solution.py:256
  48.1 4.8 %collective-permute-done.20.refs_14_ = bf16[32,512]{1,0:T(8,128)(2,1)S(1)} collective-permute-done((bf16[32,512]{1,0:T(8,128)(2,1)S(1)}, bf16[32,512]{1,0:T(8,128)(2,1)S(1)}, u32[]{:S(2)}, u32[]{:S(2)}) %collective-permute-start.20) | collective-permute-done | bytes 32800 | tf_op jit(solution)/shard_map/ppermute | solution.py:405
  53.6 2.1 %collective-permute-start.10 = (bf16[640,256]{1,0:T(8,128)(2,1)}, bf16[640,256]{1,0:T(8,128)(2,1)S(1)}, u32[]{:S(2)}, u32[]{:S(2)}) collective-permute-start(bf16[640,256]{1,0:T(8,128)(2,1)} %collective-permute-done.9.refs_11_), channel_id=1, source_target_pairs={{0,2},{2,4},{4,6},{6,7},{7,5},{5,3},{3,1},{1,0},{8,10},{10,12},{12... | collective-permute-start | bytes 983048 | tf_op jit(solution)/shard_map/ppermute | solution.py:408
  55.6 3.3 %absorb.6.refs_14_ = f32[1024,256]{1,0:T(8,128)S(1)} custom-call(s32[1]{0:T(128)} %bitcast.me_ref.refs_0_, s32[1,8]{1,0:T(1,128)} %refs_1_.15, s32[1]{0:T(128)S(6)} %copy.13.refs_2_, s32[1,4]{1,0:T(1,128)} %refs_3_.15, bf16[8,1024,1024]{2,1,0:T(8,128)(2,1)} %bitcast.30, f32[4,256,256]{2,1,0:T(8,128)} %bitcast.38, bf16[640,256]{1,0:T(8,128)(2,1)S(1)} %slice.7.refs_6_, ...), custom_call_target="tpu_custom_call" | custom-call | flops 536870912 | bytes 4194304 | tf_op jit(solution)/shard_map/absorb/pallas_call | solution.py:223
  58.9 1.2 collective-permute-start.7
  61.1 1.4 collective-permute-start.22
  62.5 6.5 %absorb.7 = (f32[1024,256]{1,0:T(8,128)S(1)}, f32[256,256]{1,0:T(8,128)S(1)}) custom-call(s32[1]{0:T(128)} %bitcast.me_ref.refs_0_, s32[1,8]{1,0:T(1,128)} %refs_1_.15, s32[1]{0:T(128)S(6)} %copy.13.refs_2_, s32[1,4]{1,0:T(1,128)} %refs_3_.15, bf16[8,1024,1024]{2,1,0:T(8,128)(2,1)} %bitcast.31, f32[4,256,256]{2,1,0:T(8,128)} %bitcast.39, ...), custom_call_target="tpu_custom_call" | custom-call | flops 2147483648 | bytes 16777216 | tf_op jit(solution)/shard_map/absorb/pallas_call | solution.py:223
  69.1 4.1 %absorb.8 = (f32[1024,256]{1,0:T(8,128)S(1)}, f32[256,256]{1,0:T(8,128)S(1)}) custom-call(s32[1]{0:T(128)} %bitcast.me_ref.refs_0_, s32[1,8]{1,0:T(1,128)} %refs_1_.15, s32[1]{0:T(128)S(6)} %copy.13.refs_2_, s32[1,4]{1,0:T(1,128)} %refs_3_.15, bf16[8,1024,1024]{2,1,0:T(8,128)(2,1)} %bitcast.32, f32[4,256,256]{2,1,0:T(8,128)} %bitcast.40, ...), custom_call_target="tpu_custom_call" | custom-call | flops 1073741824 | bytes 8388608 | tf_op jit(solution)/shard_map/absorb/pallas_call | solution.py:223
  73.3 6.0 %back.2 = (f32[1024,256]{1,0:T(8,128)}, bf16[640,256]{1,0:T(8,128)(2,1)S(1)}) custom-call(s32[1]{0:T(128)} %bitcast.me_ref.refs_0_, s32[1,8]{1,0:T(1,128)} %refs_1_.15, s32[1]{0:T(128)S(6)} %copy.13.refs_2_, s32[1,4]{1,0:T(1,128)} %refs_3_.15, s32[1]{0:T(128)S(6)} %copy.14.rank_ref.refs_4_, bf16[8,1024,1024]{2,1,0:T(8,128)(2,1)} %bitcast.33, ...), custom_call_target="tpu_custom_call" | custom-call | flops 1610612736 | bytes 6291456 | tf_op jit(solution)/shard_map/back/pallas_call | solution.py:343
  79.3 3.0 %front.3 = (bf16[640,256]{1,0:T(8,128)(2,1)S(1)}, bf16[128,512]{1,0:T(8,128)(2,1)S(1)}, f32[128,512]{1,0:T(8,128)S(1)}) custom-call(s32[1]{0:T(128)} %bitcast.me_ref.refs_0_, s32[1]{0:T(128)S(6)} %copy.14.rank_ref.refs_4_, f32[1024,256]{1,0:T(8,128)} %get-tuple-element.16.v_in, f32[1024,256]{1,0:T(8,128)} %refs_12_.3, f32[256,512]{1,0:T(8,128)} %bitcast.48), custom_call_target="tpu_custom_call" | custom-call | flops 402653184 | bytes 2097152 | tf_op jit(solution)/shard_map/front/pallas_call | solution.py:102
  82.4 1.4 collective-permute-start.27
  84.4 2.9 %collective-permute-done.37 = bf16[128,512]{1,0:T(8,128)(2,1)S(1)} collective-permute-done((bf16[128,512]{1,0:T(8,128)(2,1)S(1)}, bf16[128,512]{1,0:T(8,128)(2,1)S(1)}, u32[]{:S(2)}, u32[]{:S(2)}) %collective-permute-start.37) | collective-permute-done | bytes 131104 | tf_op jit(solution)/shard_map/ppermute | solution.py:405
  87.4 1.4 collective-permute-start.38
  89.5 1.4 collective-permute-start.34
  90.9 1.6 %collective-permute-done.27.refs_9_ = bf16[640,256]{1,0:T(8,128)(2,1)S(1)} collective-permute-done((bf16[640,256]{1,0:T(8,128)(2,1)S(1)}, bf16[640,256]{1,0:T(8,128)(2,1)S(1)}, u32[]{:S(2)}, u32[]{:S(2)}) %collective-permute-start.27) | collective-permute-done | bytes 327712 | tf_op jit(solution)/shard_map/ppermute | solution.py:408
  94.4 1.4 collective-permute-start.24
  96.8 4.6 %collective-permute-done.31.refs_7_ = bf16[640,256]{1,0:T(8,128)(2,1)S(1)} collective-permute-done((bf16[640,256]{1,0:T(8,128)(2,1)S(1)}, bf16[640,256]{1,0:T(8,128)(2,1)S(1)}, u32[]{:S(2)}, u32[]{:S(2)}) %collective-permute-start.31) | collective-permute-done | bytes 327712 | tf_op jit(solution)/shard_map/ppermute | solution.py:408
  101.4 2.4 %collective-permute-start.32 = (bf16[640,256]{1,0:T(8,128)(2,1)S(1)}, bf16[640,256]{1,0:T(8,128)(2,1)S(1)}, u32[]{:S(2)}, u32[]{:S(2)}) collective-permute-start(bf16[640,256]{1,0:T(8,128)(2,1)S(1)} %collective-permute-done.31.refs_7_), channel_id=1, source_target_pairs={{0,2},{2,4},{4,6},{6,7},{7,5},{5,3},{3,1},{1,0},{8,10},{10,12},{12... | collective-permute-start | bytes 983048 | tf_op jit(solution)/shard_map/ppermute | solution.py:408
  103.8 4.1 %collective-permute-done.28.refs_13_ = bf16[640,256]{1,0:T(8,128)(2,1)S(1)} collective-permute-done((bf16[640,256]{1,0:T(8,128)(2,1)S(1)}, bf16[640,256]{1,0:T(8,128)(2,1)S(1)}, u32[]{:S(2)}, u32[]{:S(2)}) %collective-permute-start.28) | collective-permute-done | bytes 327712 | tf_op jit(solution)/shard_map/ppermute | solution.py:408
  108.8 2.4 %collective-permute-start.25 = (bf16[640,256]{1,0:T(8,128)(2,1)S(1)}, bf16[640,256]{1,0:T(8,128)(2,1)S(1)}, u32[]{:S(2)}, u32[]{:S(2)}) collective-permute-start(bf16[640,256]{1,0:T(8,128)(2,1)S(1)} %collective-permute-done.24.refs_10_), channel_id=1, source_target_pairs={{0,2},{2,4},{4,6},{6,7},{7,5},{5,3},{3,1},{1,0},{8,10},{10,12},{12... | collective-permute-start | bytes 983048 | tf_op jit(solution)/shard_map/ppermute | solution.py:408
  111.3 1.2 collective-permute-done.40.refs_1_
  113.4 3.0 %collective-permute-done.41.refs_2_ = bf16[32,512]{1,0:T(8,128)(2,1)S(1)} collective-permute-done((bf16[32,512]{1,0:T(8,128)(2,1)S(1)}, bf16[32,512]{1,0:T(8,128)(2,1)S(1)}, u32[]{:S(2)}, u32[]{:S(2)}) %collective-permute-start.41) | collective-permute-done | bytes 32800 | tf_op jit(solution)/shard_map/ppermute | solution.py:405
  116.4 3.3 %collective-permute-done.42.refs_3_ = bf16[32,512]{1,0:T(8,128)(2,1)S(1)} collective-permute-done((bf16[32,512]{1,0:T(8,128)(2,1)S(1)}, bf16[32,512]{1,0:T(8,128)(2,1)S(1)}, u32[]{:S(2)}, u32[]{:S(2)}) %collective-permute-start.42) | collective-permute-done | bytes 32800 | tf_op jit(solution)/shard_map/ppermute | solution.py:405
  119.7 2.7 %far.3.refs_13_ = bf16[32,512]{1,0:T(8,128)(2,1)S(1)} custom-call(s32[1]{0:T(128)} %bitcast.4.row_ref, s32[1,2]{1,0:T(1,128)S(1)} %copy-done.3, bf16[32,512]{1,0:T(8,128)(2,1)S(1)} %fusion.2.refs_0_, bf16[32,512]{1,0:T(8,128)(2,1)S(1)} %collective-permute-done.40.refs_1_, bf16[32,512]{1,0:T(8,128)(2,1)S(1)} %collective-permute-done.41.refs_2_, ...), custom_call_target="tpu_custom_call" | custom-call | flops 16777216 | bytes 2097152 | tf_op jit(solution)/shard_map/far/pallas_call | solution.py:256
  123.3 4.0 %collective-permute-done.43.refs_14_ = bf16[32,512]{1,0:T(8,128)(2,1)S(1)} collective-permute-done((bf16[32,512]{1,0:T(8,128)(2,1)S(1)}, bf16[32,512]{1,0:T(8,128)(2,1)S(1)}, u32[]{:S(2)}, u32[]{:S(2)}) %collective-permute-start.43) | collective-permute-done | bytes 32800 | tf_op jit(solution)/shard_map/ppermute | solution.py:405
  128.0 1.4 collective-permute-start.33
  130.0 3.3 %absorb.9.refs_14_ = f32[1024,256]{1,0:T(8,128)S(1)} custom-call(s32[1]{0:T(128)} %bitcast.me_ref.refs_0_, s32[1,8]{1,0:T(1,128)} %refs_1_.15, s32[1]{0:T(128)S(6)} %copy.13.refs_2_, s32[1,4]{1,0:T(1,128)} %refs_3_.15, bf16[8,1024,1024]{2,1,0:T(8,128)(2,1)} %bitcast.34, f32[4,256,256]{2,1,0:T(8,128)} %bitcast.42, ...), custom_call_target="tpu_custom_call" | custom-call | flops 536870912 | bytes 4194304 | tf_op jit(solution)/shard_map/absorb/pallas_call | solution.py:223
  133.3 1.2 collective-permute-start.30
  135.4 1.5 collective-permute-start.45
  136.9 6.8 %absorb.10 = (f32[1024,256]{1,0:T(8,128)S(1)}, f32[256,256]{1,0:T(8,128)S(1)}) custom-call(s32[1]{0:T(128)} %bitcast.me_ref.refs_0_, s32[1,8]{1,0:T(1,128)} %refs_1_.15, s32[1]{0:T(128)S(6)} %copy.13.refs_2_, s32[1,4]{1,0:T(1,128)} %refs_3_.15, bf16[8,1024,1024]{2,1,0:T(8,128)(2,1)} %bitcast.35, f32[4,256,256]{2,1,0:T(8,128)} %bitcast.43, ...), custom_call_target="tpu_custom_call" | custom-call | flops 2147483648 | bytes 16777216 | tf_op jit(solution)/shard_map/absorb/pallas_call | solution.py:223
  143.7 4.1 %absorb.11 = (f32[1024,256]{1,0:T(8,128)S(1)}, f32[256,256]{1,0:T(8,128)S(1)}) custom-call(s32[1]{0:T(128)} %bitcast.me_ref.refs_0_, s32[1,8]{1,0:T(1,128)} %refs_1_.15, s32[1]{0:T(128)S(6)} %copy.13.refs_2_, s32[1,4]{1,0:T(1,128)} %refs_3_.15, bf16[8,1024,1024]{2,1,0:T(8,128)(2,1)} %bitcast.36, f32[4,256,256]{2,1,0:T(8,128)} %bitcast.44, ...), custom_call_target="tpu_custom_call" | custom-call | flops 1073741824 | bytes 8388608 | tf_op jit(solution)/shard_map/absorb/pallas_call | solution.py:223
  147.8 5.8 %back.3 = f32[1024,256]{1,0:T(8,128)} custom-call(s32[1]{0:T(128)} %bitcast.me_ref.refs_0_, s32[1,8]{1,0:T(1,128)} %refs_1_.15, s32[1]{0:T(128)S(6)} %copy.13.refs_2_, s32[1,4]{1,0:T(1,128)} %refs_3_.15, s32[1]{0:T(128)S(6)} %copy.14.rank_ref.refs_4_, bf16[8,1024,1024]{2,1,0:T(8,128)(2,1)} %bitcast.37, f32[4,256,256]{2,1,0:T(8,128)} %bitcast.45, ...), custom_call_target="tpu_custom_call" | custom-call | flops 1610612736 | bytes 6291456 | tf_op jit(solution)/shard_map/back/pallas_call | solution.py:343
  (79 shorter events, 15.9 us)
Async XLA Ops:
  4.3 51.4 %copy-start = (bf16[640,256]{1,0:T(8,128)(2,1)}, bf16[640,256]{1,0:T(8,128)(2,1)S(1)}, u32[]{:S(2)}) copy-start(bf16[640,256]{1,0:T(8,128)(2,1)S(1)} %get-tuple-element.18.refs_7_) | copy-start | bytes 983044
  4.3 5.3 %collective-permute-start.14 = (bf16[128,512]{1,0:T(8,128)(2,1)S(1)}, bf16[128,512]{1,0:T(8,128)(2,1)S(1)}, u32[]{:S(2)}, u32[]{:S(2)}) collective-permute-start(bf16[128,512]{1,0:T(8,128)(2,1)S(1)} %get-tuple-element.24), channel_id=1, source_target_pairs={{0,1},{1,0},{2,3},{3,2},{4,5},{5,4},{6,7},{7,6},{8,9},{9,8},{10,11... | collective-permute-start | bytes 393224 | tf_op jit(solution)/shard_map/ppermute | solution.py:405
  5.9 10.6 %collective-permute-start.4 = (bf16[640,256]{1,0:T(8,128)(2,1)S(1)}, bf16[640,256]{1,0:T(8,128)(2,1)S(1)}, u32[]{:S(2)}, u32[]{:S(2)}) collective-permute-start(bf16[640,256]{1,0:T(8,128)(2,1)S(1)} %get-tuple-element.18.refs_7_), channel_id=1, source_target_pairs={{2,0},{4,2},{6,4},{7,6},{5,7},{3,5},{1,3},{0,1},{10,8},{12,10},{14... | collective-permute-start | bytes 983048 | tf_op jit(solution)/shard_map/ppermute | solution.py:408
  7.4 10.6 %collective-permute-start = (bf16[640,256]{1,0:T(8,128)(2,1)S(1)}, bf16[640,256]{1,0:T(8,128)(2,1)S(1)}, u32[]{:S(2)}, u32[]{:S(2)}) collective-permute-start(bf16[640,256]{1,0:T(8,128)(2,1)S(1)} %slice.7.refs_6_), channel_id=1, source_target_pairs={{0,2},{2,4},{4,6},{6,7},{7,5},{5,3},{3,1},{1,0},{8,10},{10,12},{12... | collective-permute-start | bytes 983048 | tf_op jit(solution)/shard_map/ppermute | solution.py:408
  9.7 10.0 %collective-permute-start.15 = (bf16[64,512]{1,0:T(8,128)(2,1)S(1)}, bf16[64,512]{1,0:T(8,128)(2,1)S(1)}, u32[]{:S(2)}, u32[]{:S(2)}) collective-permute-start(bf16[64,512]{1,0:T(8,128)(2,1)S(1)} %fusion), channel_id=1, source_target_pairs={{0,2},{1,3},{2,0},{3,1},{4,6},{5,7},{6,4},{7,5},{8,10},{9,11},{10,... | collective-permute-start | bytes 196616 | tf_op jit(solution)/shard_map/ppermute | solution.py:405
  12.4 13.1 %collective-permute-start.8 = (bf16[640,256]{1,0:T(8,128)(2,1)S(1)}, bf16[640,256]{1,0:T(8,128)(2,1)S(1)}, u32[]{:S(2)}, u32[]{:S(2)}) collective-permute-start(bf16[640,256]{1,0:T(8,128)(2,1)S(1)} %get-tuple-element.18.refs_7_), channel_id=1, source_target_pairs={{0,2},{2,4},{4,6},{6,7},{7,5},{5,3},{3,1},{1,0},{8,10},{10,12},{12... | collective-permute-start | bytes 983048 | tf_op jit(solution)/shard_map/ppermute | solution.py:408
  12.5 15.6 %collective-permute-start.11 = (bf16[640,256]{1,0:T(8,128)(2,1)S(1)}, bf16[640,256]{1,0:T(8,128)(2,1)S(1)}, u32[]{:S(2)}, u32[]{:S(2)}) collective-permute-start(bf16[640,256]{1,0:T(8,128)(2,1)S(1)} %slice.7.refs_6_), channel_id=1, source_target_pairs={{2,0},{4,2},{6,4},{7,6},{5,7},{3,5},{1,3},{0,1},{10,8},{12,10},{14... | collective-permute-start | bytes 983048 | tf_op jit(solution)/shard_map/ppermute | solution.py:408
  16.4 15.4 %collective-permute-start.5 = (bf16[640,256]{1,0:T(8,128)(2,1)S(1)}, bf16[640,256]{1,0:T(8,128)(2,1)S(1)}, u32[]{:S(2)}, u32[]{:S(2)}) collective-permute-start(bf16[640,256]{1,0:T(8,128)(2,1)S(1)} %collective-permute-done.4.refs_9_), channel_id=1, source_target_pairs={{2,0},{4,2},{6,4},{7,6},{5,7},{3,5},{1,3},{0,1},{10,8},{12,10},{14... | collective-permute-start | bytes 983048 | tf_op jit(solution)/shard_map/ppermute | solution.py:408
  18.1 15.2 %collective-permute-start.1 = (bf16[640,256]{1,0:T(8,128)(2,1)S(1)}, bf16[640,256]{1,0:T(8,128)(2,1)S(1)}, u32[]{:S(2)}, u32[]{:S(2)}) collective-permute-start(bf16[640,256]{1,0:T(8,128)(2,1)S(1)} %collective-permute-done.refs_6_), channel_id=1, source_target_pairs={{0,2},{2,4},{4,6},{6,7},{7,5},{5,3},{3,1},{1,0},{8,10},{10,12},{12... | collective-permute-start | bytes 983048 | tf_op jit(solution)/shard_map/ppermute | solution.py:408
  19.7 16.1 %collective-permute-start.16 = (bf16[32,512]{1,0:T(8,128)(2,1)S(1)}, bf16[32,512]{1,0:T(8,128)(2,1)S(1)}, u32[]{:S(2)}, u32[]{:S(2)}) collective-permute-start(bf16[32,512]{1,0:T(8,128)(2,1)S(1)} %fusion.4), channel_id=1, source_target_pairs={{0,4},{1,5},{2,6},{3,7},{4,0},{5,1},{6,2},{7,3},{8,12},{9,13},{10,... | collective-permute-start | bytes 98312 | tf_op jit(solution)/shard_map/ppermute | solution.py:405
  25.6 28.0 %collective-permute-start.9 = (bf16[640,256]{1,0:T(8,128)(2,1)S(1)}, bf16[640,256]{1,0:T(8,128)(2,1)}, u32[]{:S(2)}, u32[]{:S(2)}) collective-permute-start(bf16[640,256]{1,0:T(8,128)(2,1)S(1)} %collective-permute-done.8.refs_7_), channel_id=1, source_target_pairs={{0,2},{2,4},{4,6},{6,7},{7,5},{5,3},{3,1},{1,0},{8,10},{10,12},{12... | collective-permute-start | bytes 983048 | tf_op jit(solution)/shard_map/ppermute | solution.py:408
  28.1 27.6 %collective-permute-start.12 = (bf16[640,256]{1,0:T(8,128)(2,1)S(1)}, bf16[640,256]{1,0:T(8,128)(2,1)}, u32[]{:S(2)}, u32[]{:S(2)}) collective-permute-start(bf16[640,256]{1,0:T(8,128)(2,1)S(1)} %collective-permute-done.11.refs_8_), channel_id=1, source_target_pairs={{2,0},{4,2},{6,4},{7,6},{5,7},{3,5},{1,3},{0,1},{10,8},{12,10},{14... | collective-permute-start | bytes 983048 | tf_op jit(solution)/shard_map/ppermute | solution.py:408
  31.9 27.0 %collective-permute-start.6 = (bf16[640,256]{1,0:T(8,128)(2,1)S(1)}, bf16[640,256]{1,0:T(8,128)(2,1)S(1)}, u32[]{:S(2)}, u32[]{:S(2)}) collective-permute-start(bf16[640,256]{1,0:T(8,128)(2,1)S(1)} %collective-permute-done.5.refs_13_), channel_id=1, source_target_pairs={{2,0},{4,2},{6,4},{7,6},{5,7},{3,5},{1,3},{0,1},{10,8},{12,10},{14... | collective-permute-start | bytes 983048 | tf_op jit(solution)/shard_map/ppermute | solution.py:408
  33.3 26.8 %collective-permute-start.2 = (bf16[640,256]{1,0:T(8,128)(2,1)S(1)}, bf16[640,256]{1,0:T(8,128)(2,1)S(1)}, u32[]{:S(2)}, u32[]{:S(2)}) collective-permute-start(bf16[640,256]{1,0:T(8,128)(2,1)S(1)} %collective-permute-done.1.refs_10_), channel_id=1, source_target_pairs={{0,2},{2,4},{4,6},{6,7},{7,5},{5,3},{3,1},{1,0},{8,10},{10,12},{12... | collective-permute-start | bytes 983048 | tf_op jit(solution)/shard_map/ppermute | solution.py:408
  35.8 1.3 collective-permute-start.17
  37.1 3.9 %collective-permute-start.18 = (bf16[32,512]{1,0:T(8,128)(2,1)S(1)}, bf16[32,512]{1,0:T(8,128)(2,1)S(1)}, u32[]{:S(2)}, u32[]{:S(2)}) collective-permute-start(bf16[32,512]{1,0:T(8,128)(2,1)S(1)} %fusion.3.refs_0_), channel_id=1, source_target_pairs={{0,16},{8,24},{16,0},{24,8},{1,17},{9,25},{17,1},{25,9},{2,18},{10... | collective-permute-start | bytes 98312 | tf_op jit(solution)/shard_map/ppermute | solution.py:405
  41.0 3.6 %collective-permute-start.19 = (bf16[32,512]{1,0:T(8,128)(2,1)S(1)}, bf16[32,512]{1,0:T(8,128)(2,1)S(1)}, u32[]{:S(2)}, u32[]{:S(2)}) collective-permute-start(bf16[32,512]{1,0:T(8,128)(2,1)S(1)} %fusion.3.refs_0_), channel_id=1, source_target_pairs={{0,24},{8,16},{16,8},{24,0},{1,25},{9,17},{17,9},{25,1},{2,26},{10... | collective-permute-start | bytes 98312 | tf_op jit(solution)/shard_map/ppermute | solution.py:405
  48.0 4.9 %collective-permute-start.20 = (bf16[32,512]{1,0:T(8,128)(2,1)S(1)}, bf16[32,512]{1,0:T(8,128)(2,1)S(1)}, u32[]{:S(2)}, u32[]{:S(2)}) collective-permute-start(bf16[32,512]{1,0:T(8,128)(2,1)S(1)} %far.2.refs_13_), channel_id=1, source_target_pairs={{0,4},{1,5},{2,6},{3,7},{4,0},{5,1},{6,2},{7,3},{8,12},{9,13},{10,... | collective-permute-start | bytes 98312 | tf_op jit(solution)/shard_map/ppermute | solution.py:405
  52.9 8.2 %collective-permute-start.21 = (bf16[64,512]{1,0:T(8,128)(2,1)S(1)}, bf16[64,512]{1,0:T(8,128)(2,1)S(1)}, u32[]{:S(2)}, u32[]{:S(2)}) collective-permute-start(bf16[64,512]{1,0:T(8,128)(2,1)S(1)} %pad_maximum_fusion.2), channel_id=1, source_target_pairs={{0,2},{1,3},{2,0},{3,1},{4,6},{5,7},{6,4},{7,5},{8,10},{9,11},{10,... | collective-permute-start | bytes 196616 | tf_op jit(solution)/shard_map/ppermute | solution.py:405
  53.6 15.5 %collective-permute-start.10 = (bf16[640,256]{1,0:T(8,128)(2,1)}, bf16[640,256]{1,0:T(8,128)(2,1)S(1)}, u32[]{:S(2)}, u32[]{:S(2)}) collective-permute-start(bf16[640,256]{1,0:T(8,128)(2,1)} %collective-permute-done.9.refs_11_), channel_id=1, source_target_pairs={{0,2},{2,4},{4,6},{6,7},{7,5},{5,3},{3,1},{1,0},{8,10},{10,12},{12... | collective-permute-start | bytes 983048 | tf_op jit(solution)/shard_map/ppermute | solution.py:408
  55.6 13.5 %collective-permute-start.13 = (bf16[640,256]{1,0:T(8,128)(2,1)}, bf16[640,256]{1,0:T(8,128)(2,1)S(1)}, u32[]{:S(2)}, u32[]{:S(2)}) collective-permute-start(bf16[640,256]{1,0:T(8,128)(2,1)} %collective-permute-done.12.refs_12_), channel_id=1, source_target_pairs={{2,0},{4,2},{6,4},{7,6},{5,7},{3,5},{1,3},{0,1},{10,8},{12,10},{14... | collective-permute-start | bytes 983048 | tf_op jit(solution)/shard_map/ppermute | solution.py:408
  58.9 14.3 %collective-permute-start.7 = (bf16[640,256]{1,0:T(8,128)(2,1)S(1)}, bf16[640,256]{1,0:T(8,128)(2,1)S(1)}, u32[]{:S(2)}, u32[]{:S(2)}) collective-permute-start(bf16[640,256]{1,0:T(8,128)(2,1)S(1)} %collective-permute-done.6.refs_9_), channel_id=1, source_target_pairs={{2,0},{4,2},{6,4},{7,6},{5,7},{3,5},{1,3},{0,1},{10,8},{12,10},{14... | collective-permute-start | bytes 983048 | tf_op jit(solution)/shard_map/ppermute | solution.py:408
  60.1 13.1 %collective-permute-start.3 = (bf16[640,256]{1,0:T(8,128)(2,1)S(1)}, bf16[640,256]{1,0:T(8,128)(2,1)S(1)}, u32[]{:S(2)}, u32[]{:S(2)}) collective-permute-start(bf16[640,256]{1,0:T(8,128)(2,1)S(1)} %collective-permute-done.2.refs_6_), channel_id=1, source_target_pairs={{0,2},{2,4},{4,6},{6,7},{7,5},{5,3},{3,1},{1,0},{8,10},{10,12},{12... | collective-permute-start | bytes 983048 | tf_op jit(solution)/shard_map/ppermute | solution.py:408
  61.1 12.1 %collective-permute-start.22 = (bf16[128,512]{1,0:T(8,128)(2,1)S(1)}, bf16[128,512]{1,0:T(8,128)(2,1)S(1)}, u32[]{:S(2)}, u32[]{:S(2)}) collective-permute-start(bf16[128,512]{1,0:T(8,128)(2,1)S(1)} %pad_maximum_fusion), channel_id=1, source_target_pairs={{0,1},{1,0},{2,3},{3,2},{4,5},{5,4},{6,7},{7,6},{8,9},{9,8},{10,11... | collective-permute-start | bytes 393224 | tf_op jit(solution)/shard_map/ppermute | solution.py:405
  82.3 47.7 %copy-start.1 = (bf16[640,256]{1,0:T(8,128)(2,1)}, bf16[640,256]{1,0:T(8,128)(2,1)S(1)}, u32[]{:S(2)}) copy-start(bf16[640,256]{1,0:T(8,128)(2,1)S(1)} %get-tuple-element.27.refs_7_) | copy-start | bytes 983044
  82.3 5.0 %collective-permute-start.37 = (bf16[128,512]{1,0:T(8,128)(2,1)S(1)}, bf16[128,512]{1,0:T(8,128)(2,1)S(1)}, u32[]{:S(2)}, u32[]{:S(2)}) collective-permute-start(bf16[128,512]{1,0:T(8,128)(2,1)S(1)} %get-tuple-element.33), channel_id=1, source_target_pairs={{0,1},{1,0},{2,3},{3,2},{4,5},{5,4},{6,7},{7,6},{8,9},{9,8},{10,11... | collective-permute-start | bytes 393224 | tf_op jit(solution)/shard_map/ppermute | solution.py:405
  82.4 10.1 %collective-permute-start.27 = (bf16[640,256]{1,0:T(8,128)(2,1)S(1)}, bf16[640,256]{1,0:T(8,128)(2,1)S(1)}, u32[]{:S(2)}, u32[]{:S(2)}) collective-permute-start(bf16[640,256]{1,0:T(8,128)(2,1)S(1)} %get-tuple-element.27.refs_7_), channel_id=1, source_target_pairs={{2,0},{4,2},{6,4},{7,6},{5,7},{3,5},{1,3},{0,1},{10,8},{12,10},{14... | collective-permute-start | bytes 983048 | tf_op jit(solution)/shard_map/ppermute | solution.py:408
  83.8 10.6 %collective-permute-start.23 = (bf16[640,256]{1,0:T(8,128)(2,1)S(1)}, bf16[640,256]{1,0:T(8,128)(2,1)S(1)}, u32[]{:S(2)}, u32[]{:S(2)}) collective-permute-start(bf16[640,256]{1,0:T(8,128)(2,1)S(1)} %get-tuple-element.26.refs_6_), channel_id=1, source_target_pairs={{0,2},{2,4},{4,6},{6,7},{7,5},{5,3},{3,1},{1,0},{8,10},{10,12},{12... | collective-permute-start | bytes 983048 | tf_op jit(solution)/shard_map/ppermute | solution.py:408
  87.4 8.3 %collective-permute-start.38 = (bf16[64,512]{1,0:T(8,128)(2,1)S(1)}, bf16[64,512]{1,0:T(8,128)(2,1)S(1)}, u32[]{:S(2)}, u32[]{:S(2)}) collective-permute-start(bf16[64,512]{1,0:T(8,128)(2,1)S(1)} %fusion.1), channel_id=1, source_target_pairs={{0,2},{1,3},{2,0},{3,1},{4,6},{5,7},{6,4},{7,5},{8,10},{9,11},{10,... | collective-permute-start | bytes 196616 | tf_op jit(solution)/shard_map/ppermute | solution.py:405
  88.8 12.6 %collective-permute-start.31 = (bf16[640,256]{1,0:T(8,128)(2,1)S(1)}, bf16[640,256]{1,0:T(8,128)(2,1)S(1)}, u32[]{:S(2)}, u32[]{:S(2)}) collective-permute-start(bf16[640,256]{1,0:T(8,128)(2,1)S(1)} %get-tuple-element.27.refs_7_), channel_id=1, source_target_pairs={{0,2},{2,4},{4,6},{6,7},{7,5},{5,3},{3,1},{1,0},{8,10},{10,12},{12... | collective-permute-start | bytes 983048 | tf_op jit(solution)/shard_map/ppermute | solution.py:408
  89.5 14.3 %collective-permute-start.34 = (bf16[640,256]{1,0:T(8,128)(2,1)S(1)}, bf16[640,256]{1,0:T(8,128)(2,1)S(1)}, u32[]{:S(2)}, u32[]{:S(2)}) collective-permute-start(bf16[640,256]{1,0:T(8,128)(2,1)S(1)} %get-tuple-element.26.refs_6_), channel_id=1, source_target_pairs={{2,0},{4,2},{6,4},{7,6},{5,7},{3,5},{1,3},{0,1},{10,8},{12,10},{14... | collective-permute-start | bytes 983048 | tf_op jit(solution)/shard_map/ppermute | solution.py:408
  92.5 15.4 %collective-permute-start.28 = (bf16[640,256]{1,0:T(8,128)(2,1)S(1)}, bf16[640,256]{1,0:T(8,128)(2,1)S(1)}, u32[]{:S(2)}, u32[]{:S(2)}) collective-permute-start(bf16[640,256]{1,0:T(8,128)(2,1)S(1)} %collective-permute-done.27.refs_9_), channel_id=1, source_target_pairs={{2,0},{4,2},{6,4},{7,6},{5,7},{3,5},{1,3},{0,1},{10,8},{12,10},{14... | collective-permute-start | bytes 983048 | tf_op jit(solution)/shard_map/ppermute | solution.py:408
  94.4 14.4 %collective-permute-start.24 = (bf16[640,256]{1,0:T(8,128)(2,1)S(1)}, bf16[640,256]{1,0:T(8,128)(2,1)S(1)}, u32[]{:S(2)}, u32[]{:S(2)}) collective-permute-start(bf16[640,256]{1,0:T(8,128)(2,1)S(1)} %collective-permute-done.23.refs_6_), channel_id=1, source_target_pairs={{0,2},{2,4},{4,6},{6,7},{7,5},{5,3},{3,1},{1,0},{8,10},{10,12},{12... | collective-permute-start | bytes 983048 | tf_op jit(solution)/shard_map/ppermute | solution.py:408
  95.8 15.4 %collective-permute-start.39 = (bf16[32,512]{1,0:T(8,128)(2,1)S(1)}, bf16[32,512]{1,0:T(8,128)(2,1)S(1)}, u32[]{:S(2)}, u32[]{:S(2)}) collective-permute-start(bf16[32,512]{1,0:T(8,128)(2,1)S(1)} %fusion.5), channel_id=1, source_target_pairs={{0,4},{1,5},{2,6},{3,7},{4,0},{5,1},{6,2},{7,3},{8,12},{9,13},{10,... | collective-permute-start | bytes 98312 | tf_op jit(solution)/shard_map/ppermute | solution.py:405
  101.4 26.6 %collective-permute-start.32 = (bf16[640,256]{1,0:T(8,128)(2,1)S(1)}, bf16[640,256]{1,0:T(8,128)(2,1)S(1)}, u32[]{:S(2)}, u32[]{:S(2)}) collective-permute-start(bf16[640,256]{1,0:T(8,128)(2,1)S(1)} %collective-permute-done.31.refs_7_), channel_id=1, source_target_pairs={{0,2},{2,4},{4,6},{6,7},{7,5},{5,3},{3,1},{1,0},{8,10},{10,12},{12... | collective-permute-start | bytes 983048 | tf_op jit(solution)/shard_map/ppermute | solution.py:408
  103.8 25.6 %collective-permute-start.35 = (bf16[640,256]{1,0:T(8,128)(2,1)S(1)}, bf16[640,256]{1,0:T(8,128)(2,1)S(1)}, u32[]{:S(2)}, u32[]{:S(2)}) collective-permute-start(bf16[640,256]{1,0:T(8,128)(2,1)S(1)} %collective-permute-done.34.refs_8_), channel_id=1, source_target_pairs={{2,0},{4,2},{6,4},{7,6},{5,7},{3,5},{1,3},{0,1},{10,8},{12,10},{14... | collective-permute-start | bytes 983048 | tf_op jit(solution)/shard_map/ppermute | solution.py:408
  107.9 25.4 %collective-permute-start.29 = (bf16[640,256]{1,0:T(8,128)(2,1)S(1)}, bf16[640,256]{1,0:T(8,128)(2,1)S(1)}, u32[]{:S(2)}, u32[]{:S(2)}) collective-permute-start(bf16[640,256]{1,0:T(8,128)(2,1)S(1)} %collective-permute-done.28.refs_13_), channel_id=1, source_target_pairs={{2,0},{4,2},{6,4},{7,6},{5,7},{3,5},{1,3},{0,1},{10,8},{12,10},{14... | collective-permute-start | bytes 983048 | tf_op jit(solution)/shard_map/ppermute | solution.py:408
  108.8 25.7 %collective-permute-start.25 = (bf16[640,256]{1,0:T(8,128)(2,1)S(1)}, bf16[640,256]{1,0:T(8,128)(2,1)S(1)}, u32[]{:S(2)}, u32[]{:S(2)}) collective-permute-start(bf16[640,256]{1,0:T(8,128)(2,1)S(1)} %collective-permute-done.24.refs_10_), channel_id=1, source_target_pairs={{0,2},{2,4},{4,6},{6,7},{7,5},{5,3},{3,1},{1,0},{8,10},{10,12},{12... | collective-permute-start | bytes 983048 | tf_op jit(solution)/shard_map/ppermute | solution.py:408
  111.2 1.3 collective-permute-start.40
  112.5 3.9 %collective-permute-start.41 = (bf16[32,512]{1,0:T(8,128)(2,1)S(1)}, bf16[32,512]{1,0:T(8,128)(2,1)S(1)}, u32[]{:S(2)}, u32[]{:S(2)}) collective-permute-start(bf16[32,512]{1,0:T(8,128)(2,1)S(1)} %fusion.2.refs_0_), channel_id=1, source_target_pairs={{0,16},{8,24},{16,0},{24,8},{1,17},{9,25},{17,1},{25,9},{2,18},{10... | collective-permute-start | bytes 98312 | tf_op jit(solution)/shard_map/ppermute | solution.py:405
  116.4 3.3 %collective-permute-start.42 = (bf16[32,512]{1,0:T(8,128)(2,1)S(1)}, bf16[32,512]{1,0:T(8,128)(2,1)S(1)}, u32[]{:S(2)}, u32[]{:S(2)}) collective-permute-start(bf16[32,512]{1,0:T(8,128)(2,1)S(1)} %fusion.2.refs_0_), channel_id=1, source_target_pairs={{0,24},{8,16},{16,8},{24,0},{1,25},{9,17},{17,9},{25,1},{2,26},{10... | collective-permute-start | bytes 98312 | tf_op jit(solution)/shard_map/ppermute | solution.py:405
  122.5 4.9 %collective-permute-start.43 = (bf16[32,512]{1,0:T(8,128)(2,1)S(1)}, bf16[32,512]{1,0:T(8,128)(2,1)S(1)}, u32[]{:S(2)}, u32[]{:S(2)}) collective-permute-start(bf16[32,512]{1,0:T(8,128)(2,1)S(1)} %far.3.refs_13_), channel_id=1, source_target_pairs={{0,4},{1,5},{2,6},{3,7},{4,0},{5,1},{6,2},{7,3},{8,12},{9,13},{10,... | collective-permute-start | bytes 98312 | tf_op jit(solution)/shard_map/ppermute | solution.py:405
  127.4 8.0 %collective-permute-start.44 = (bf16[64,512]{1,0:T(8,128)(2,1)S(1)}, bf16[64,512]{1,0:T(8,128)(2,1)S(1)}, u32[]{:S(2)}, u32[]{:S(2)}) collective-permute-start(bf16[64,512]{1,0:T(8,128)(2,1)S(1)} %pad_maximum_fusion.3), channel_id=1, source_target_pairs={{0,2},{1,3},{2,0},{3,1},{4,6},{5,7},{6,4},{7,5},{8,10},{9,11},{10,... | collective-permute-start | bytes 196616 | tf_op jit(solution)/shard_map/ppermute | solution.py:405
  128.0 15.7 %collective-permute-start.33 = (bf16[640,256]{1,0:T(8,128)(2,1)S(1)}, bf16[640,256]{1,0:T(8,128)(2,1)S(1)}, u32[]{:S(2)}, u32[]{:S(2)}) collective-permute-start(bf16[640,256]{1,0:T(8,128)(2,1)S(1)} %collective-permute-done.32.refs_11_), channel_id=1, source_target_pairs={{0,2},{2,4},{4,6},{6,7},{7,5},{5,3},{3,1},{1,0},{8,10},{10,12},{12... | collective-permute-start | bytes 983048 | tf_op jit(solution)/shard_map/ppermute | solution.py:408
  129.4 14.3 %collective-permute-start.36 = (bf16[640,256]{1,0:T(8,128)(2,1)S(1)}, bf16[640,256]{1,0:T(8,128)(2,1)S(1)}, u32[]{:S(2)}, u32[]{:S(2)}) collective-permute-start(bf16[640,256]{1,0:T(8,128)(2,1)S(1)} %collective-permute-done.35.refs_12_), channel_id=1, source_target_pairs={{2,0},{4,2},{6,4},{7,6},{5,7},{3,5},{1,3},{0,1},{10,8},{12,10},{14... | collective-permute-start | bytes 983048 | tf_op jit(solution)/shard_map/ppermute | solution.py:408
  133.3 14.5 %collective-permute-start.30 = (bf16[640,256]{1,0:T(8,128)(2,1)S(1)}, bf16[640,256]{1,0:T(8,128)(2,1)S(1)}, u32[]{:S(2)}, u32[]{:S(2)}) collective-permute-start(bf16[640,256]{1,0:T(8,128)(2,1)S(1)} %collective-permute-done.29.refs_9_), channel_id=1, source_target_pairs={{2,0},{4,2},{6,4},{7,6},{5,7},{3,5},{1,3},{0,1},{10,8},{12,10},{14... | collective-permute-start | bytes 983048 | tf_op jit(solution)/shard_map/ppermute | solution.py:408
  134.5 13.3 %collective-permute-start.26 = (bf16[640,256]{1,0:T(8,128)(2,1)S(1)}, bf16[640,256]{1,0:T(8,128)(2,1)S(1)}, u32[]{:S(2)}, u32[]{:S(2)}) collective-permute-start(bf16[640,256]{1,0:T(8,128)(2,1)S(1)} %collective-permute-done.25.refs_6_), channel_id=1, source_target_pairs={{0,2},{2,4},{4,6},{6,7},{7,5},{5,3},{3,1},{1,0},{8,10},{10,12},{12... | collective-permute-start | bytes 983048 | tf_op jit(solution)/shard_map/ppermute | solution.py:408
  135.4 12.4 %collective-permute-start.45 = (bf16[128,512]{1,0:T(8,128)(2,1)S(1)}, bf16[128,512]{1,0:T(8,128)(2,1)S(1)}, u32[]{:S(2)}, u32[]{:S(2)}) collective-permute-start(bf16[128,512]{1,0:T(8,128)(2,1)S(1)} %pad_maximum_fusion.1), channel_id=1, source_target_pairs={{0,1},{1,0},{2,3},{3,2},{4,5},{5,4},{6,7},{7,6},{8,9},{9,8},{10,11... | collective-permute-start | bytes 393224 | tf_op jit(solution)/shard_map/ppermute | solution.py:405
  (2 other events, 47.2 us)
